TPU v7x, 32 devices: a whole 2x2x4 slice. The times are simulated.
32 devices in a mesh: dp: 8 (over y, x, core), tensor: 4 (over z).
Axes of the slice: x: 2, y: 2, z: 4, core: 2. Of those that a mesh axis runs over, the one named last changes fastest.
Arguments:
- tokens: bfloat16 [8192, 2048], P(('dp', 'tensor')), may hold values from -6 to 6
- norm_attn: bfloat16 [2048], P('dp'), may hold values from 0.5 to 1.5
- w_query: bfloat16 [2048, 2048], P('dp', 'tensor'), may hold values from -0.125 to 0.125
- key_matrix: bfloat16 [2048, 1024], P('dp', 'tensor'), may hold values from -0.125 to 0.125
- value_matrix: bfloat16 [2048, 1024], P('dp', 'tensor'), may hold values from -0.125 to 0.125
- gain_query: bfloat16 [128], P('dp'), may hold values from 0.25 to 1.75
- gain_key: bfloat16 [128], P('dp'), may hold values from 0.25 to 1.75
- w_output: bfloat16 [2048, 2048], P('tensor', 'dp'), may hold values from -0.5 to 0.5
- norm_ffn: bfloat16 [2048], P('dp'), may hold values from 0.5 to 1.5
- w_gate: bfloat16 [2048, 6144], P('dp', 'tensor'), may hold values from -0.125 to 0.125
- w_up: bfloat16 [2048, 6144], P('dp', 'tensor'), may hold values from -0.125 to 0.125
- w_down: bfloat16 [6144, 2048], P('tensor', 'dp'), may hold values from -0.078125 to 0.078125
- cotangent: bfloat16 [8192, 2048], P(('dp', 'tensor')), may hold values from -6 to 6
- lengths: int32 [8], replicated, may hold values from 769 to 1024, as said below
- deal_order: int32 [8], replicated, may hold values from 0 to 7, as said below
Outputs:
- block_out: bfloat16 [8192, 2048], P(('dp', 'tensor'))
- grad_tokens: bfloat16 [8192, 2048], P(('dp', 'tensor'))
- grad_norm_attn: float32 [2048], P('dp')
- grad_query: float32 [2048, 2048], P('dp', 'tensor')
- grad_key: float32 [2048, 1024], P('dp', 'tensor')
- grad_value: float32 [2048, 1024], P('dp', 'tensor')
- grad_gain_query: float32 [128], P('dp')
- grad_gain_key: float32 [128], P('dp')
- grad_output: float32 [2048, 2048], P('tensor', 'dp')
- grad_norm_ffn: float32 [2048], P('dp')
- grad_gate: float32 [2048, 6144], P('dp', 'tensor')
- grad_up: float32 [2048, 6144], P('dp', 'tensor')
- grad_down: float32 [6144, 2048], P('tensor', 'dp')
Inputs may be any that keep to these rules, and one draw needn't show every extreme that they name: Data group g takes sequence deal_order[g]; deal_order is a permutation. `lengths`: one group's sequence fills all 1024 of its rows and another's leaves 256 - 1 rows of padding.
All inputs are finite; a program needn't handle non-finite values.
Results may differ from a plain program's by a relative error of at most 0.023.
Values may be sent and summed in bfloat16 or wider, within the bound.
No kernel may reach another device: no remote copies, remote signals or barrier semaphores. Data moves between devices by JAX's collectives and lax.ppermute only.
A program may use at most 192 MiB of HBM per device.

v0:
```python
import jax
import jax.numpy as jnp
from jax import lax
from jax.sharding import PartitionSpec as P

QUERY_HEADS = 16
KEY_VALUE_HEADS = 8
HEAD_SIZE = 128


norm_eps = 1e-06
rope_base = 1000000.0


def rms_scale(value_vectors):
    return lax.rsqrt(jnp.mean(value_vectors * value_vectors, axis=-1, keepdims=True) + norm_eps)


def rope_tables(position):
    half_dim = HEAD_SIZE // 2
    inverse_freq = rope_base ** (-2.0 * jnp.arange(half_dim, dtype=jnp.float32) / HEAD_SIZE)
    angles = position.astype(jnp.float32)[:, None] * inverse_freq[None, :]
    angles = jnp.concatenate([angles, angles], axis=1)
    return (jnp.cos(angles), jnp.sin(angles))


def rotate_half(value_vectors):
    half_dim = value_vectors.shape[-1] // 2
    return jnp.concatenate([-value_vectors[..., half_dim:], value_vectors[..., :half_dim]], axis=-1)


def rotate_back(value_vectors):
    half_dim = value_vectors.shape[-1] // 2
    return jnp.concatenate([value_vectors[..., half_dim:], -value_vectors[..., :half_dim]], axis=-1)


def group_layout(lengths, deal_order, group_id, count_of_rows):
    slots = jnp.arange(deal_order.shape[0], dtype=jnp.int32)
    seq_taken = jnp.sum(jnp.where(slots == group_id, deal_order, 0))
    seq_len = jnp.sum(jnp.where(slots == seq_taken, lengths, 0))
    row_index = jnp.arange(count_of_rows, dtype=jnp.int32)
    segment = (row_index >= seq_len).astype(jnp.int32)
    seg_start = jnp.where(segment == 0, 0, seq_len)
    return (segment, row_index - seg_start, row_index < seq_len)


def contract_rows(left, right):
    return lax.dot_general(
        left, right, (((0,), (0,)), ((), ())), preferred_element_type=jnp.float32
    )


def times_transpose(left, right):
    return lax.dot_general(
        left, right, (((1,), (1,)), ((), ())), preferred_element_type=jnp.float32
    )


def masked_scores(query_head, key_head, allowed):
    scores = jnp.einsum(
        "qgd,kd->gqk", query_head, key_head, preferred_element_type=jnp.float32
    ) * HEAD_SIZE ** (-0.5)
    return jnp.where(allowed[None], scores, -1e30)


def attend_head(query_head, key_head, value_head, allowed):
    scores = masked_scores(query_head, key_head, allowed)
    top_score = jnp.max(scores, axis=-1, keepdims=True)
    raised = jnp.exp(scores - top_score)
    summed = jnp.sum(raised, axis=-1, keepdims=True)
    attn_probs = (raised / summed).astype(jnp.bfloat16)
    context = jnp.einsum("gqk,kd->qgd", attn_probs, value_head, preferred_element_type=jnp.float32)
    return (context.astype(jnp.bfloat16), top_score[..., 0] + jnp.log(summed[..., 0]))


def attend_back(query_head, key_head, value_head, d_context_head, log_total, allowed):
    scores = masked_scores(query_head, key_head, allowed)
    attn_full = jnp.exp(scores - log_total[..., None])
    attn_probs = attn_full.astype(jnp.bfloat16)
    d_value = jnp.einsum(
        "gqk,qgd->kd", attn_probs, d_context_head, preferred_element_type=jnp.float32
    )
    d_probs = jnp.einsum(
        "qgd,kd->gqk", d_context_head, value_head, preferred_element_type=jnp.float32
    )
    row_dot = jnp.sum(attn_full * d_probs, axis=-1, keepdims=True)
    d_scores = (attn_full * (d_probs - row_dot)).astype(jnp.bfloat16)
    d_query = jnp.einsum(
        "gqk,kd->qgd", d_scores, key_head, preferred_element_type=jnp.float32
    ) * HEAD_SIZE ** (-0.5)
    d_key = jnp.einsum(
        "gqk,qgd->kd", d_scores, query_head, preferred_element_type=jnp.float32
    ) * HEAD_SIZE ** (-0.5)
    return (d_query, d_key, d_value)


def norm_back(d_unit, pre_values, pre_scale, gain_values):
    mixed_terms = gain_values * d_unit
    return pre_scale * mixed_terms - pre_values * pre_scale**3 * jnp.mean(
        mixed_terms * pre_values, axis=-1, keepdims=True
    )


def local(
    tokens,
    norm_attn,
    w_query,
    key_matrix,
    value_matrix,
    gain_query,
    gain_key,
    w_output,
    norm_ffn,
    w_gate,
    w_up,
    w_down,
    cotangent,
    lengths,
    deal_order,
):
    local_rows = tokens.shape[0]
    group_rows = local_rows * lax.axis_size("tensor")
    heads_here = QUERY_HEADS // lax.axis_size("tensor")
    key_value_local = KEY_VALUE_HEADS // lax.axis_size("tensor")
    rows_per_group = QUERY_HEADS // KEY_VALUE_HEADS
    q_width = heads_here * HEAD_SIZE
    kv_width = key_value_local * HEAD_SIZE
    segment, position, live_rows = group_layout(
        lengths, deal_order, lax.axis_index("dp"), group_rows
    )
    row_index = jnp.arange(group_rows, dtype=jnp.int32)
    allowed = (segment[:, None] == segment[None, :]) & (row_index[None, :] <= row_index[:, None])
    own_live = lax.dynamic_slice_in_dim(
        live_rows, lax.axis_index("tensor") * local_rows, local_rows
    ).astype(jnp.float32)[:, None]
    cosine_table, sine_table = rope_tables(position)
    cosine_table = cosine_table[:, None, :]
    sine_table = sine_table[:, None, :]
    full_set = (
        lax.all_gather(norm_attn, "dp", axis=0, tiled=True),
        lax.all_gather(w_query, "dp", axis=0, tiled=True),
        lax.all_gather(key_matrix, "dp", axis=0, tiled=True),
        lax.all_gather(value_matrix, "dp", axis=0, tiled=True),
        lax.all_gather(gain_query, "dp", axis=0, tiled=True),
        lax.all_gather(gain_key, "dp", axis=0, tiled=True),
        lax.all_gather(w_output, "dp", axis=1, tiled=True),
        lax.all_gather(norm_ffn, "dp", axis=0, tiled=True),
        lax.all_gather(w_gate, "dp", axis=0, tiled=True),
        lax.all_gather(w_up, "dp", axis=0, tiled=True),
        lax.all_gather(w_down, "dp", axis=1, tiled=True),
    )
    qkv_weight = jnp.concatenate((full_set[1], full_set[2], full_set[3]), axis=1)
    token_rows = tokens.astype(jnp.float32)
    scale_attn = rms_scale(token_rows)
    attention_normed_input = (token_rows * scale_attn * full_set[0].astype(jnp.float32)).astype(
        jnp.bfloat16
    )
    normed_attn_all = lax.all_gather(attention_normed_input, "tensor", axis=0, tiled=True)
    projected = jnp.dot(normed_attn_all, qkv_weight, preferred_element_type=jnp.float32)
    q_pre = projected[:, :q_width].reshape(group_rows, heads_here, HEAD_SIZE)
    key_before_norm = projected[:, q_width : q_width + kv_width].reshape(
        group_rows, key_value_local, HEAD_SIZE
    )
    value_rows = projected[:, q_width + kv_width :].astype(jnp.bfloat16)
    q_scale = rms_scale(q_pre)
    q_unit = q_pre * q_scale * full_set[4].astype(jnp.float32)
    queries = (q_unit * cosine_table + rotate_half(q_unit) * sine_table).astype(jnp.bfloat16)
    k_scale = rms_scale(key_before_norm)
    k_unit = key_before_norm * k_scale * full_set[5].astype(jnp.float32)
    key_rot = (k_unit * cosine_table + rotate_half(k_unit) * sine_table).astype(jnp.bfloat16)
    query_heads = jnp.moveaxis(
        queries.reshape(group_rows, key_value_local, rows_per_group, HEAD_SIZE), 1, 0
    )
    key_heads = jnp.moveaxis(key_rot, 1, 0)
    value_heads = jnp.moveaxis(value_rows.reshape(group_rows, key_value_local, HEAD_SIZE), 1, 0)
    context_heads, log_total = lax.map(
        lambda head_parts: attend_head(head_parts[0], head_parts[1], head_parts[2], allowed),
        (query_heads, key_heads, value_heads),
    )
    context = jnp.moveaxis(context_heads, 0, 1).reshape(group_rows, q_width)
    hidden = token_rows + lax.psum_scatter(
        jnp.dot(context, full_set[6], preferred_element_type=jnp.float32).astype(jnp.bfloat16),
        "tensor",
        scatter_dimension=0,
        tiled=True,
    ).astype(jnp.float32)
    scale_ffn = rms_scale(hidden)
    normed_ffn = (hidden * scale_ffn * full_set[7].astype(jnp.float32)).astype(jnp.bfloat16)
    normed_ffn_all = lax.all_gather(normed_ffn, "tensor", axis=0, tiled=True)
    gate_proj = jnp.dot(normed_ffn_all, full_set[8], preferred_element_type=jnp.float32)
    up_proj = jnp.dot(normed_ffn_all, full_set[9], preferred_element_type=jnp.float32)
    gate_sig = jax.nn.sigmoid(gate_proj)
    activation = (gate_proj * gate_sig * up_proj).astype(jnp.bfloat16)
    block_rows = hidden + lax.psum_scatter(
        jnp.dot(activation, full_set[10], preferred_element_type=jnp.float32).astype(jnp.bfloat16),
        "tensor",
        scatter_dimension=0,
        tiled=True,
    ).astype(jnp.float32)
    block_out = (block_rows * own_live).astype(jnp.bfloat16)
    back_set = (
        lax.all_gather(norm_attn, "dp", axis=0, tiled=True),
        lax.all_gather(w_query, "dp", axis=0, tiled=True),
        lax.all_gather(key_matrix, "dp", axis=0, tiled=True),
        lax.all_gather(value_matrix, "dp", axis=0, tiled=True),
        lax.all_gather(gain_query, "dp", axis=0, tiled=True),
        lax.all_gather(gain_key, "dp", axis=0, tiled=True),
        lax.all_gather(w_output, "dp", axis=1, tiled=True),
        lax.all_gather(norm_ffn, "dp", axis=0, tiled=True),
        lax.all_gather(w_gate, "dp", axis=0, tiled=True),
        lax.all_gather(w_up, "dp", axis=0, tiled=True),
        lax.all_gather(w_down, "dp", axis=1, tiled=True),
    )
    back_qkv = jnp.concatenate((back_set[1], back_set[2], back_set[3]), axis=1)
    d_rows = cotangent.astype(jnp.float32) * own_live
    d_branch = d_rows.astype(jnp.bfloat16)
    d_branch_all = lax.all_gather(d_branch, "tensor", axis=0, tiled=True)
    d_act = times_transpose(d_branch_all, back_set[10])
    grad_down = contract_rows(activation, d_branch_all)
    d_gate = (d_act * up_proj * gate_sig * (1.0 + gate_proj * (1.0 - gate_sig))).astype(
        jnp.bfloat16
    )
    d_up = (d_act * gate_proj * gate_sig).astype(jnp.bfloat16)
    grad_gate = contract_rows(normed_ffn_all, d_gate)
    grad_up = contract_rows(normed_ffn_all, d_up)
    d_normed_ffn = lax.psum_scatter(
        (times_transpose(d_gate, back_set[8]) + times_transpose(d_up, back_set[9])).astype(
            jnp.bfloat16
        ),
        "tensor",
        scatter_dimension=0,
        tiled=True,
    ).astype(jnp.float32)
    part_norm_ffn = jnp.sum(d_normed_ffn * hidden * scale_ffn, axis=0)
    d_hidden = d_rows + norm_back(d_normed_ffn, hidden, scale_ffn, back_set[7].astype(jnp.float32))
    d_attended = d_hidden.astype(jnp.bfloat16)
    d_attended_all = lax.all_gather(d_attended, "tensor", axis=0, tiled=True)
    d_context = times_transpose(d_attended_all, back_set[6]).astype(jnp.bfloat16)
    grad_output = contract_rows(context, d_attended_all)
    d_context_heads = jnp.moveaxis(
        d_context.reshape(group_rows, key_value_local, rows_per_group, HEAD_SIZE), 1, 0
    )
    d_query_heads, d_key_heads, d_value_heads = lax.map(
        lambda head_parts: attend_back(
            head_parts[0], head_parts[1], head_parts[2], head_parts[3], head_parts[4], allowed
        ),
        (query_heads, key_heads, value_heads, d_context_heads, log_total),
    )
    d_queries = jnp.moveaxis(d_query_heads, 0, 1).reshape(group_rows, heads_here, HEAD_SIZE)
    d_keys = jnp.moveaxis(d_key_heads, 0, 1)
    d_value = jnp.moveaxis(d_value_heads, 0, 1).reshape(group_rows, kv_width)
    du_query = d_queries * cosine_table + rotate_back(d_queries * sine_table)
    part_gain_query = jnp.sum(du_query * q_pre * q_scale, axis=(0, 1))
    d_q_pre = norm_back(du_query, q_pre, q_scale, back_set[4].astype(jnp.float32))
    du_key = d_keys * cosine_table + rotate_back(d_keys * sine_table)
    part_gain_key = jnp.sum(du_key * key_before_norm * k_scale, axis=(0, 1))
    d_k_pre = norm_back(du_key, key_before_norm, k_scale, back_set[5].astype(jnp.float32))
    d_projected = jnp.concatenate(
        (d_q_pre.reshape(group_rows, q_width), d_k_pre.reshape(group_rows, kv_width), d_value),
        axis=1,
    ).astype(jnp.bfloat16)
    grad_qkv = contract_rows(normed_attn_all, d_projected)
    grad_query = grad_qkv[:, :q_width]
    grad_key = grad_qkv[:, q_width : q_width + kv_width]
    grad_value = grad_qkv[:, q_width + kv_width :]
    d_normed_attn = lax.psum_scatter(
        times_transpose(d_projected, back_qkv).astype(jnp.bfloat16),
        "tensor",
        scatter_dimension=0,
        tiled=True,
    ).astype(jnp.float32)
    part_norm_attn = jnp.sum(d_normed_attn * token_rows * scale_attn, axis=0)
    d_tokens = d_hidden + norm_back(
        d_normed_attn, token_rows, scale_attn, back_set[0].astype(jnp.float32)
    )
    gain_parts = lax.psum((part_norm_attn, part_norm_ffn, part_gain_query, part_gain_key), "tensor")
    shards = tuple(
        (
            lax.psum_scatter(
                gain_parts[0].astype(jnp.bfloat16), "dp", scatter_dimension=0, tiled=True
            ).astype(jnp.float32),
            lax.psum_scatter(
                grad_query.astype(jnp.bfloat16), "dp", scatter_dimension=0, tiled=True
            ).astype(jnp.float32),
            lax.psum_scatter(
                grad_key.astype(jnp.bfloat16), "dp", scatter_dimension=0, tiled=True
            ).astype(jnp.float32),
            lax.psum_scatter(
                grad_value.astype(jnp.bfloat16), "dp", scatter_dimension=0, tiled=True
            ).astype(jnp.float32),
            lax.psum_scatter(
                gain_parts[2].astype(jnp.bfloat16), "dp", scatter_dimension=0, tiled=True
            ).astype(jnp.float32),
            lax.psum_scatter(
                gain_parts[3].astype(jnp.bfloat16), "dp", scatter_dimension=0, tiled=True
            ).astype(jnp.float32),
            lax.psum_scatter(
                grad_output.astype(jnp.bfloat16), "dp", scatter_dimension=1, tiled=True
            ).astype(jnp.float32),
            lax.psum_scatter(
                gain_parts[1].astype(jnp.bfloat16), "dp", scatter_dimension=0, tiled=True
            ).astype(jnp.float32),
            lax.psum_scatter(
                grad_gate.astype(jnp.bfloat16), "dp", scatter_dimension=0, tiled=True
            ).astype(jnp.float32),
            lax.psum_scatter(
                grad_up.astype(jnp.bfloat16), "dp", scatter_dimension=0, tiled=True
            ).astype(jnp.float32),
            lax.psum_scatter(
                grad_down.astype(jnp.bfloat16), "dp", scatter_dimension=1, tiled=True
            ).astype(jnp.float32),
        )
    )
    return (block_out, d_tokens.astype(jnp.bfloat16)) + shards


def solution(mesh):
    return jax.shard_map(
        local,
        mesh=mesh,
        in_specs=(
            P(("dp", "tensor"), None),
            P("dp"),
            P("dp", "tensor"),
            P("dp", "tensor"),
            P("dp", "tensor"),
            P("dp"),
            P("dp"),
            P("tensor", "dp"),
            P("dp"),
            P("dp", "tensor"),
            P("dp", "tensor"),
            P("tensor", "dp"),
            P(("dp", "tensor"), None),
            P(),
            P(),
        ),
        out_specs=(
            P(("dp", "tensor"), None),
            P(("dp", "tensor"), None),
            P("dp"),
            P("dp", "tensor"),
            P("dp", "tensor"),
            P("dp", "tensor"),
            P("dp"),
            P("dp"),
            P("tensor", "dp"),
            P("dp"),
            P("dp", "tensor"),
            P("dp", "tensor"),
            P("tensor", "dp"),
        ),
        check_vma=False,
    )
```

profile of v0, /device:TPU:0, one launch (start us, length us, event | category | flops | bytes accessed | tf_op | source)
XLA Modules:
  0.0 1377.7 jit_solution(12239359164739884811)
XLA Ops:
  10.2 10.3 all-gather
  31.5 13.4 all-reduce.8
  48.0 3.2 constant_dynamic-update-slice_fusion.2
  51.2 14.9 %all-gather.18.cloned.1.call-done = bf16[2048,256]{1,0:T(8,128)(2,1)} async-done(((bf16[256,256]{1,0:T(8,128)(2,1)}), bf16[2048,256]{1,0:T(8,128)(2,1)}) %all-gather.18.cloned.1.call-update) | async-done | bytes 1048592 | tf_op jit(solution)/shard_map/all_gather | solution.py:142
  68.4 23.1 %all-gather.20.cloned.1.call-done = bf16[2048,256]{1,0:T(8,128)(2,1)} async-done(((bf16[256,256]{1,0:T(8,128)(2,1)}), bf16[2048,256]{1,0:T(8,128)(2,1)}) %all-gather.20.cloned.1.call-update) | async-done | bytes 1048592 | tf_op jit(solution)/shard_map/all_gather | solution.py:143
  93.9 80.5 %all-gather.14.cloned.1.call-done = bf16[1024,2048]{1,0:T(8,128)(2,1)} async-done(((bf16[256,2048]{1,0:T(8,128)(2,1)}), bf16[1024,2048]{1,0:T(8,128)(2,1)}) %all-gather.14.cloned.1.call-update) | async-done | bytes 4194320 | tf_op jit(solution)/shard_map/all_gather | solution.py:158
  174.3 7.6 fusion.112
  191.8 3.4 copy.69
  195.2 3.2 copy.68
  206.1 16.5 %while.28 = (s32[]{:T(128)}, bf16[2,1024,2,128]{1,3,2,0:T(8,128)(2,1)}, f32[2,2,1024]{2,1,0:T(2,128)S(1)}, bf16[2,1024,128]{1,2,0:T(8,128)(2,1)S(1)}, bf16[2,102...) while((s32[]{:T(128)}, ...), condition=%wide.region_8.9_spmd.clone, body=%wide.region_5.8_spmd.clone.sunk | while | flops 1102313472 | bytes 31004760 | solution.py:176
  210.8 3.7 fusion.170
  219.0 3.7 fusion.170
  223.7 6.3 convolution_convert_fusion.4
  230.8 8.9 all-gather.1
  239.7 65.8 %reduce-scatter.12.cloned.1.call-done = bf16[256,2048]{1,0:T(8,128)(2,1)} async-done(((bf16[1024,2048]{1,0:T(8,128)(2,1)}), bf16[256,2048]{1,0:T(8,128)(2,1)}) %reduce-scatter.12.cloned.1.call-update) | async-done | bytes 1048592 | tf_op jit(solution)/shard_map/reduce_scatter | solution.py:181
  313.3 40.3 %all-gather.26.cloned.1.call-done = bf16[2048,1536]{1,0:T(8,128)(2,1)} async-done(((bf16[256,1536]{1,0:T(8,128)(2,1)}), bf16[2048,1536]{1,0:T(8,128)(2,1)}) %all-gather.26.cloned.1.call-update) | async-done | bytes 6291472 | tf_op jit(solution)/shard_map/all_gather | solution.py:148
  353.6 83.0 %all-gather.24.cloned.1.call-done = bf16[1024,2048]{1,0:T(8,128)(2,1)} async-done(((bf16[256,2048]{1,0:T(8,128)(2,1)}), bf16[1024,2048]{1,0:T(8,128)(2,1)}) %all-gather.24.cloned.1.call-update) | async-done | bytes 4194320 | tf_op jit(solution)/shard_map/all_gather | solution.py:189
  436.6 12.0 fusion.113
  448.6 34.2 %all-gather.28.cloned.1.call-done = bf16[2048,1536]{1,0:T(8,128)(2,1)} async-done(((bf16[256,1536]{1,0:T(8,128)(2,1)}), bf16[2048,1536]{1,0:T(8,128)(2,1)}) %all-gather.28.cloned.1.call-update) | async-done | bytes 6291472 | tf_op jit(solution)/shard_map/all_gather | solution.py:149
  482.7 11.7 fusion.114
  494.4 71.2 %all-gather.32.cloned.1.call-done = bf16[1024,2048]{1,0:T(8,128)(2,1)} async-done(((bf16[256,2048]{1,0:T(8,128)(2,1)}), bf16[1024,2048]{1,0:T(8,128)(2,1)}) %all-gather.32.cloned.1.call-update) | async-done | bytes 4194320 | tf_op jit(solution)/shard_map/all_gather | solution.py:217
  565.6 47.3 %all-gather.30.cloned.1.call-done = bf16[1536,2048]{1,0:T(8,128)(2,1)} async-done(((bf16[1536,256]{1,0:T(8,128)(2,1)}), bf16[1536,2048]{1,0:T(8,128)(2,1)}) %all-gather.30.cloned.1.call-update) | async-done | bytes 6291472 | tf_op jit(solution)/shard_map/all_gather | solution.py:150
  612.9 16.5 %multiply_convert_fusion = (bf16[1024,1536]{1,0:T(8,128)(2,1)}, bf16[1024,1536]{1,0:T(8,128)(2,1)S(1)}, bf16[1024,1536]{1,0:T(8,128)(2,1)}) fusion(f32[1024,1536]{1,0:T(8,128)} %fusion.113, f32[1024,1536]{1,0:T(8,128)} %fusion.114, bf16[1024,2048]{1,0:T(8,128)(2,1)} %all-gather.32.cloned.1.call-done, bf16[1536,2048]{1,0:T(8,128)(2,1)} %all-gather.30.cloned.1.call-done), kind=kOutput, calls=%fused_computation.75 | convolution fusion | flops 6467616768 | bytes 32505856 | tf_op jit(solution)/shard_map/dot_general | solution.py:54
  629.4 10.0 fusion.115
  639.4 10.6 add_convert_fusion
  650.1 11.1 convolution_convert_fusion.3
  661.3 65.7 %reduce-scatter.16.cloned.1.call-done = bf16[256,2048]{1,0:T(8,128)(2,1)} async-done(((bf16[1024,2048]{1,0:T(8,128)(2,1)}), bf16[256,2048]{1,0:T(8,128)(2,1)}) %reduce-scatter.16.cloned.1.call-update) | async-done | bytes 1048592 | tf_op jit(solution)/shard_map/reduce_scatter | solution.py:226
  729.5 77.1 %reduce-scatter.14.cloned.1.call-done = bf16[256,2048]{1,0:T(8,128)(2,1)} async-done(((bf16[1024,2048]{1,0:T(8,128)(2,1)}), bf16[256,2048]{1,0:T(8,128)(2,1)}) %reduce-scatter.14.cloned.1.call-update) | async-done | bytes 1048592 | tf_op jit(solution)/shard_map/reduce_scatter | solution.py:194
  806.6 5.0 fusion.106
  811.7 11.5 convolution_convert_fusion.2
  823.3 11.7 convolution_convert_fusion.1
  838.3 11.3 convolution_convert_fusion
  849.7 43.4 %all-gather.34.cloned.1.call-done = bf16[1024,2048]{1,0:T(8,128)(2,1)} async-done(((bf16[256,2048]{1,0:T(8,128)(2,1)}), bf16[1024,2048]{1,0:T(8,128)(2,1)}) %all-gather.34.cloned.1.call-update) | async-done | bytes 4194320 | tf_op jit(solution)/shard_map/all_gather | solution.py:237
  893.1 6.2 convolution_convert_fusion.8
  901.8 27.5 %while.29 = (s32[]{:T(128)}, f32[2,1024,2,128]{1,3,2,0:T(8,128)}, f32[2,1024,128]{2,1,0:T(8,128)}, bf16[2,1024,128]{2,1,0:T(8,128)(2,1)}, bf16[2,1024,128]{2,1,0...) while((s32[]{:T(128)}, f32[2,1024,2,128]{1,3,2,0:T(8,128)}, ...), condition=%wide.region_16.17_spmd.clone, body=%wide.region_14.16_spmd.clone.sunk | while | flops 2719348736 | bytes 101516552 | solution.py:243
  942.2 6.3 convolution_convert_fusion.5
  952.9 6.2 convolution_convert_fusion.7
  959.2 3.1 slice.71
  962.4 8.4 convolution_convert_fusion.6
  974.9 47.1 %reduce-scatter.30.cloned.1.call-done = bf16[256,1536]{1,0:T(8,128)(2,1)} async-done(((bf16[2048,1536]{1,0:T(8,128)(2,1)}), bf16[256,1536]{1,0:T(8,128)(2,1)}) %reduce-scatter.30.cloned.1.call-update) | async-done | bytes 786448 | tf_op jit(solution)/shard_map/reduce_scatter | solution.py:306
  1024.5 62.9 %reduce-scatter.32.cloned.1.call-done = bf16[1536,256]{1,0:T(8,128)(2,1)} async-done(((bf16[1536,2048]{1,0:T(8,128)(2,1)}), bf16[1536,256]{1,0:T(8,128)(2,1)}) %reduce-scatter.32.cloned.1.call-update) | async-done | bytes 786448 | tf_op jit(solution)/shard_map/reduce_scatter | solution.py:309
  1089.8 36.7 %reduce-scatter.22.cloned.1.call-done = bf16[256,256]{1,0:T(8,128)(2,1)} async-done(((bf16[2048,256]{1,0:T(8,128)(2,1)}), bf16[256,256]{1,0:T(8,128)(2,1)}) %reduce-scatter.22.cloned.1.call-update) | async-done | bytes 131088 | tf_op jit(solution)/shard_map/reduce_scatter | solution.py:285
  1128.0 37.6 %reduce-scatter.24.cloned.1.call-done = bf16[256,256]{1,0:T(8,128)(2,1)} async-done(((bf16[2048,256]{1,0:T(8,128)(2,1)}), bf16[256,256]{1,0:T(8,128)(2,1)}) %reduce-scatter.24.cloned.1.call-update) | async-done | bytes 131088 | tf_op jit(solution)/shard_map/reduce_scatter | solution.py:288
  1167.3 42.8 %reduce-scatter.26.cloned.1.call-done = bf16[512,256]{1,0:T(8,128)(2,1)} async-done(((bf16[512,2048]{1,0:T(8,128)(2,1)}), bf16[512,256]{1,0:T(8,128)(2,1)}) %reduce-scatter.26.cloned.1.call-update) | async-done | bytes 262160 | tf_op jit(solution)/shard_map/reduce_scatter | solution.py:297
  1211.8 43.1 %reduce-scatter.20.cloned.1.call-done = bf16[256,512]{1,0:T(8,128)(2,1)} async-done(((bf16[2048,512]{1,0:T(8,128)(2,1)}), bf16[256,512]{1,0:T(8,128)(2,1)}) %reduce-scatter.20.cloned.1.call-update) | async-done | bytes 262160 | tf_op jit(solution)/shard_map/reduce_scatter | solution.py:282
  1256.7 77.3 %reduce-scatter.18.cloned.1.call-done = bf16[256,2048]{1,0:T(8,128)(2,1)} async-done(((bf16[1024,2048]{1,0:T(8,128)(2,1)}), bf16[256,2048]{1,0:T(8,128)(2,1)}) %reduce-scatter.18.cloned.1.call-update) | async-done | bytes 1048592 | tf_op jit(solution)/shard_map/reduce_scatter | solution.py:266
  1335.9 18.2 %all-reduce.6 = (bf16[2048]{0:T(1024)(128)(2,1)S(1)}, bf16[128]{0:T(256)(128)(2,1)S(1)}, bf16[128]{0:T(256)(128)(2,1)S(1)}, bf16[2048]{0:T(1024)(128)(2,1)S(1)}) all-reduce(f32[2048]{0:T(1024)S(1)} %get-tuple-element.175, f32[128]{0:T(128)S(1)} %bitcast_reduce_fusion, ...), channel_id=1, replica_groups=mesh['dp'=8,'tensor'=4] {'tensor'}, use_global_device_ids=true, to_apply=%region_22.23 | all-reduce | flops 4352 | bytes 26112 | tf_op jit(solution)/shard_map/psum | solution.py:276
  1354.1 12.3 all-reduce.7
  (279 shorter events, 130.5 us)
Async XLA Ops:
  7.2 22.6 %copy-start.48 = (u32[32]{0:T(128)S(1)}, u32[32]{0:T(128)}, u32[]{:S(2)}) copy-start(u32[32]{0:T(128)} %constant.97) | copy-start | bytes 388
  7.2 19.2 %copy-start.51 = (s32[8]{0:T(128)S(1)}, s32[8]{0:T(128)}, u32[]{:S(2)}) copy-start(s32[8]{0:T(128)} %param.33) | copy-start | bytes 100
  7.2 19.8 %copy-start.52 = (s32[8]{0:T(128)S(1)}, s32[8]{0:T(128)}, u32[]{:S(2)}) copy-start(s32[8]{0:T(128)} %param.32) | copy-start | bytes 100
  7.2 23.8 %copy-start.53 = (bf16[16]{0:T(256)(128)(2,1)S(1)}, bf16[16]{0:T(256)(128)(2,1)}, u32[]{:S(2)}) copy-start(bf16[16]{0:T(256)(128)(2,1)} %param.25) | copy-start | bytes 100
  7.2 24.1 %copy-start.54 = (bf16[16]{0:T(256)(128)(2,1)S(1)}, bf16[16]{0:T(256)(128)(2,1)}, u32[]{:S(2)}) copy-start(bf16[16]{0:T(256)(128)(2,1)} %param.24) | copy-start | bytes 100
  7.2 40.8 %all-gather.16.cloned.1.call-start = ((), (), s32[]{:S(2)}) async-start(), calls=%async_computation.12 | async-start | bytes 2359296 | tf_op jit(solution)/shard_map/all_gather | solution.py:141
  8.0 58.1 %all-gather.18.cloned.1.call-start = ((), (), s32[]{:S(2)}) async-start(), calls=%async_computation.13 | async-start | bytes 1179648 | tf_op jit(solution)/shard_map/all_gather | solution.py:142
  8.7 82.8 %all-gather.20.cloned.1.call-start = ((), (), s32[]{:S(2)}) async-start(), calls=%async_computation.14 | async-start | bytes 1179648 | tf_op jit(solution)/shard_map/all_gather | solution.py:143
  9.5 164.9 %all-gather.14.cloned.1.call-start = ((), (), s32[]{:S(2)}) async-start(), calls=%async_computation.11 | async-start | bytes 5242880 | tf_op jit(solution)/shard_map/all_gather | solution.py:158
  25.7 197.0 %all-gather.22.cloned.1.call-start = ((), (), s32[]{:S(2)}) async-start(), calls=%async_computation.15 | async-start | bytes 2359296 | tf_op jit(solution)/shard_map/all_gather | solution.py:146
  26.3 279.2 %reduce-scatter.12.cloned.1.call-start = ((), (), s32[]{:S(2)}) async-start(), calls=%async_computation.16 | async-start | bytes 5242880 | tf_op jit(solution)/shard_map/reduce_scatter | solution.py:181
  44.9 155.3 %copy-start.45 = (f32[128]{0:T(128)}, f32[128]{0:T(128)S(1)}, u32[]{:S(2)}) copy-start(f32[128]{0:T(128)S(1)} %convert_element_type.188) | copy-start | bytes 1540
  48.0 155.0 %copy-start.43 = (f32[128]{0:T(128)}, f32[128]{0:T(128)S(1)}, u32[]{:S(2)}) copy-start(f32[128]{0:T(128)S(1)} %convert_element_type.191) | copy-start | bytes 1540
  185.4 14.9 %copy-start.34 = (f32[1024,2]{0,1:T(2,128)}, f32[1024,2]{0,1:T(2,128)S(1)}, u32[]{:S(2)}) copy-start(f32[1024,2]{0,1:T(2,128)S(1)} %get-tuple-element.251) | copy-start | bytes 24580
  185.7 14.5 %copy-start.4 = (f32[1024,2,128]{2,0,1:T(8,128)}, f32[1024,2,128]{2,0,1:T(8,128)S(1)}, u32[]{:S(2)}) copy-start(f32[1024,2,128]{2,0,1:T(8,128)S(1)} %copy.66) | copy-start | bytes 3145732
  191.8 6.5 slice-start
  230.0 75.5 %copy-start = (bf16[256,2048]{1,0:T(8,128)(2,1)S(1)}, bf16[256,2048]{1,0:T(8,128)(2,1)}, u32[]{:S(2)}) copy-start(bf16[256,2048]{1,0:T(8,128)(2,1)} %param.19) | copy-start | bytes 3145732
  230.0 81.3 %copy-start.23 = (bf16[256,2048]{1,0:T(8,128)(2,1)S(1)}, bf16[256,2048]{1,0:T(8,128)(2,1)}, u32[]{:S(2)}) copy-start(bf16[256,2048]{1,0:T(8,128)(2,1)} %param.31) | copy-start | bytes 3145732
  230.0 123.6 %all-gather.26.cloned.1.call-start = ((), (), s32[]{:S(2)}) async-start(), calls=%async_computation.18 | async-start | bytes 7077888 | tf_op jit(solution)/shard_map/all_gather | solution.py:148
  230.8 205.9 %all-gather.24.cloned.1.call-start = ((), (), s32[]{:S(2)}) async-start(), calls=%async_computation.17 | async-start | bytes 5242880 | tf_op jit(solution)/shard_map/all_gather | solution.py:189
  309.8 173.0 %all-gather.28.cloned.1.call-start = ((), (), s32[]{:S(2)}) async-start(), calls=%async_computation.19 | async-start | bytes 7077888 | tf_op jit(solution)/shard_map/all_gather | solution.py:149
  310.5 255.1 %all-gather.32.cloned.1.call-start = ((), (), s32[]{:S(2)}) async-start(), calls=%async_computation.22 | async-start | bytes 5242880 | tf_op jit(solution)/shard_map/all_gather | solution.py:217
  312.5 300.3 %all-gather.30.cloned.1.call-start = ((), (), s32[]{:S(2)}) async-start(), calls=%async_computation.20 | async-start | bytes 7077888 | tf_op jit(solution)/shard_map/all_gather | solution.py:150
  313.3 413.7 %reduce-scatter.16.cloned.1.call-start = ((), (), s32[]{:S(2)}) async-start(), calls=%async_computation.23 | async-start | bytes 5242880 | tf_op jit(solution)/shard_map/reduce_scatter | solution.py:226
  629.4 10.0 copy-start.56
  629.4 10.0 copy-start.49
  650.1 156.5 %reduce-scatter.14.cloned.1.call-start = ((), (), s32[]{:S(2)}) async-start(), calls=%async_computation.21 | async-start | bytes 5242880 | tf_op jit(solution)/shard_map/reduce_scatter | solution.py:194
  661.2 65.8 %copy-start.9 = (bf16[256,2048]{1,0:T(8,128)(2,1)S(1)}, bf16[256,2048]{1,0:T(8,128)(2,1)}, u32[]{:S(2)}) copy-start(bf16[256,2048]{1,0:T(8,128)(2,1)} %reduce-scatter.12.cloned.1.call-done) | copy-start | bytes 3145732
  661.2 231.8 %all-gather.34.cloned.1.call-start = ((), (), s32[]{:S(2)}) async-start(), calls=%async_computation.24 | async-start | bytes 5242880 | tf_op jit(solution)/shard_map/all_gather | solution.py:237
  811.7 160.5 %reduce-scatter.28.cloned.1.call-start = ((), (), s32[]{:S(2)}) async-start(), calls=%async_computation.30 | async-start | bytes 7077888 | tf_op jit(solution)/shard_map/reduce_scatter | solution.py:303
  823.2 198.8 %reduce-scatter.30.cloned.1.call-start = ((), (), s32[]{:S(2)}) async-start(), calls=%async_computation.31 | async-start | bytes 7077888 | tf_op jit(solution)/shard_map/reduce_scatter | solution.py:306
  835.0 252.4 %reduce-scatter.32.cloned.1.call-start = ((), (), s32[]{:S(2)}) async-start(), calls=%async_computation.32 | async-start | bytes 7077888 | tf_op jit(solution)/shard_map/reduce_scatter | solution.py:309
  849.7 52.1 %copy-start.15 = (bf16[2,1024,2,128]{3,1,2,0:T(8,128)(2,1)S(1)}, bf16[2,1024,2,128]{3,1,2,0:T(8,128)(2,1)}, u32[]{:S(2)}) copy-start(bf16[2,1024,2,128]{3,1,2,0:T(8,128)(2,1)} %copy-done.14) | copy-start | bytes 3145732
  849.7 276.8 %reduce-scatter.22.cloned.1.call-start = ((), (), s32[]{:S(2)}) async-start(), calls=%async_computation.27 | async-start | bytes 1179648 | tf_op jit(solution)/shard_map/reduce_scatter | solution.py:285
  931.1 5.3 copy-start.8
  931.2 5.3 copy-start.25
  952.1 213.5 %reduce-scatter.24.cloned.1.call-start = ((), (), s32[]{:S(2)}) async-start(), calls=%async_computation.28 | async-start | bytes 1179648 | tf_op jit(solution)/shard_map/reduce_scatter | solution.py:288
  952.9 257.1 %reduce-scatter.26.cloned.1.call-start = ((), (), s32[]{:S(2)}) async-start(), calls=%async_computation.29 | async-start | bytes 2359296 | tf_op jit(solution)/shard_map/reduce_scatter | solution.py:297
  959.1 3.3 copy-start.29
  959.1 3.3 copy-start.31
  959.1 295.8 %reduce-scatter.20.cloned.1.call-start = ((), (), s32[]{:S(2)}) async-start(), calls=%async_computation.26 | async-start | bytes 2359296 | tf_op jit(solution)/shard_map/reduce_scatter | solution.py:282
  962.3 371.7 %reduce-scatter.18.cloned.1.call-start = ((), (), s32[]{:S(2)}) async-start(), calls=%async_computation.25 | async-start | bytes 5242880 | tf_op jit(solution)/shard_map/reduce_scatter | solution.py:266
  972.1 361.9 %copy-start.1 = (bf16[256,2048]{1,0:T(8,128)(2,1)S(1)}, bf16[256,2048]{1,0:T(8,128)(2,1)}, u32[]{:S(2)}) copy-start(bf16[256,2048]{1,0:T(8,128)(2,1)} %param.19) | copy-start | bytes 3145732
  972.1 361.9 %copy-start.37 = (f32[8,1,256]{2,1,0:T(1,128)S(1)}, f32[8,1,256]{2,1,0:T(1,128)}, u32[]{:S(2)}) copy-start(f32[8,1,256]{2,1,0:T(1,128)} %copy-done.36) | copy-start | bytes 24580
  972.2 361.8 %copy-start.42 = (f32[256]{0:T(256)S(1)}, f32[256]{0:T(256)}, u32[]{:S(2)}) copy-start(f32[256]{0:T(256)} %copy-done.41) | copy-start | bytes 3076
  974.9 361.0 %copy-start.40 = (f32[2048]{0:T(1024)S(1)}, f32[2048]{0:T(1024)}, u32[]{:S(2)}) copy-start(f32[2048]{0:T(1024)} %get-tuple-element.171) | copy-start | bytes 24580
  974.9 392.8 %copy-start.17 = (f32[256,2048]{1,0:T(8,128)S(1)}, f32[256,2048]{1,0:T(8,128)}, u32[]{:S(2)}) copy-start(f32[256,2048]{1,0:T(8,128)} %get-tuple-element.223) | copy-start | bytes 6291460
  974.9 392.8 %copy-start.47 = (f32[256]{0:T(256)S(1)}, f32[256]{0:T(256)}, u32[]{:S(2)}) copy-start(f32[256]{0:T(256)} %get-tuple-element.252) | copy-start | bytes 3076
  (37 other events, 68.7 us)
Sparse Core Ops, SparseCore 0:
  10.0 30.6 all-gather.15
  42.5 23.5 all-gather.17
  68.0 23.4 all-gather.19
  93.5 80.7 all-gather.13
  176.0 26.7 all-gather.21
  230.1 75.3 reduce-scatter.11
  307.5 46.0 all-gather.25
  355.8 80.7 all-gather.23
  438.7 44.0 all-gather.27
  484.8 80.7 all-gather.31
  567.6 45.1 all-gather.29
  650.2 76.7 reduce-scatter.15
  729.3 77.2 reduce-scatter.13
  811.8 81.2 all-gather.33
  896.7 60.2 reduce-scatter.27
  960.2 61.7 reduce-scatter.29
  1025.6 61.7 reduce-scatter.31
  1090.4 35.9 reduce-scatter.21
  1129.6 35.9 reduce-scatter.23
  1168.8 41.2 reduce-scatter.25
  1213.7 41.2 reduce-scatter.19
  1257.2 76.7 reduce-scatter.17
where the time goes:
time: 1390 us; the launch traced here: 1380 us
  waiting for transfers between devices  999 us (72%)
  matrix products  176 us (13%)
  other arithmetic  76.2 us (5%)
  blocking collectives  63.1 us (5%)
  local copies, waits for them, and re-layouts  44.3 us (3%)
  between operations  17.5 us (1%)
    all_gather x1, waiting for transfers between devices, local(): normed_ffn_all = lax.all_gather(normed_ffn, 'tensor', axis=0, tiled=True)  83 us
    all_gather x1, waiting for transfers between devices, local(): lax.all_gather(attention_normed_input, 'tensor', axis=0, tiled=True)  80.5 us
    reduce_scatter x1, waiting for transfers between devices, local(): lax.psum_scatter(times_transpose(d_projected, back_qkv).astype(jnp.bfloat...  77.3 us
    reduce_scatter x1, waiting for transfers between devices, local(): lax.psum_scatter(jnp.dot(activation, full_set[10], preferred_element_type...  77.1 us
    all_gather x1, waiting for transfers between devices, local(): d_branch_all = lax.all_gather(d_branch, 'tensor', axis=0, tiled=True)  71.2 us
    reduce_scatter x1, waiting for transfers between devices, local(): lax.psum_scatter(jnp.dot(context, full_set[6], preferred_element_type=jnp...  65.8 us
    reduce_scatter x1, waiting for transfers between devices, local(): lax.psum_scatter((times_transpose(d_gate, back_set[8]) + times_transpose(...  65.7 us
    reduce_scatter x1, waiting for transfers between devices, local(): lax.psum_scatter(grad_down.astype(jnp.bfloat16), 'dp', scatter_dimension=...  62.9 us
  transfers between devices with their start and end apart: 22, of which 19 were waited for; matrix products, arithmetic and copies ran while one was open for 17% of the time, Pallas kernels for 0%

commit v1 on v0

v1 whole, which is shorter than its diff:
```python
import functools

import jax
import jax.numpy as jnp
from jax import lax
from jax.experimental import pallas as pl
from jax.experimental.pallas import tpu as pltpu
from jax.sharding import PartitionSpec as P

QUERY_HEADS = 16
KEY_VALUE_HEADS = 8
HEAD_SIZE = 128

norm_eps = 1e-06
rope_base = 1000000.0
score_scale = HEAD_SIZE ** (-0.5)
f32 = jnp.float32
bf16 = jnp.bfloat16
WAYS = 4
ROOM = 58 << 20


def nn(left, right):
    return lax.dot_general(left, right, (((1,), (0,)), ((), ())), preferred_element_type=f32)


def nt(left, right):
    return lax.dot_general(left, right, (((1,), (1,)), ((), ())), preferred_element_type=f32)


def tn(left, right):
    return lax.dot_general(left, right, (((0,), (0,)), ((), ())), preferred_element_type=f32)


def rms_scale(value_vectors):
    return lax.rsqrt(jnp.mean(value_vectors * value_vectors, axis=-1, keepdims=True) + norm_eps)


def norm_back(d_unit, pre_values, pre_scale, gain_values):
    mixed_terms = gain_values * d_unit
    return pre_scale * mixed_terms - pre_values * pre_scale**3 * jnp.mean(
        mixed_terms * pre_values, axis=-1, keepdims=True
    )


def rope_tables(position):
    half_dim = HEAD_SIZE // 2
    inverse_freq = rope_base ** (-2.0 * jnp.arange(half_dim, dtype=f32) / HEAD_SIZE)
    angles = position.astype(f32)[:, None] * inverse_freq[None, :]
    cosine, sine = jnp.cos(angles), jnp.sin(angles)
    return jnp.concatenate([cosine, cosine], axis=1), jnp.concatenate([-sine, sine], axis=1)


def sequence_length(lengths, deal_order, group_id):
    slots = jnp.arange(deal_order.shape[0], dtype=jnp.int32)
    seq_taken = jnp.sum(jnp.where(slots == group_id, deal_order, 0))
    return jnp.sum(jnp.where(slots == seq_taken, lengths, 0))


def shift_by(value, step):
    return lax.ppermute(value, "tensor", [(i, (i + step) % WAYS) for i in range(WAYS)])


def hop(value):
    return shift_by(value, 1)


def together(*values):
    return lax.optimization_barrier(values)


def add(block, arrived):
    return (block.astype(f32) + arrived.astype(f32)).astype(bf16)


def whole(shape, index=None):
    rank = len(shape)
    place = index if index is not None else (0,) * rank
    return pl.BlockSpec(shape, lambda *_: place, pipeline_mode=pl.Buffered(1))


def call(kernel, grid, in_specs, outs, out_specs, scratch=(), flops=0, size=0, exps=0):
    return pl.pallas_call(
        kernel,
        grid=grid,
        in_specs=in_specs,
        out_shape=[jax.ShapeDtypeStruct(s, d) for s, d in outs],
        out_specs=out_specs,
        scratch_shapes=list(scratch),
        compiler_params=pltpu.CompilerParams(vmem_limit_bytes=ROOM),
        cost_estimate=pl.CostEstimate(flops=flops, bytes_accessed=size, transcendentals=exps),
    )


def pick_slot(step, slots, x_s):
    for j, ref in enumerate(slots):

        @pl.when(step == j)
        def _():
            x_s[...] = ref[...]


def project_kernel(own, below, far, above, w, gain, gain_q, gain_k, cos, sin, normed, qkv, pre, x_s):
    pick_slot(pl.program_id(0), (own, below, far, above), x_s)
    x = x_s[...].astype(f32)
    n = (x * rms_scale(x) * gain[...]).astype(bf16)
    normed[...] = n
    projected = nn(n, w[...])
    heads = pre.shape[1] // HEAD_SIZE
    queries = heads * 2 // 3
    pre[...] = projected[:, : heads * HEAD_SIZE]
    c, s = cos[...], sin[...]
    for h in range(heads):
        cols = slice(h * HEAD_SIZE, (h + 1) * HEAD_SIZE)
        head = projected[:, cols]
        unit = head * rms_scale(head) * (gain_q[...] if h < queries else gain_k[...])
        qkv[:, cols] = (unit * c + pltpu.roll(unit, HEAD_SIZE // 2, 1) * s).astype(bf16)
    qkv[:, heads * HEAD_SIZE :] = projected[:, heads * HEAD_SIZE :].astype(bf16)


def project(x_slots, w, gain, gain_q, gain_k, cos, sin):
    rows, width = x_slots[0].shape
    cols = 1024
    pre_cols = 768
    tile = lambda c: pl.BlockSpec((rows, c), lambda j: (j, 0))
    return call(
        project_kernel,
        (WAYS,),
        [whole(x.shape) for x in x_slots]
        + [whole((width, cols)), whole(gain.shape), whole(gain_q.shape), whole(gain_k.shape)]
        + [tile(HEAD_SIZE), tile(HEAD_SIZE)],
        [((WAYS * rows, width), bf16), ((WAYS * rows, cols), bf16), ((WAYS * rows, pre_cols), f32)],
        [tile(width), tile(cols), tile(pre_cols)],
        [pltpu.VMEM((rows, width), bf16)],
        flops=2 * WAYS * rows * width * cols,
        size=20 << 20,
    )(*x_slots, w, gain, gain_q, gain_k, cos, sin)


def shard_starts(place, size):
    return [pl.multiple_of(lax.rem(place[0] + WAYS - s, WAYS) * size, size) for s in range(WAYS)]


def causal_fill(scores):
    row = lax.broadcasted_iota(jnp.int32, scores.shape, 0)
    col = lax.broadcasted_iota(jnp.int32, scores.shape, 1)
    return jnp.where(col <= row, scores, -1e30)


def attend_kernel(place, q, k, v, ctx, lse):
    size = q.shape[0] // WAYS
    starts = shard_starts(place, size)
    for s in range(WAYS):
        rows = pl.ds(starts[s], size)
        for g in range(q.shape[1] // HEAD_SIZE):
            cols = slice(g * HEAD_SIZE, (g + 1) * HEAD_SIZE)
            query = q[rows, cols]
            blocks = []
            for t in range(s + 1):
                scores = nt(query, k[pl.ds(starts[t], size), :])
                blocks.append(causal_fill(scores) if t == s else scores)
            top = functools.reduce(
                jnp.maximum, [jnp.max(b, axis=-1, keepdims=True) for b in blocks]
            )
            raised = [jnp.exp((b - top) * score_scale) for b in blocks]
            summed = functools.reduce(
                jnp.add, [jnp.sum(b, axis=-1, keepdims=True) for b in raised]
            )
            inverse = 1.0 / summed
            out = functools.reduce(
                jnp.add,
                [
                    nn((b * inverse).astype(bf16), v[pl.ds(starts[t], size), :])
                    for t, b in enumerate(raised)
                ],
            )
            ctx[rows, cols] = out.astype(bf16)
            lse[rows, g : g + 1] = top * score_scale + jnp.log(summed)


def attend(place, qkv):
    rows = qkv.shape[0]
    pairs = 2
    return call(
        attend_kernel,
        (pairs,),
        [
            pl.BlockSpec(memory_space=pltpu.SMEM),
            pl.BlockSpec((rows, 2 * HEAD_SIZE), lambda p: (0, p)),
            pl.BlockSpec((rows, HEAD_SIZE), lambda p: (0, 4 + p)),
            pl.BlockSpec((rows, HEAD_SIZE), lambda p: (0, 6 + p)),
        ],
        [((rows, 4 * HEAD_SIZE), bf16), ((rows, 2 * HEAD_SIZE), f32)],
        [
            pl.BlockSpec((rows, 2 * HEAD_SIZE), lambda p: (0, p)),
            pl.BlockSpec((rows, HEAD_SIZE), lambda p: (0, p)),
        ],
        flops=8 * rows * rows * HEAD_SIZE,
        size=2 << 20,
        exps=2 * rows * rows,
    )(place, qkv, qkv, qkv)


def mix_kernel(own, below, far, above, c0, c1, c2, c3, w, gain, normed, hidden, ctx_rows, acc, c_s):
    k = pl.program_id(0)
    size = own.shape[0]

    @pl.when(k == 0)
    def _():
        for i, ref in enumerate((own, below, far, above)):
            acc[i * size : (i + 1) * size] = ref[...].astype(f32)

    for kk, ref in enumerate((c0, c1, c2, c3)):

        @pl.when(k == kk)
        def _():
            for i in range(WAYS):
                source = (i - kk) % WAYS
                c_s[i * size : (i + 1) * size] = ref[source * size : (source + 1) * size]

    ctx_rows[...] = c_s[:size]
    for i in range(WAYS):
        rows = slice(i * size, (i + 1) * size)
        acc[rows] += nt(c_s[rows], w[...])

    @pl.when(k == WAYS - 1)
    def _():
        hidden[...] = acc[:size]
        for i in range(WAYS):
            rows = slice(i * size, (i + 1) * size)
            h = acc[rows]
            normed[rows] = (h * rms_scale(h) * gain[...]).astype(bf16)


def mix(x_slots, contexts, w_out_full, gain):
    size, width = x_slots[0].shape
    rows, inner = contexts[0].shape
    return call(
        mix_kernel,
        (WAYS,),
        [whole(x.shape) for x in x_slots]
        + [whole(c.shape) for c in contexts]
        + [pl.BlockSpec((width, inner), lambda k: (0, k)), whole(gain.shape)],
        [((rows, width), bf16), ((size, width), f32), ((size, WAYS * inner), bf16)],
        [whole((rows, width)), whole((size, width)), pl.BlockSpec((size, inner), lambda k: (0, k))],
        [pltpu.VMEM((rows, width), f32), pltpu.VMEM((rows, inner), bf16)],
        flops=2 * rows * width * WAYS * inner,
        size=24 << 20,
    )(*x_slots, *contexts, w_out_full, gain)


def feed_kernel(n, w_gate, w_up, out):
    size = 256
    for i in range(n.shape[0] // size):
        rows = slice(i * size, (i + 1) * size)
        gate = nn(n[rows], w_gate[...])
        up = nn(n[rows], w_up[...])
        sig = 1.0 / (1.0 + jnp.exp(-gate))
        silu = gate * sig
        out[0, rows] = (up * sig * (1.0 + gate * (1.0 - sig))).astype(bf16)
        out[1, rows] = silu.astype(bf16)
        out[2, rows] = (silu * up).astype(bf16)


def feed(normed, weights, ff_width):
    rows, width = normed.shape
    tile = 256
    tiles = ff_width // tile
    col = lambda c: pl.BlockSpec((width, tile), lambda j: (0, c * tiles + j))
    return call(
        feed_kernel,
        (tiles,),
        [whole((rows, width)), col(0), col(1)],
        [((3, rows, ff_width), bf16)],
        [pl.BlockSpec((3, rows, tile), lambda j: (0, 0, j))],
        flops=4 * rows * width * ff_width,
        size=26 << 20,
        exps=rows * ff_width,
    )(normed, weights, weights)[0]


def feed_back_kernel(d, w_down, slopes, out):
    size = 256
    for i in range(d.shape[0] // size):
        rows = slice(i * size, (i + 1) * size)
        d_act = nn(d[rows], w_down[...])
        out[0, rows] = (d_act * slopes[0, rows].astype(f32)).astype(bf16)
        out[1, rows] = (d_act * slopes[1, rows].astype(f32)).astype(bf16)


def feed_back(d_branch, w_down, forward):
    rows, width = d_branch.shape
    ff_width = forward.shape[2]
    tile = 256
    return call(
        feed_back_kernel,
        (ff_width // tile,),
        [
            whole((rows, width)),
            pl.BlockSpec((width, tile), lambda j: (0, j)),
            pl.BlockSpec((2, rows, tile), lambda j: (0, 0, j)),
        ],
        [((2, rows, ff_width), bf16)],
        [pl.BlockSpec((2, rows, tile), lambda j: (0, 0, j))],
        flops=2 * rows * width * ff_width,
        size=22 << 20,
    )(d_branch, w_down, forward)[0]


def back_kernel(slots, size, lone, a, b, wa, wb, *outs):
    for slot, out in zip(slots, outs):
        rows = slice(0, size) if lone else slice(slot * size, (slot + 1) * size)
        out[...] = (nt(a[0, rows], wa[...]) + nt(b[0, rows], wb[...])).astype(bf16)


def slot_shapes(slots, size, width, tile):
    return [((size, width), bf16) for _ in slots], [
        pl.BlockSpec((size, tile), lambda n: (0, n)) for _ in slots
    ]


def back_feed(d_all, weights, slots, width, size):
    ff_width = d_all.shape[2]
    tile = 512
    lone = len(slots) == 1
    rows = size if lone else WAYS * size
    row_at = slots[0] if lone else 0
    outs, out_specs = slot_shapes(slots, size, width, tile)
    return call(
        functools.partial(back_kernel, slots, size, lone),
        (width // tile,),
        [
            whole((1, rows, ff_width), (0, row_at, 0)),
            whole((1, rows, ff_width), (1, row_at, 0)),
            pl.BlockSpec((tile, ff_width), lambda n: (n, 0)),
            pl.BlockSpec((tile, ff_width), lambda n: (n, 1)),
        ],
        outs,
        out_specs,
        flops=4 * len(slots) * size * width * ff_width,
        size=20 << 20,
    )(d_all, d_all, weights, weights)


def down_kernel(slots, size, a, wa, *outs):
    for slot, out in zip(slots, outs):
        out[...] = nt(a[0, slot * size : (slot + 1) * size], wa[...]).astype(bf16)


def down(d_all, weights, slots, width, size):
    ff_width = d_all.shape[2]
    tile = 512
    rows = WAYS * size
    outs, out_specs = slot_shapes(slots, size, width, tile)
    return call(
        functools.partial(down_kernel, slots, size),
        (width // tile,),
        [whole((1, rows, ff_width), (2, 0, 0)), pl.BlockSpec((tile, ff_width), lambda n: (n, 0))],
        outs,
        out_specs,
        flops=2 * rows * width * ff_width,
        size=14 << 20,
    )(d_all, weights)


def grads_kernel(n, a, out):
    width = a.shape[2]
    n_tile = n[...]
    for c in range(a.shape[0]):
        out[:, c * width : (c + 1) * width] = tn(n_tile, a[c]).astype(bf16)


def row_grads(left, right, first, count):
    rows, width = left.shape
    cols = right.shape[2]
    tile = 256
    return call(
        grads_kernel,
        (width // tile,),
        [
            pl.BlockSpec((rows, tile), lambda j: (0, j)),
            whole((count, rows, cols), (first // count, 0, 0)),
        ],
        [((width, count * cols), bf16)],
        [pl.BlockSpec((tile, count * cols), lambda j: (j, 0))],
        flops=2 * rows * width * cols * count,
        size=(4 + 9 * count) << 20,
    )(left, right)[0]


def branch_kernel(own, arrived, hidden, cotangent, live, gain, w, d_hidden, d_attended, c0, c1, c2, c3):
    k = pl.program_id(0)

    @pl.when(k == 0)
    def _():
        d_normed = own[...].astype(f32) + arrived[...].astype(f32)
        h = hidden[...]
        total = cotangent[...].astype(f32) * live[...] + norm_back(
            d_normed, h, rms_scale(h), gain[...]
        )
        d_hidden[...] = total
        d_attended[...] = total.astype(bf16)

    value = nn(d_attended[...], w[...]).astype(bf16)
    for kk, ref in enumerate((c0, c1, c2, c3)):

        @pl.when(k == kk)
        def _():
            ref[...] = value


def branch(parts, hidden, cotangent, live, gain, w_out_full, inner):
    size, width = hidden.shape
    return call(
        branch_kernel,
        (WAYS,),
        [whole((size, width))] * 4
        + [whole(live.shape), whole(gain.shape), pl.BlockSpec((width, inner), lambda k: (0, k))],
        [((size, width), f32), ((size, width), bf16)] + [((size, inner), bf16)] * WAYS,
        [whole((size, width))] * 2 + [whole((size, inner))] * WAYS,
        flops=2 * size * width * WAYS * inner,
        size=16 << 20,
    )(*parts, hidden, cotangent, live, gain, w_out_full)


def head_back(d_head, pre_head, gain, c, s):
    d_unit = d_head * c - pltpu.roll(d_head, HEAD_SIZE // 2, 1) * s
    scale = rms_scale(pre_head)
    return norm_back(d_unit, pre_head, scale, gain), jnp.sum(
        d_unit * pre_head * scale, axis=0, keepdims=True
    )


def attend_back_kernel(place, q, k, v, d0, d1, d2, d3, lse, pre_q, pre_k, cos, sin, gain_q, gain_k, dq_out, dk_out, dv_out, sum_q, sum_k, d_s, dk, dv):
    size = q.shape[0] // WAYS
    starts = shard_starts(place, size)
    for slot, ref in enumerate((d0, d1, d2, d3)):
        d_s[slot * size : (slot + 1) * size] = ref[...]
    dk[...] = jnp.zeros_like(dk)
    dv[...] = jnp.zeros_like(dv)
    total_q = jnp.zeros((1, HEAD_SIZE), f32)
    for s in range(WAYS):
        rows = pl.ds(starts[s], size)
        for g in range(q.shape[1] // HEAD_SIZE):
            cols = slice(g * HEAD_SIZE, (g + 1) * HEAD_SIZE)
            query, d_out, log_total = q[rows, cols], d_s[rows, cols], lse[rows, g : g + 1]
            probs, d_probs = [], []
            for t in range(s + 1):
                seen = pl.ds(starts[t], size)
                scores = nt(query, k[seen, :]) * score_scale
                scores = causal_fill(scores) if t == s else scores
                probs.append(jnp.exp(scores - log_total))
                d_probs.append(nt(d_out, v[seen, :]))
            row_dot = functools.reduce(
                jnp.add, [jnp.sum(p * d, axis=-1, keepdims=True) for p, d in zip(probs, d_probs)]
            )
            d_query = jnp.zeros((size, HEAD_SIZE), f32)
            for t in range(s + 1):
                seen = pl.ds(starts[t], size)
                d_scores = (probs[t] * (d_probs[t] - row_dot)).astype(bf16)
                dv[seen, :] += tn(probs[t].astype(bf16), d_out)
                dk[seen, :] += tn(d_scores, query)
                d_query += nn(d_scores, k[seen, :])
            d_pre, part = head_back(
                d_query * score_scale, pre_q[rows, cols], gain_q[...], cos[rows, :], sin[rows, :]
            )
            dq_out[rows, cols] = d_pre.astype(bf16)
            total_q += part
    d_pre, part = head_back(dk[...] * score_scale, pre_k[...], gain_k[...], cos[...], sin[...])
    dk_out[...] = d_pre.astype(bf16)
    dv_out[...] = dv[...].astype(bf16)
    sum_q[...] = jnp.broadcast_to(total_q, sum_q.shape)
    sum_k[...] = jnp.broadcast_to(part, sum_k.shape)


def attend_back(place, qkv, d_slots, lse, pre, cos, sin, gain_q, gain_k):
    rows = qkv.shape[0]
    size = rows // WAYS
    one, two = HEAD_SIZE, 2 * HEAD_SIZE
    cols = lambda r, c, at=0: pl.BlockSpec((r, c), lambda p: (0, at + p))
    return call(
        attend_back_kernel,
        (2,),
        [pl.BlockSpec(memory_space=pltpu.SMEM), cols(rows, two), cols(rows, one, 4), cols(rows, one, 6)]
        + [cols(size, two)] * WAYS
        + [cols(rows, one), cols(rows, two), cols(rows, one, 4)]
        + [whole((rows, one)), whole((rows, one)), whole((1, one)), whole((1, one))],
        [
            ((rows, 2 * two), bf16),
            ((rows, two), bf16),
            ((rows, two), bf16),
            ((8, two), f32),
            ((8, two), f32),
        ],
        [cols(rows, two), cols(rows, one), cols(rows, one), cols(8, one), cols(8, one)],
        [pltpu.VMEM((rows, two), bf16), pltpu.VMEM((rows, one), f32), pltpu.VMEM((rows, one), f32)],
        flops=40 * rows * rows * HEAD_SIZE,
        size=12 << 20,
        exps=4 * rows * rows,
    )(place, qkv, qkv, qkv, *d_slots, lse, pre, pre, cos, sin, gain_q, gain_k)


def back_project_kernel(size, q, k, v, w, *outs):
    for slot, out in zip((1, 2, 3, 0), outs):
        rows = slice(slot * size, (slot + 1) * size)
        total = nt(q[rows], w[:, :512]) + nt(k[rows], w[:, 512:768]) + nt(v[rows], w[:, 768:])
        out[...] = total.astype(bf16)


def back_project(parts, w, width, size):
    tile = 512
    outs, out_specs = slot_shapes((1, 2, 3, 0), size, width, tile)
    return call(
        functools.partial(back_project_kernel, size),
        (width // tile,),
        [whole(p.shape) for p in parts] + [pl.BlockSpec((tile, 1024), lambda n: (n, 0))],
        outs,
        out_specs,
        flops=2 * WAYS * size * width * 1024,
        size=10 << 20,
    )(*parts, w)


def attend_grads_kernel(n, q, k, v, d, c, gains, out):
    n_tile = n[...]
    at = 0
    for ref in (q, k, v):
        wide = ref.shape[1]
        out[:, at : at + wide] = tn(n_tile, ref[...]).astype(bf16)
        at += wide
    out[:, at : at + c.shape[1]] = tn(d[...], c[...]).astype(bf16)
    out[:, at + c.shape[1] :] = gains[...]


def attend_grads(normed, parts, d_attended, ctx_rows, gains):
    rows, width = normed.shape
    tile = 256
    cols = sum(p.shape[1] for p in parts) + ctx_rows.shape[1] + gains.shape[1]
    return call(
        attend_grads_kernel,
        (width // tile,),
        [pl.BlockSpec((rows, tile), lambda j: (0, j))]
        + [whole(p.shape) for p in parts]
        + [
            pl.BlockSpec((d_attended.shape[0], tile), lambda j: (0, j)),
            whole(ctx_rows.shape),
            pl.BlockSpec((tile, gains.shape[1]), lambda j: (j, 0)),
        ],
        [((width, cols), bf16)],
        [pl.BlockSpec((tile, cols), lambda j: (j, 0))],
        flops=2 * rows * width * 1536,
        size=20 << 20,
    )(normed, *parts, d_attended, ctx_rows, gains)[0]


def local(
    tokens,
    norm_attn,
    w_query,
    key_matrix,
    value_matrix,
    gain_query,
    gain_key,
    w_output,
    norm_ffn,
    w_gate,
    w_up,
    w_down,
    cotangent,
    lengths,
    deal_order,
):
    place = lax.axis_index("tensor")
    data_ways = lax.axis_size("dp")
    size, width = tokens.shape
    shard_rows = norm_attn.shape[0]
    gain_rows = gain_query.shape[0]
    q_width = w_query.shape[1]
    kv_width = key_matrix.shape[1]
    qkv_width = q_width + 2 * kv_width
    ff_width = w_gate.shape[1]
    place_ref = place.reshape(1).astype(jnp.int32)

    x1 = hop(tokens)
    x2 = hop(x1)
    x3 = hop(x2)
    seq_len = sequence_length(lengths, deal_order, lax.axis_index("dp"))
    offsets = jnp.arange(size, dtype=jnp.int32)
    own_live = (place * size + offsets < seq_len).astype(f32)[:, None]
    x3, d_branch, w_out = together(x3, (cotangent.astype(f32) * own_live).astype(bf16), w_output.T)
    x_slots = [tokens, x1, x2, x3]
    d1 = hop(d_branch)
    w1 = hop(w_out)
    w2 = hop(w1)
    w3 = hop(w2)

    column = lambda v: jnp.pad(v, (0, shard_rows - v.shape[0]))[:, None]
    attn_part = jnp.concatenate(
        [w_query, key_matrix, value_matrix]
        + [column(v) for v in (norm_attn, norm_ffn, gain_query, gain_key)]
        + [jnp.zeros((shard_rows, 124), bf16)],
        axis=1,
    )
    attn_full = lax.all_gather(attn_part, "dp", axis=0, tiled=True)
    gain_block = attn_full[:, qkv_width : qkv_width + 4].astype(f32)
    norm_attn_all = gain_block[:, 0].reshape(1, width)
    norm_ffn_all = gain_block[:, 1].reshape(1, width)
    by_shard = gain_block.reshape(data_ways, shard_rows, 4)[:, :gain_rows]
    gain_q = by_shard[:, :, 2].reshape(1, HEAD_SIZE)
    gain_k = by_shard[:, :, 3].reshape(1, HEAD_SIZE)

    gate_up_full = lax.all_gather(
        jnp.concatenate([w_gate, w_up], axis=1), "dp", axis=0, tiled=True
    )
    w_out_full = lax.all_gather(
        jnp.concatenate([w_out, w1, w2, w3], axis=1), "dp", axis=0, tiled=True
    )
    down_full = lax.all_gather(w_down.T, "dp", axis=0, tiled=True)

    position = jnp.concatenate([((place - j) % WAYS) * size + offsets for j in range(WAYS)])
    cos, sin = rope_tables(position)

    normed_attn, qkv, pre = project(x_slots, attn_full, norm_attn_all, gain_q, gain_k, cos, sin)
    context, log_total = attend(place_ref, qkv)
    context, d1 = together(context, d1)
    c1 = hop(context)
    c2 = hop(c1)
    c3, d1 = together(hop(c2), d1)
    d2 = hop(d1)
    normed_ffn, hidden, ctx_rows = mix(x_slots, [context, c1, c2, c3], w_out_full, norm_ffn_all)

    normed_ffn, d2 = together(normed_ffn, d2)
    d3 = hop(d2)
    forward = feed(normed_ffn, gate_up_full, ff_width)
    d_branch_all = jnp.concatenate([d_branch, d1, d2, d3], axis=0)
    grads_down = row_grads(d_branch_all, forward, 2, 1)
    forward, grads_down = together(forward, grads_down)
    grads_down = lax.psum_scatter(grads_down, "dp", scatter_dimension=0, tiled=True)
    d_all = feed_back(d_branch_all, down_full, forward)
    (b1,) = back_feed(d_all, gate_up_full, (1,), width, size)
    b_sum = hop(b1)
    b2, b3, b0 = back_feed(d_all, gate_up_full, (2, 3, 0), width, size)
    b_sum, d_all = together(add(b2, b_sum), d_all)
    b_sum = hop(b_sum)
    grads_feed = row_grads(normed_ffn, d_all, 0, 2)
    b_sum, grads_feed, forward = together(add(b3, b_sum), grads_feed, forward)
    b_sum = hop(b_sum)
    y1, y2, y3, y0 = down(forward, down_full, (1, 2, 3, 0), width, size)
    b_sum, y1, y2, y3, y0 = together(b_sum, y1, y2, y3, y0)
    grads_feed, grads_down = together(grads_feed, grads_down)
    grads_feed = lax.psum_scatter(grads_feed, "dp", scatter_dimension=0, tiled=True)

    d_hidden, d_attended, p0, p1, p2, p3 = branch(
        (b0, b_sum), hidden, cotangent, own_live, norm_ffn_all, w_out_full, q_width
    )
    s1, s2, s3, y1 = together(shift_by(p3, 1), shift_by(p2, 2), shift_by(p1, -1), y1)
    y_sum = hop(y1)
    d_q, d_k, d_v, sum_q, sum_k = attend_back(
        place_ref, qkv, [p0, s1, s2, s3], log_total, pre, cos, sin, gain_q, gain_k
    )
    d_q, y_sum = together(d_q, y_sum)
    parts = (d_q, d_k, d_v)
    e1, e2, e3, e0 = back_project(parts, attn_full, width, size)
    e_sum, d_q = together(e1, d_q)
    parts = (d_q, d_k, d_v)
    e_sum = hop(e_sum)
    spread = lambda v: jnp.pad(
        v.reshape(data_ways, gain_rows), ((0, 0), (0, shard_rows - gain_rows))
    ).reshape(-1, 1)
    gains = jnp.concatenate(
        [
            spread(sum_q[0, :HEAD_SIZE] + sum_q[0, HEAD_SIZE:]),
            spread(sum_k[0, :HEAD_SIZE] + sum_k[0, HEAD_SIZE:]),
            jnp.zeros((width, 126), f32),
        ],
        axis=1,
    ).astype(bf16)
    grads_attn = attend_grads(normed_attn, parts, d_attended, ctx_rows, gains)
    grads_attn, grads_feed, e_sum = together(grads_attn, grads_feed, e_sum)
    grads_attn = lax.psum_scatter(grads_attn, "dp", scatter_dimension=0, tiled=True)
    e_sum = hop(add(e2, e_sum))
    e_sum, y_sum = together(hop(add(e3, e_sum)), y_sum)
    d_normed_attn = e0.astype(f32) + e_sum.astype(f32)

    y_sum = hop(add(y2, y_sum))
    y_sum = hop(add(y3, y_sum))
    ffn_out = y0.astype(f32) + y_sum.astype(f32)
    block_out = ((hidden + ffn_out) * own_live).astype(bf16)
    own_tokens = tokens.astype(f32)
    d_tokens = d_hidden + norm_back(d_normed_attn, own_tokens, rms_scale(own_tokens), norm_attn_all)

    grads_feed = grads_feed.astype(f32)
    grad_gate, grad_up = grads_feed[:, :ff_width], grads_feed[:, ff_width:]
    grad_down = grads_down.astype(f32).T
    grad_qkv = grads_attn[:, :qkv_width].astype(f32)
    grad_query = grad_qkv[:, :q_width]
    grad_key = grad_qkv[:, q_width : q_width + kv_width]
    grad_value = grad_qkv[:, q_width + kv_width :]
    g0, g1, g2, g3 = [
        grads_attn[:, qkv_width + k * q_width : qkv_width + (k + 1) * q_width] for k in range(WAYS)
    ]
    grad_output = (
        g0.astype(f32)
        + shift_by(g1, -1).astype(f32)
        + shift_by(g2, 2).astype(f32)
        + shift_by(g3, 1).astype(f32)
    ).T
    gain_sums = grads_attn[:gain_rows, qkv_width + WAYS * q_width :].astype(f32)
    own_attn = jnp.sum(
        attn_part[:, :qkv_width].astype(f32) * grad_qkv, axis=1
    ) / norm_attn.astype(f32)
    own_ffn = jnp.sum(
        w_gate.astype(f32) * grad_gate + w_up.astype(f32) * grad_up, axis=1
    ) / norm_ffn.astype(f32)
    small = jnp.concatenate([own_attn, own_ffn, gain_sums[:, 0], gain_sums[:, 1]])
    small = small + shift_by(small, 1)
    small = small + shift_by(small, 2)
    grad_norm_attn = small[:shard_rows]
    grad_norm_ffn = small[shard_rows : 2 * shard_rows]
    grad_gain_query = small[2 * shard_rows : 2 * shard_rows + gain_rows]
    grad_gain_key = small[2 * shard_rows + gain_rows :]
    return (
        block_out,
        d_tokens.astype(bf16),
        grad_norm_attn,
        grad_query,
        grad_key,
        grad_value,
        grad_gain_query,
        grad_gain_key,
        grad_output,
        grad_norm_ffn,
        grad_gate,
        grad_up,
        grad_down,
    )


def solution(mesh):
    return jax.shard_map(
        local,
        mesh=mesh,
        in_specs=(
            P(("dp", "tensor"), None),
            P("dp"),
            P("dp", "tensor"),
            P("dp", "tensor"),
            P("dp", "tensor"),
            P("dp"),
            P("dp"),
            P("tensor", "dp"),
            P("dp"),
            P("dp", "tensor"),
            P("dp", "tensor"),
            P("tensor", "dp"),
            P(("dp", "tensor"), None),
            P(),
            P(),
        ),
        out_specs=(
            P(("dp", "tensor"), None),
            P(("dp", "tensor"), None),
            P("dp"),
            P("dp", "tensor"),
            P("dp", "tensor"),
            P("dp", "tensor"),
            P("dp"),
            P("dp"),
            P("tensor", "dp"),
            P("dp"),
            P("dp", "tensor"),
            P("dp", "tensor"),
            P("tensor", "dp"),
        ),
        check_vma=False,
    )
```

time: 1390 us -> 638 us (0.46)
  waiting for transfers between devices: 999 us -> 337 us
  Pallas kernels: 0 us -> 191 us
  matrix products: 176 us -> 0 us
  blocking collectives: 63.1 us -> 0 us
  other arithmetic: 76.2 us -> 34.1 us
  starting transfers between devices: 0.88 us -> 34.2 us
  local copies, waits for them, and re-layouts: 44.3 us -> 23.1 us
    reduce_scatter x11 -> x3, waiting for transfers between devices: 556 us -> 0.02 us  [the longest x1 0.02 us: local(): lax.psum_scatter(grads_down, 'dp', scatter_dimension=0, tiled=True)]
    all_gather x11 -> x4, waiting for transfers between devices: 438 us -> 0.04 us  [the longest x1 0.02 us: local(): lax.all_gather(jnp.concatenate([w_out, w1, w2, w3], axis=1), 'dp', axis=0...]
    ppermute x0 -> x29, waiting for transfers between devices: none -> 337 us  [shift_by(): lax.ppermute(value, 'tensor', [(i, (i + step) % WAYS) for i in range(WAYS)])]
    pallas_call x0 -> x14, Pallas kernels: none -> 191 us  [the longest x2 31 us: row_grads(): call(grads_kernel, (width // tile,), [pl.BlockSpec((rows, tile), lambda j...]
    dot_general x29 -> x0, matrix products: 176 us -> none  [the longest x5 51.7 us: times_transpose(): lax.dot_general(left, right, (((1,), (1,)), ((), ())), preferred_element_...]
    ppermute x0 -> x29, starting transfers between devices: none -> 33.9 us  [shift_by(): lax.ppermute(value, 'tensor', [(i, (i + step) % WAYS) for i in range(WAYS)])]
    unnamed x2 -> x0, blocking collectives: 25.6 us -> none
    convert_element_type x23 -> x15, other arithmetic: 36.7 us -> 15.7 us  [the longest x6 5.77 us: add(): return (block.astype(f32) + arrived.astype(f32)).astype(bf16)]
  transfers between devices with their start and end apart: 22 -> 36, of which waited for: 19 -> 26; matrix products, arithmetic and copies ran while one was open for 17% -> 7% of each run, Pallas kernels for 0% -> 30%
where the time goes in v1:
time: 638 us; the launch traced here: 635 us
  waiting for transfers between devices  337 us (53%)
  Pallas kernels  191 us (30%)
  starting transfers between devices  34.2 us (5%)
  other arithmetic  34.1 us (5%)
  local copies, waits for them, and re-layouts  23.1 us (4%)
  between operations  15.1 us (2%)
    ppermute x29, waiting for transfers between devices, shift_by(): lax.ppermute(value, 'tensor', [(i, (i + step) % WAYS) for i in range(WAYS)])  337 us
    ppermute x29, starting transfers between devices, shift_by(): lax.ppermute(value, 'tensor', [(i, (i + step) % WAYS) for i in range(WAYS)])  33.9 us
    pallas_call x2, Pallas kernels, row_grads(): call(grads_kernel, (width // tile,), [pl.BlockSpec((rows, tile), lambda j...  31 us
    pallas_call x2, Pallas kernels, back_feed(): call(functools.partial(back_kernel, slots, size, lone), (width // tile,),...  24.6 us
    pallas_call x1, Pallas kernels, feed(): call(feed_kernel, (tiles,), [whole((rows, width)), col(0), col(1)], [((3,...  19.6 us
    pallas_call x1, Pallas kernels, mix(): call(mix_kernel, (WAYS,), [whole(x.shape) for x in x_slots] + [whole(c.sh...  18.9 us
    pallas_call x1, Pallas kernels, attend_back(): call(attend_back_kernel, (2,), [pl.BlockSpec(memory_space=pltpu.SMEM), co...  18 us
    pallas_call x1, Pallas kernels, feed_back(): call(feed_back_kernel, (ff_width // tile,), [whole((rows, width)), pl.Blo...  14 us
  transfers between devices with their start and end apart: 36, of which 26 were waited for; matrix products, arithmetic and copies ran while one was open for 7% of the time, Pallas kernels for 30%

profile of v1, /device:TPU:0, one launch (start us, length us, event | category | flops | bytes accessed | tf_op | source)
XLA Modules:
  0.0 634.6 jit_solution(3161104689061751606)
XLA Ops:
  12.5 3.1 collective-permute-start
  15.6 25.2 %collective-permute-done.below = bf16[256,2048]{1,0:T(8,128)(2,1)S(1)} collective-permute-done((bf16[256,2048]{1,0:T(8,128)(2,1)S(1)}, bf16[256,2048]{1,0:T(8,128)(2,1)S(1)}, u32[]{:S(2)}, u32[]{:S(2)}) %collective-permute-start) | collective-permute-done | bytes 1048608 | tf_op jit(solution)/shard_map/ppermute | solution.py:61
  41.7 26.2 %collective-permute-done.1.far = bf16[256,2048]{1,0:T(8,128)(2,1)} collective-permute-done((bf16[256,2048]{1,0:T(8,128)(2,1)S(1)}, bf16[256,2048]{1,0:T(8,128)(2,1)}, u32[]{:S(2)}, u32[]{:S(2)}) %collective-permute-start.1) | collective-permute-done | bytes 1048608 | tf_op jit(solution)/shard_map/ppermute | solution.py:61
  71.0 22.5 %collective-permute-done.2.above = bf16[256,2048]{1,0:T(8,128)(2,1)} collective-permute-done((bf16[256,2048]{1,0:T(8,128)(2,1)}, bf16[256,2048]{1,0:T(8,128)(2,1)}, u32[]{:S(2)}, u32[]{:S(2)}) %collective-permute-start.2) | collective-permute-done | bytes 1048608 | tf_op jit(solution)/shard_map/ppermute | solution.py:61
  93.5 8.2 %collective-permute-done.7 = bf16[256,512]{1,0:T(8,128)(2,1)S(1)} collective-permute-done((bf16[256,512]{1,0:T(8,128)(2,1)S(1)}, bf16[256,512]{1,0:T(8,128)(2,1)S(1)}, u32[]{:S(2)}, u32[]{:S(2)}) %collective-permute-start.7) | collective-permute-done | bytes 262176 | tf_op jit(solution)/shard_map/ppermute | solution.py:61
  101.7 8.6 %collective-permute-done.8 = bf16[256,512]{1,0:T(8,128)(2,1)S(1)} collective-permute-done((bf16[256,512]{1,0:T(8,128)(2,1)S(1)}, bf16[256,512]{1,0:T(8,128)(2,1)S(1)}, u32[]{:S(2)}, u32[]{:S(2)}) %collective-permute-start.8) | collective-permute-done | bytes 262176 | tf_op jit(solution)/shard_map/ppermute | solution.py:61
  110.3 8.2 %collective-permute-done.9 = bf16[256,512]{1,0:T(8,128)(2,1)S(1)} collective-permute-done((bf16[256,512]{1,0:T(8,128)(2,1)S(1)}, bf16[256,512]{1,0:T(8,128)(2,1)S(1)}, u32[]{:S(2)}, u32[]{:S(2)}) %collective-permute-start.9) | collective-permute-done | bytes 262176 | tf_op jit(solution)/shard_map/ppermute | solution.py:61
  130.5 12.0 %shard_map.246 = (bf16[1024,2048]{1,0:T(8,128)(2,1)}, bf16[1024,1024]{1,0:T(8,128)(2,1)}, f32[1024,768]{1,0:T(8,128)}) custom-call(bf16[256,2048]{1,0:T(8,128)(2,1)} %own.3, bf16[256,2048]{1,0:T(8,128)(2,1)} %copy-done.26, bf16[256,2048]{1,0:T(8,128)(2,1)} %collective-permute-done.1.far, bf16[256,2048]{1,0:T(8,128)(2,1)} %collective-permute-done.2.above, ...), custom_call_target="tpu_custom_call" | custom-call | flops 4294967296 | bytes 20971520 | tf_op jit(solution)/shard_map/pallas_call | solution.py:126
  142.5 10.3 %shard_map.247 = (bf16[1024,512]{1,0:T(8,128)(2,1)}, f32[1024,256]{1,0:T(8,128)}) custom-call(s32[1]{0:T(128)} %bitcast.1.place, bf16[1024,1024]{1,0:T(8,128)(2,1)} %get-tuple-element.80.q.k.v, bf16[1024,1024]{1,0:T(8,128)(2,1)} %get-tuple-element.80.q.k.v, bf16[1024,1024]{1,0:T(8,128)(2,1)} %get-tuple-element.80.q.k.v), custom_call_target="tpu_custom_call" | custom-call | flops 1073741824 | bytes 2097152 | tf_op jit(solution)/shard_map/pallas_call | solution.py:184
  152.8 23.5 %collective-permute-done.4.c1 = bf16[1024,512]{1,0:T(8,128)(2,1)S(1)} collective-permute-done((bf16[1024,512]{1,0:T(8,128)(2,1)}, bf16[1024,512]{1,0:T(8,128)(2,1)S(1)}, u32[]{:S(2)}, u32[]{:S(2)}) %collective-permute-start.4) | collective-permute-done | bytes 1048608 | tf_op jit(solution)/shard_map/ppermute | solution.py:61
  176.3 23.3 %collective-permute-done.5.c2 = bf16[1024,512]{1,0:T(8,128)(2,1)S(1)} collective-permute-done((bf16[1024,512]{1,0:T(8,128)(2,1)S(1)}, bf16[1024,512]{1,0:T(8,128)(2,1)S(1)}, u32[]{:S(2)}, u32[]{:S(2)}) %collective-permute-start.5) | collective-permute-done | bytes 1048608 | tf_op jit(solution)/shard_map/ppermute | solution.py:61
  199.7 22.1 %collective-permute-done.6.c3 = bf16[1024,512]{1,0:T(8,128)(2,1)S(1)} collective-permute-done((bf16[1024,512]{1,0:T(8,128)(2,1)S(1)}, bf16[1024,512]{1,0:T(8,128)(2,1)S(1)}, u32[]{:S(2)}, u32[]{:S(2)}) %collective-permute-start.6) | collective-permute-done | bytes 1048608 | tf_op jit(solution)/shard_map/ppermute | solution.py:61
  223.0 18.9 %shard_map.248 = (bf16[1024,2048]{1,0:T(8,128)(2,1)}, f32[256,2048]{1,0:T(8,128)}, bf16[256,2048]{1,0:T(8,128)(2,1)}) custom-call(bf16[256,2048]{1,0:T(8,128)(2,1)} %own.3, bf16[256,2048]{1,0:T(8,128)(2,1)} %copy-done.26, bf16[256,2048]{1,0:T(8,128)(2,1)} %collective-permute-done.1.far, bf16[256,2048]{1,0:T(8,128)(2,1)} %collective-permute-done.2.above, ...), custom_call_target="tpu_custom_call" | custom-call | flops 8589934592 | bytes 25165824 | tf_op jit(solution)/shard_map/pallas_call | solution.py:238
  241.9 4.4 collective-permute-done.10
  249.5 15.0 %collective-permute-done.11 = bf16[256,2048]{1,0:T(8,128)(2,1)S(1)} collective-permute-done((bf16[256,2048]{1,0:T(8,128)(2,1)S(1)}, bf16[256,2048]{1,0:T(8,128)(2,1)S(1)}, u32[]{:S(2)}, u32[]{:S(2)}) %collective-permute-start.11) | collective-permute-done | bytes 1048608 | tf_op jit(solution)/shard_map/ppermute | solution.py:61
  265.5 19.6 %shard_map.249.a.slopes = bf16[3,1024,1536]{2,1,0:T(8,128)(2,1)} custom-call(bf16[1024,2048]{1,0:T(8,128)(2,1)} %get-tuple-element.91.n, bf16[2048,3072]{1,0:T(8,128)(2,1)} %all-gather.11.cloned.1.call-done.w_gate.w_up.wa.wb, bf16[2048,3072]{1,0:T(8,128)(2,1)} %all-gather.11.cloned.1.call-done.w_gate.w_up.wa.wb), custom_call_target="tpu_custom_call" | custom-call | flops 12884901888 | bytes 27262976 | tf_op jit(solution)/shard_map/pallas_call | solution.py:270
  285.2 12.1 %shard_map.250 = bf16[2048,1536]{1,0:T(8,128)(2,1)} custom-call(bf16[1024,2048]{1,0:T(8,128)(2,1)} %constant_dynamic-update-slice_fusion.n.d, bf16[3,1024,1536]{2,1,0:T(8,128)(2,1)} %shard_map.249.a.slopes), custom_call_target="tpu_custom_call" | custom-call | flops 6442450944 | bytes 13631488 | tf_op jit(solution)/shard_map/pallas_call | solution.py:377
  297.4 14.0 %shard_map.251.a.b = bf16[2,1024,1536]{2,1,0:T(8,128)(2,1)} custom-call(bf16[1024,2048]{1,0:T(8,128)(2,1)} %constant_dynamic-update-slice_fusion.n.d, bf16[2048,1536]{1,0:T(8,128)(2,1)} %all-gather.9.cloned.1.call-done.w_down.wa, bf16[3,1024,1536]{2,1,0:T(8,128)(2,1)} %shard_map.249.a.slopes), custom_call_target="tpu_custom_call" | custom-call | flops 6442450944 | bytes 23068672 | tf_op jit(solution)/shard_map/pallas_call | solution.py:295
  311.4 8.5 %shard_map.253 = bf16[256,2048]{1,0:T(8,128)(2,1)} custom-call(bf16[2,1024,1536]{2,1,0:T(8,128)(2,1)} %shard_map.251.a.b, bf16[2,1024,1536]{2,1,0:T(8,128)(2,1)} %shard_map.251.a.b, bf16[2048,3072]{1,0:T(8,128)(2,1)} %all-gather.11.cloned.1.call-done.w_gate.w_up.wa.wb, bf16[2048,3072]{1,0:T(8,128)(2,1)} %all-gather.11.cloned.1.call-done.w_gate.w_up.wa.wb), custom_call_target="tpu_custom_call" | custom-call | flops 3221225472 | bytes 20971520 | tf_op jit(solution)/shard_map/pallas_call | solution.py:329
  319.9 16.1 %shard_map.252 = (bf16[256,2048]{1,0:T(8,128)(2,1)}, bf16[256,2048]{1,0:T(8,128)(2,1)}, bf16[256,2048]{1,0:T(8,128)(2,1)}) custom-call(bf16[2,1024,1536]{2,1,0:T(8,128)(2,1)} %shard_map.251.a.b, bf16[2,1024,1536]{2,1,0:T(8,128)(2,1)} %shard_map.251.a.b, bf16[2048,3072]{1,0:T(8,128)(2,1)} %all-gather.11.cloned.1.call-done.w_gate.w_up.wa.wb, ...), custom_call_target="tpu_custom_call" | custom-call | flops 9663676416 | bytes 20971520 | tf_op jit(solution)/shard_map/pallas_call | solution.py:329
  336.0 8.2 %collective-permute-done.12 = bf16[256,2048]{1,0:T(8,128)(2,1)S(1)} collective-permute-done((bf16[256,2048]{1,0:T(8,128)(2,1)}, bf16[256,2048]{1,0:T(8,128)(2,1)S(1)}, u32[]{:S(2)}, u32[]{:S(2)}) %collective-permute-start.12) | collective-permute-done | bytes 1048608 | tf_op jit(solution)/shard_map/ppermute | solution.py:61
  345.9 11.6 %collective-permute-start.13 = (bf16[256,2048]{1,0:T(8,128)(2,1)S(1)}, bf16[256,2048]{1,0:T(8,128)(2,1)S(1)}, u32[]{:S(2)}, u32[]{:S(2)}) collective-permute-start(bf16[256,2048]{1,0:T(8,128)(2,1)S(1)} %add_convert_fusion.5), channel_id=1, source_target_pairs={{0,1},{1,2},{2,3},{3,0},{4,5},{5,6},{6,7},{7,4},{8,9},{9,10},{10,1... | collective-permute-start | bytes 3145736 | tf_op jit(solution)/shard_map/ppermute | solution.py:61
  357.5 18.9 %shard_map.254 = bf16[2048,3072]{1,0:T(8,128)(2,1)} custom-call(bf16[1024,2048]{1,0:T(8,128)(2,1)} %get-tuple-element.91.n, bf16[2,1024,1536]{2,1,0:T(8,128)(2,1)} %shard_map.251.a.b), custom_call_target="tpu_custom_call" | custom-call | flops 12884901888 | bytes 23068672 | tf_op jit(solution)/shard_map/pallas_call | solution.py:377
  376.3 4.4 collective-permute-done.13
  382.6 11.0 %shard_map.255 = (bf16[256,2048]{1,0:T(8,128)(2,1)}, bf16[256,2048]{1,0:T(8,128)(2,1)}, bf16[256,2048]{1,0:T(8,128)(2,1)}, bf16[256,2048]{1,0:T(8,128)(2,1)}) custom-call(bf16[3,1024,1536]{2,1,0:T(8,128)(2,1)} %shard_map.249.a.slopes, bf16[2048,1536]{1,0:T(8,128)(2,1)} %all-gather.9.cloned.1.call-done.w_down.wa), custom_call_target="tpu_custom_call" | custom-call | flops 6442450944 | bytes 14680064 | tf_op jit(solution)/shard_map/pallas_call | solution.py:355
  393.6 10.1 %collective-permute-done.14.arrived = bf16[256,2048]{1,0:T(8,128)(2,1)S(1)} collective-permute-done((bf16[256,2048]{1,0:T(8,128)(2,1)S(1)}, bf16[256,2048]{1,0:T(8,128)(2,1)S(1)}, u32[]{:S(2)}, u32[]{:S(2)}) %collective-permute-start.14) | collective-permute-done | bytes 1048608 | tf_op jit(solution)/shard_map/ppermute | solution.py:61
  404.6 10.4 %shard_map.256 = (f32[256,2048]{1,0:T(8,128)}, bf16[256,2048]{1,0:T(8,128)(2,1)}, bf16[256,512]{1,0:T(8,128)(2,1)}, bf16[256,512]{1,0:T(8,128)(2,1)}, bf16[256,5...) custom-call(bf16[256,2048]{1,0:T(8,128)(2,1)} %get-tuple-element.106.own, bf16[256,2048]{1,0:T(8,128)(2,1)} %copy-done.14, ...), custom_call_target="tpu_custom_call" | custom-call | flops 2147483648 | bytes 16777216 | tf_op jit(solution)/shard_map/pallas_call | solution.py:414
  415.2 2.3 collective-permute-start.16
  419.4 6.7 %collective-permute-done.15.d1 = bf16[256,512]{1,0:T(8,128)(2,1)S(1)} collective-permute-done((bf16[256,512]{1,0:T(8,128)(2,1)}, bf16[256,512]{1,0:T(8,128)(2,1)S(1)}, u32[]{:S(2)}, u32[]{:S(2)}) %collective-permute-start.15) | collective-permute-done | bytes 262176 | tf_op jit(solution)/shard_map/ppermute | solution.py:61
  426.0 5.6 collective-permute-done.16.d2
  431.7 6.1 collective-permute-start.18
  437.9 18.0 %shard_map.257 = (bf16[1024,512]{1,0:T(8,128)(2,1)}, bf16[1024,256]{1,0:T(8,128)(2,1)}, bf16[1024,256]{1,0:T(8,128)(2,1)}, f32[8,256]{1,0:T(8,128)}, f32[8,256]{1,0:T(8,128)}) custom-call(s32[1]{0:T(128)} %bitcast.1.place, bf16[1024,1024]{1,0:T(8,128)(2,1)} %get-tuple-element.80.q.k.v, bf16[1024,1024]{1,0:T(8,128)(2,1)} %get-tuple-element.80.q.k.v, ...), custom_call_target="tpu_custom_call" | custom-call | flops 5368709120 | bytes 12582912 | tf_op jit(solution)/shard_map/pallas_call | solution.py:481
  458.2 2.6 collective-permute-done.18
  460.8 7.8 %shard_map.258 = (bf16[256,2048]{1,0:T(8,128)(2,1)}, bf16[256,2048]{1,0:T(8,128)(2,1)}, bf16[256,2048]{1,0:T(8,128)(2,1)}, bf16[256,2048]{1,0:T(8,128)(2,1)}) custom-call(bf16[1024,512]{1,0:T(8,128)(2,1)} %get-tuple-element.127.q, bf16[1024,256]{1,0:T(8,128)(2,1)} %get-tuple-element.121.k, bf16[1024,256]{1,0:T(8,128)(2,1)} %get-tuple-element.122.v, ...), custom_call_target="tpu_custom_call" | custom-call | flops 4294967296 | bytes 10485760 | tf_op jit(solution)/shard_map/pallas_call | solution.py:513
  468.7 2.4 collective-permute-start.19
  472.2 13.6 %shard_map.259 = bf16[2048,3200]{1,0:T(8,128)(2,1)} custom-call(bf16[1024,2048]{1,0:T(8,128)(2,1)} %get-tuple-element.125.n, bf16[1024,512]{1,0:T(8,128)(2,1)} %get-tuple-element.127.q, bf16[1024,256]{1,0:T(8,128)(2,1)} %get-tuple-element.121.k, bf16[1024,256]{1,0:T(8,128)(2,1)} %get-tuple-element.122.v, bf16[256,2048]{1,0:T(8,128)(2,1)} %get-tuple-element.128.d, ...), custom_call_target="tpu_custom_call" | custom-call | flops 6442450944 | bytes 20971520 | tf_op jit(solution)/shard_map/pallas_call | solution.py:539
  485.8 9.2 %collective-permute-done.19 = bf16[256,2048]{1,0:T(8,128)(2,1)S(1)} collective-permute-done((bf16[256,2048]{1,0:T(8,128)(2,1)}, bf16[256,2048]{1,0:T(8,128)(2,1)S(1)}, u32[]{:S(2)}, u32[]{:S(2)}) %collective-permute-start.19) | collective-permute-done | bytes 1048608 | tf_op jit(solution)/shard_map/ppermute | solution.py:61
  496.2 24.6 %collective-permute-done.20 = bf16[256,2048]{1,0:T(8,128)(2,1)S(1)} collective-permute-done((bf16[256,2048]{1,0:T(8,128)(2,1)S(1)}, bf16[256,2048]{1,0:T(8,128)(2,1)S(1)}, u32[]{:S(2)}, u32[]{:S(2)}) %collective-permute-start.20) | collective-permute-done | bytes 1048608 | tf_op jit(solution)/shard_map/ppermute | solution.py:61
  521.2 24.4 %collective-permute-done.21 = bf16[256,2048]{1,0:T(8,128)(2,1)} collective-permute-done((bf16[256,2048]{1,0:T(8,128)(2,1)S(1)}, bf16[256,2048]{1,0:T(8,128)(2,1)}, u32[]{:S(2)}, u32[]{:S(2)}) %collective-permute-start.21) | collective-permute-done | bytes 1048608 | tf_op jit(solution)/shard_map/ppermute | solution.py:61
  549.0 3.6 add_reduce_fusion
  552.7 2.1 fusion
  554.7 16.2 %collective-permute-done.22 = bf16[256,2048]{1,0:T(8,128)(2,1)} collective-permute-done((bf16[256,2048]{1,0:T(8,128)(2,1)}, bf16[256,2048]{1,0:T(8,128)(2,1)}, u32[]{:S(2)}, u32[]{:S(2)}) %collective-permute-start.22) | collective-permute-done | bytes 1048608 | tf_op jit(solution)/shard_map/ppermute | solution.py:61
  572.7 3.1 fusion.4
  575.8 19.6 %collective-permute-done.23 = bf16[256,2048]{1,0:T(8,128)(2,1)S(1)} collective-permute-done((bf16[256,2048]{1,0:T(8,128)(2,1)S(1)}, bf16[256,2048]{1,0:T(8,128)(2,1)S(1)}, u32[]{:S(2)}, u32[]{:S(2)}) %collective-permute-start.23) | collective-permute-done | bytes 1048608 | tf_op jit(solution)/shard_map/ppermute | solution.py:61
  600.5 4.3 collective-permute-done.24
  608.6 2.9 collective-permute-start.27
  614.1 5.1 collective-permute-done.28
  619.2 7.2 %collective-permute-done.27 = bf16[256,512]{1,0:T(8,128)(2,1)S(1)} collective-permute-done((bf16[256,512]{1,0:T(8,128)(2,1)S(1)}, bf16[256,512]{1,0:T(8,128)(2,1)S(1)}, u32[]{:S(2)}, u32[]{:S(2)}) %collective-permute-start.27) | collective-permute-done | bytes 262176 | tf_op jit(solution)/shard_map/ppermute | solution.py:61
  (191 shorter events, 55.8 us)
Async XLA Ops:
  7.2 60.8 %copy-start.22 = (bf16[512,256]{1,0:T(8,128)(2,1)S(1)}, bf16[512,256]{1,0:T(8,128)(2,1)}, u32[]{:S(2)}) copy-start(bf16[512,256]{1,0:T(8,128)(2,1)} %param.22) | copy-start | bytes 786436
  7.2 60.9 %copy-start.33 = (s32[8]{0:T(128)S(1)}, s32[8]{0:T(128)}, u32[]{:S(2)}) copy-start(s32[8]{0:T(128)} %param.29) | copy-start | bytes 100
  7.2 61.6 %copy-start.34 = (s32[8]{0:T(128)S(1)}, s32[8]{0:T(128)}, u32[]{:S(2)}) copy-start(s32[8]{0:T(128)} %param.28) | copy-start | bytes 100
  7.2 63.5 %copy-start.2 = (bf16[256,2048]{1,0:T(8,128)(2,1)S(1)}, bf16[256,2048]{1,0:T(8,128)(2,1)}, u32[]{:S(2)}) copy-start(bf16[256,2048]{1,0:T(8,128)(2,1)} %cotangent.1) | copy-start | bytes 3145732
  7.2 119.1 %all-gather.5.cloned.1.call-start = ((), (), s32[]{:S(2)}) async-start(), calls=%async_computation.3 | async-start | bytes 5308416 | tf_op jit(solution)/shard_map/all_gather | solution.py:604
  12.4 210.6 %all-gather.7.cloned.1.call-start = ((), (), s32[]{:S(2)}) async-start(), calls=%async_computation.4 | async-start | bytes 9437184 | tf_op jit(solution)/shard_map/all_gather | solution.py:615
  12.5 28.3 %collective-permute-start = (bf16[256,2048]{1,0:T(8,128)(2,1)S(1)}, bf16[256,2048]{1,0:T(8,128)(2,1)S(1)}, u32[]{:S(2)}, u32[]{:S(2)}) collective-permute-start(bf16[256,2048]{1,0:T(8,128)(2,1)S(1)} %copy-done.3), channel_id=1, source_target_pairs={{0,1},{1,2},{2,3},{3,0},{4,5},{5,6},{6,7},{7,4},{8,9},{9,10},{10,1... | collective-permute-start | bytes 3145736 | tf_op jit(solution)/shard_map/ppermute | solution.py:61
  41.7 26.2 %collective-permute-start.1 = (bf16[256,2048]{1,0:T(8,128)(2,1)S(1)}, bf16[256,2048]{1,0:T(8,128)(2,1)}, u32[]{:S(2)}, u32[]{:S(2)}) collective-permute-start(bf16[256,2048]{1,0:T(8,128)(2,1)S(1)} %collective-permute-done.below), channel_id=1, source_target_pairs={{0,1},{1,2},{2,3},{3,0},{4,5},{5,6},{6,7},{7,4},{8,9},{9,10},{10,1... | collective-permute-start | bytes 3145736 | tf_op jit(solution)/shard_map/ppermute | solution.py:61
  68.0 25.5 %collective-permute-start.2 = (bf16[256,2048]{1,0:T(8,128)(2,1)}, bf16[256,2048]{1,0:T(8,128)(2,1)}, u32[]{:S(2)}, u32[]{:S(2)}) collective-permute-start(bf16[256,2048]{1,0:T(8,128)(2,1)} %collective-permute-done.1.far), channel_id=1, source_target_pairs={{0,1},{1,2},{2,3},{3,0},{4,5},{5,6},{6,7},{7,4},{8,9},{9,10},{10,1... | collective-permute-start | bytes 3145736 | tf_op jit(solution)/shard_map/ppermute | solution.py:61
  71.0 48.7 %copy-start.6 = (bf16[256,1536]{1,0:T(8,128)(2,1)S(1)}, bf16[256,1536]{1,0:T(8,128)(2,1)}, u32[]{:S(2)}) copy-start(bf16[256,1536]{1,0:T(8,128)(2,1)} %param.25) | copy-start | bytes 2359300
  71.0 48.7 %copy-start.7 = (bf16[256,1536]{1,0:T(8,128)(2,1)S(1)}, bf16[256,1536]{1,0:T(8,128)(2,1)}, u32[]{:S(2)}) copy-start(bf16[256,1536]{1,0:T(8,128)(2,1)} %param.24) | copy-start | bytes 2359300
  93.5 8.2 %collective-permute-start.7 = (bf16[256,512]{1,0:T(8,128)(2,1)S(1)}, bf16[256,512]{1,0:T(8,128)(2,1)S(1)}, u32[]{:S(2)}, u32[]{:S(2)}) collective-permute-start(bf16[256,512]{1,0:T(8,128)(2,1)S(1)} %bitcast.24), channel_id=1, source_target_pairs={{0,1},{1,2},{2,3},{3,0},{4,5},{5,6},{6,7},{7,4},{8,9},{9,10},{10,1... | collective-permute-start | bytes 786440 | tf_op jit(solution)/shard_map/ppermute | solution.py:61
  101.7 8.6 %collective-permute-start.8 = (bf16[256,512]{1,0:T(8,128)(2,1)S(1)}, bf16[256,512]{1,0:T(8,128)(2,1)S(1)}, u32[]{:S(2)}, u32[]{:S(2)}) collective-permute-start(bf16[256,512]{1,0:T(8,128)(2,1)S(1)} %collective-permute-done.7), channel_id=1, source_target_pairs={{0,1},{1,2},{2,3},{3,0},{4,5},{5,6},{6,7},{7,4},{8,9},{9,10},{10,1... | collective-permute-start | bytes 786440 | tf_op jit(solution)/shard_map/ppermute | solution.py:61
  110.3 8.2 %collective-permute-start.9 = (bf16[256,512]{1,0:T(8,128)(2,1)S(1)}, bf16[256,512]{1,0:T(8,128)(2,1)S(1)}, u32[]{:S(2)}, u32[]{:S(2)}) collective-permute-start(bf16[256,512]{1,0:T(8,128)(2,1)S(1)} %collective-permute-done.8), channel_id=1, source_target_pairs={{0,1},{1,2},{2,3},{3,0},{4,5},{5,6},{6,7},{7,4},{8,9},{9,10},{10,1... | collective-permute-start | bytes 786440 | tf_op jit(solution)/shard_map/ppermute | solution.py:61
  119.6 145.9 %all-gather.11.cloned.1.call-start = ((), (), s32[]{:S(2)}) async-start(), calls=%async_computation.6 | async-start | bytes 14155776 | tf_op jit(solution)/shard_map/all_gather | solution.py:612
  121.0 176.4 %all-gather.9.cloned.1.call-start = ((), (), s32[]{:S(2)}) async-start(), calls=%async_computation.5 | async-start | bytes 7077888 | tf_op jit(solution)/shard_map/all_gather | solution.py:618
  122.3 258.9 %reduce-scatter.4.cloned.1.call-start = ((), (), s32[]{:S(2)}) async-start(), calls=%async_computation.7 | async-start | bytes 7077888 | tf_op jit(solution)/shard_map/reduce_scatter | solution.py:638
  126.4 26.4 %collective-permute-start.3 = (bf16[256,2048]{1,0:T(8,128)(2,1)S(1)}, bf16[256,2048]{1,0:T(8,128)(2,1)S(1)}, u32[]{:S(2)}, u32[]{:S(2)}) collective-permute-start(bf16[256,2048]{1,0:T(8,128)(2,1)S(1)} %multiply_convert_fusion.1), channel_id=1, source_target_pairs={{0,1},{1,2},{2,3},{3,0},{4,5},{5,6},{6,7},{7,4},{8,9},{9,10},{10,1... | collective-permute-start | bytes 3145736 | tf_op jit(solution)/shard_map/ppermute | solution.py:61
  152.7 23.6 %collective-permute-start.4 = (bf16[1024,512]{1,0:T(8,128)(2,1)}, bf16[1024,512]{1,0:T(8,128)(2,1)S(1)}, u32[]{:S(2)}, u32[]{:S(2)}) collective-permute-start(bf16[1024,512]{1,0:T(8,128)(2,1)} %get-tuple-element.83.c0), channel_id=1, source_target_pairs={{0,1},{1,2},{2,3},{3,0},{4,5},{5,6},{6,7},{7,4},{8,9},{9,10},{10,1... | collective-permute-start | bytes 3145736 | tf_op jit(solution)/shard_map/ppermute | solution.py:61
  176.3 23.3 %copy-start.27 = (bf16[1024,512]{1,0:T(8,128)(2,1)}, bf16[1024,512]{1,0:T(8,128)(2,1)S(1)}, u32[]{:S(2)}) copy-start(bf16[1024,512]{1,0:T(8,128)(2,1)S(1)} %collective-permute-done.4.c1) | copy-start | bytes 3145732
  176.3 23.3 %collective-permute-start.5 = (bf16[1024,512]{1,0:T(8,128)(2,1)S(1)}, bf16[1024,512]{1,0:T(8,128)(2,1)S(1)}, u32[]{:S(2)}, u32[]{:S(2)}) collective-permute-start(bf16[1024,512]{1,0:T(8,128)(2,1)S(1)} %collective-permute-done.4.c1), channel_id=1, source_target_pairs={{0,1},{1,2},{2,3},{3,0},{4,5},{5,6},{6,7},{7,4},{8,9},{9,10},{10,1... | collective-permute-start | bytes 3145736 | tf_op jit(solution)/shard_map/ppermute | solution.py:61
  199.6 22.1 %collective-permute-start.6 = (bf16[1024,512]{1,0:T(8,128)(2,1)S(1)}, bf16[1024,512]{1,0:T(8,128)(2,1)S(1)}, u32[]{:S(2)}, u32[]{:S(2)}) collective-permute-start(bf16[1024,512]{1,0:T(8,128)(2,1)S(1)} %collective-permute-done.5.c2), channel_id=1, source_target_pairs={{0,1},{1,2},{2,3},{3,0},{4,5},{5,6},{6,7},{7,4},{8,9},{9,10},{10,1... | collective-permute-start | bytes 3145736 | tf_op jit(solution)/shard_map/ppermute | solution.py:61
  222.7 23.6 %collective-permute-start.10 = (bf16[256,2048]{1,0:T(8,128)(2,1)S(1)}, bf16[256,2048]{1,0:T(8,128)(2,1)S(1)}, u32[]{:S(2)}, u32[]{:S(2)}) collective-permute-start(bf16[256,2048]{1,0:T(8,128)(2,1)S(1)} %collective-permute-done.3), channel_id=1, source_target_pairs={{0,1},{1,2},{2,3},{3,0},{4,5},{5,6},{6,7},{7,4},{8,9},{9,10},{10,1... | collective-permute-start | bytes 3145736 | tf_op jit(solution)/shard_map/ppermute | solution.py:61
  246.3 18.2 %collective-permute-start.11 = (bf16[256,2048]{1,0:T(8,128)(2,1)S(1)}, bf16[256,2048]{1,0:T(8,128)(2,1)S(1)}, u32[]{:S(2)}, u32[]{:S(2)}) collective-permute-start(bf16[256,2048]{1,0:T(8,128)(2,1)S(1)} %collective-permute-done.10), channel_id=1, source_target_pairs={{0,1},{1,2},{2,3},{3,0},{4,5},{5,6},{6,7},{7,4},{8,9},{9,10},{10,1... | collective-permute-start | bytes 3145736 | tf_op jit(solution)/shard_map/ppermute | solution.py:61
  297.4 197.7 %reduce-scatter.6.cloned.1.call-start = ((), (), s32[]{:S(2)}) async-start(), calls=%async_computation.8 | async-start | bytes 14155776 | tf_op jit(solution)/shard_map/reduce_scatter | solution.py:651
  319.9 24.3 %collective-permute-start.12 = (bf16[256,2048]{1,0:T(8,128)(2,1)}, bf16[256,2048]{1,0:T(8,128)(2,1)S(1)}, u32[]{:S(2)}, u32[]{:S(2)}) collective-permute-start(bf16[256,2048]{1,0:T(8,128)(2,1)} %shard_map.253), channel_id=1, source_target_pairs={{0,1},{1,2},{2,3},{3,0},{4,5},{5,6},{6,7},{7,4},{8,9},{9,10},{10,1... | collective-permute-start | bytes 3145736 | tf_op jit(solution)/shard_map/ppermute | solution.py:61
  345.9 34.9 %copy-start.15 = (bf16[256,2048]{1,0:T(8,128)(2,1)S(1)}, bf16[256,2048]{1,0:T(8,128)(2,1)}, u32[]{:S(2)}) copy-start(bf16[256,2048]{1,0:T(8,128)(2,1)} %get-tuple-element.93) | copy-start | bytes 3145732
  345.9 34.9 %collective-permute-start.13 = (bf16[256,2048]{1,0:T(8,128)(2,1)S(1)}, bf16[256,2048]{1,0:T(8,128)(2,1)S(1)}, u32[]{:S(2)}, u32[]{:S(2)}) collective-permute-start(bf16[256,2048]{1,0:T(8,128)(2,1)S(1)} %add_convert_fusion.5), channel_id=1, source_target_pairs={{0,1},{1,2},{2,3},{3,0},{4,5},{5,6},{6,7},{7,4},{8,9},{9,10},{10,1... | collective-permute-start | bytes 3145736 | tf_op jit(solution)/shard_map/ppermute | solution.py:61
  381.2 215.7 %reduce-scatter.8.cloned.1.call-start = ((), (), s32[]{:S(2)}) async-start(), calls=%async_computation.9 | async-start | bytes 14745600 | tf_op jit(solution)/shard_map/reduce_scatter | solution.py:680
  381.2 22.4 %collective-permute-start.14 = (bf16[256,2048]{1,0:T(8,128)(2,1)S(1)}, bf16[256,2048]{1,0:T(8,128)(2,1)S(1)}, u32[]{:S(2)}, u32[]{:S(2)}) collective-permute-start(bf16[256,2048]{1,0:T(8,128)(2,1)S(1)} %add_convert_fusion.4), channel_id=1, source_target_pairs={{0,1},{1,2},{2,3},{3,0},{4,5},{5,6},{6,7},{7,4},{8,9},{9,10},{10,1... | collective-permute-start | bytes 3145736 | tf_op jit(solution)/shard_map/ppermute | solution.py:61
  415.0 11.0 %collective-permute-start.15 = (bf16[256,512]{1,0:T(8,128)(2,1)}, bf16[256,512]{1,0:T(8,128)(2,1)S(1)}, u32[]{:S(2)}, u32[]{:S(2)}) collective-permute-start(bf16[256,512]{1,0:T(8,128)(2,1)} %get-tuple-element.109), channel_id=1, source_target_pairs={{0,1},{1,2},{2,3},{3,0},{4,5},{5,6},{6,7},{7,4},{8,9},{9,10},{10,1... | collective-permute-start | bytes 786440 | tf_op jit(solution)/shard_map/ppermute | solution.py:61
  415.2 16.5 %collective-permute-start.16 = (bf16[256,512]{1,0:T(8,128)(2,1)}, bf16[256,512]{1,0:T(8,128)(2,1)S(1)}, u32[]{:S(2)}, u32[]{:S(2)}) collective-permute-start(bf16[256,512]{1,0:T(8,128)(2,1)} %get-tuple-element.110), channel_id=1, source_target_pairs={{0,2},{1,3},{2,0},{3,1},{4,6},{5,7},{6,4},{7,5},{8,10},{9,11},{10,... | collective-permute-start | bytes 786440 | tf_op jit(solution)/shard_map/ppermute | solution.py:61
  417.5 14.2 %collective-permute-start.17 = (bf16[256,512]{1,0:T(8,128)(2,1)}, bf16[256,512]{1,0:T(8,128)(2,1)S(1)}, u32[]{:S(2)}, u32[]{:S(2)}) collective-permute-start(bf16[256,512]{1,0:T(8,128)(2,1)} %get-tuple-element.111), channel_id=1, source_target_pairs={{0,3},{1,0},{2,1},{3,2},{4,7},{5,4},{6,5},{7,6},{8,11},{9,8},{10,9... | collective-permute-start | bytes 786440 | tf_op jit(solution)/shard_map/ppermute | solution.py:61
  431.7 29.1 %collective-permute-start.18 = (bf16[256,2048]{1,0:T(8,128)(2,1)}, bf16[256,2048]{1,0:T(8,128)(2,1)S(1)}, u32[]{:S(2)}, u32[]{:S(2)}) collective-permute-start(bf16[256,2048]{1,0:T(8,128)(2,1)} %get-tuple-element.119), channel_id=1, source_target_pairs={{0,1},{1,2},{2,3},{3,0},{4,5},{5,6},{6,7},{7,4},{8,9},{9,10},{10,1... | collective-permute-start | bytes 3145736 | tf_op jit(solution)/shard_map/ppermute | solution.py:61
  468.7 26.4 %collective-permute-start.19 = (bf16[256,2048]{1,0:T(8,128)(2,1)}, bf16[256,2048]{1,0:T(8,128)(2,1)S(1)}, u32[]{:S(2)}, u32[]{:S(2)}) collective-permute-start(bf16[256,2048]{1,0:T(8,128)(2,1)} %get-tuple-element.135), channel_id=1, source_target_pairs={{0,1},{1,2},{2,3},{3,0},{4,5},{5,6},{6,7},{7,4},{8,9},{9,10},{10,1... | collective-permute-start | bytes 3145736 | tf_op jit(solution)/shard_map/ppermute | solution.py:61
  495.0 25.7 %copy-start.12 = (bf16[256,2048]{1,0:T(8,128)(2,1)S(1)}, bf16[256,2048]{1,0:T(8,128)(2,1)}, u32[]{:S(2)}) copy-start(bf16[256,2048]{1,0:T(8,128)(2,1)} %get-tuple-element.123) | copy-start | bytes 3145732
  495.5 50.2 %copy-start.11 = (bf16[256,2048]{1,0:T(8,128)(2,1)S(1)}, bf16[256,2048]{1,0:T(8,128)(2,1)}, u32[]{:S(2)}) copy-start(bf16[256,2048]{1,0:T(8,128)(2,1)} %get-tuple-element.105) | copy-start | bytes 3145732
  495.5 25.3 %collective-permute-start.20 = (bf16[256,2048]{1,0:T(8,128)(2,1)S(1)}, bf16[256,2048]{1,0:T(8,128)(2,1)S(1)}, u32[]{:S(2)}, u32[]{:S(2)}) collective-permute-start(bf16[256,2048]{1,0:T(8,128)(2,1)S(1)} %add_convert_fusion.3), channel_id=1, source_target_pairs={{0,1},{1,2},{2,3},{3,0},{4,5},{5,6},{6,7},{7,4},{8,9},{9,10},{10,1... | collective-permute-start | bytes 3145736 | tf_op jit(solution)/shard_map/ppermute | solution.py:61
  521.2 26.1 %copy-start.19 = (bf16[256,1536]{1,0:T(8,128)(2,1)S(1)}, bf16[256,1536]{1,0:T(8,128)(2,1)}, u32[]{:S(2)}) copy-start(bf16[256,1536]{1,0:T(8,128)(2,1)} %reduce-scatter.4.cloned.1.call-done) | copy-start | bytes 2359300
  521.2 24.5 %collective-permute-start.21 = (bf16[256,2048]{1,0:T(8,128)(2,1)S(1)}, bf16[256,2048]{1,0:T(8,128)(2,1)}, u32[]{:S(2)}, u32[]{:S(2)}) collective-permute-start(bf16[256,2048]{1,0:T(8,128)(2,1)S(1)} %add_convert_fusion.2), channel_id=1, source_target_pairs={{0,1},{1,2},{2,3},{3,0},{4,5},{5,6},{6,7},{7,4},{8,9},{9,10},{10,1... | collective-permute-start | bytes 3145736 | tf_op jit(solution)/shard_map/ppermute | solution.py:61
  547.0 23.9 %collective-permute-start.22 = (bf16[256,2048]{1,0:T(8,128)(2,1)}, bf16[256,2048]{1,0:T(8,128)(2,1)}, u32[]{:S(2)}, u32[]{:S(2)}) collective-permute-start(bf16[256,2048]{1,0:T(8,128)(2,1)} %add_convert_fusion.1), channel_id=1, source_target_pairs={{0,1},{1,2},{2,3},{3,0},{4,5},{5,6},{6,7},{7,4},{8,9},{9,10},{10,1... | collective-permute-start | bytes 3145736 | tf_op jit(solution)/shard_map/ppermute | solution.py:61
  572.5 22.8 %collective-permute-start.23 = (bf16[256,2048]{1,0:T(8,128)(2,1)S(1)}, bf16[256,2048]{1,0:T(8,128)(2,1)S(1)}, u32[]{:S(2)}, u32[]{:S(2)}) collective-permute-start(bf16[256,2048]{1,0:T(8,128)(2,1)S(1)} %add_convert_fusion), channel_id=1, source_target_pairs={{0,1},{1,2},{2,3},{3,0},{4,5},{5,6},{6,7},{7,4},{8,9},{9,10},{10,1... | collective-permute-start | bytes 3145736 | tf_op jit(solution)/shard_map/ppermute | solution.py:61
  572.6 22.7 %copy-start = (f32[256,2048]{1,0:T(8,128)S(1)}, f32[256,2048]{1,0:T(8,128)}, u32[]{:S(2)}) copy-start(f32[256,2048]{1,0:T(8,128)} %get-tuple-element.87.hidden) | copy-start | bytes 6291460
  599.2 5.5 collective-permute-start.24
  604.8 8.1 %collective-permute-start.25 = (f32[544]{0:T(1024)S(1)}, f32[544]{0:T(1024)S(1)}, u32[]{:S(2)}, u32[]{:S(2)}) collective-permute-start(f32[544]{0:T(1024)S(1)} %fusion.10), channel_id=1, source_target_pairs={{0,2},{1,3},{2,0},{3,1},{4,6},{5,7},{6,4},{7,5},{8,10},{9,11},{10,... | collective-permute-start | bytes 6536 | tf_op jit(solution)/shard_map/ppermute | solution.py:61
  606.5 7.5 %collective-permute-start.26 = (bf16[256,512]{1,0:T(8,128)(2,1)S(1)}, bf16[256,512]{1,0:T(8,128)(2,1)S(1)}, u32[]{:S(2)}, u32[]{:S(2)}) collective-permute-start(bf16[256,512]{1,0:T(8,128)(2,1)S(1)} %get-tuple-element.195), channel_id=1, source_target_pairs={{0,3},{1,0},{2,1},{3,2},{4,7},{5,4},{6,5},{7,6},{8,11},{9,8},{10,9... | collective-permute-start | bytes 786440 | tf_op jit(solution)/shard_map/ppermute | solution.py:61
  607.0 12.2 %collective-permute-start.28 = (bf16[256,512]{1,0:T(8,128)(2,1)S(1)}, bf16[256,512]{1,0:T(8,128)(2,1)S(1)}, u32[]{:S(2)}, u32[]{:S(2)}) collective-permute-start(bf16[256,512]{1,0:T(8,128)(2,1)S(1)} %get-tuple-element.196), channel_id=1, source_target_pairs={{0,1},{1,2},{2,3},{3,0},{4,5},{5,6},{6,7},{7,4},{8,9},{9,10},{10,1... | collective-permute-start | bytes 786440 | tf_op jit(solution)/shard_map/ppermute | solution.py:61
  608.6 17.8 %collective-permute-start.27 = (bf16[256,512]{1,0:T(8,128)(2,1)S(1)}, bf16[256,512]{1,0:T(8,128)(2,1)S(1)}, u32[]{:S(2)}, u32[]{:S(2)}) collective-permute-start(bf16[256,512]{1,0:T(8,128)(2,1)S(1)} %get-tuple-element.197), channel_id=1, source_target_pairs={{0,2},{1,3},{2,0},{3,1},{4,6},{5,7},{6,4},{7,5},{8,10},{9,11},{10,... | collective-permute-start | bytes 786440 | tf_op jit(solution)/shard_map/ppermute | solution.py:61
  (23 other events, 229.5 us)
Sparse Core Ops, SparseCore 0:
  12.6 41.6 all-gather.4
  119.7 52.3 all-gather.6
  174.6 72.1 all-gather.10
  248.5 45.5 all-gather.8
  297.5 61.5 reduce-scatter.3
  381.3 90.4 reduce-scatter.5
  495.2 93.2 reduce-scatter.7

commit v2 on v1

--- a/solution.py
+++ b/solution.py
@@ -201,52 +201,40 @@
     )(place, qkv, qkv, qkv)
 
 
-def mix_kernel(own, below, far, above, c0, c1, c2, c3, w, gain, normed, hidden, ctx_rows, acc, c_s):
-    k = pl.program_id(0)
+def mix_kernel(own, below, far, above, c0, c1, c2, c3, wa, wb, gain, normed, hidden, ctx_rows, x_s, c_s):
+    i = pl.program_id(0)
     size = own.shape[0]
-
-    @pl.when(k == 0)
+    inner = c0.shape[1]
+    pick_slot(i, (own, below, far, above), x_s)
+    for k, ref in enumerate((c0, c1, c2, c3)):
+        start = pl.multiple_of(lax.rem(i + WAYS - k, WAYS) * size, size)
+        c_s[:, k * inner : (k + 1) * inner] = ref[pl.ds(start, size), :]
+    wide = wa.shape[1]
+    h = x_s[...].astype(f32) + nt(c_s[:, :wide], wa[...]) + nt(c_s[:, wide:], wb[...])
+    normed[...] = (h * rms_scale(h) * gain[...]).astype(bf16)
+
+    @pl.when(i == 0)
     def _():
-        for i, ref in enumerate((own, below, far, above)):
-            acc[i * size : (i + 1) * size] = ref[...].astype(f32)
-
-    for kk, ref in enumerate((c0, c1, c2, c3)):
-
-        @pl.when(k == kk)
-        def _():
-            for i in range(WAYS):
-                source = (i - kk) % WAYS
-                c_s[i * size : (i + 1) * size] = ref[source * size : (source + 1) * size]
-
-    ctx_rows[...] = c_s[:size]
-    for i in range(WAYS):
-        rows = slice(i * size, (i + 1) * size)
-        acc[rows] += nt(c_s[rows], w[...])
-
-    @pl.when(k == WAYS - 1)
-    def _():
-        hidden[...] = acc[:size]
-        for i in range(WAYS):
-            rows = slice(i * size, (i + 1) * size)
-            h = acc[rows]
-            normed[rows] = (h * rms_scale(h) * gain[...]).astype(bf16)
-
-
-def mix(x_slots, contexts, w_out_full, gain):
+        hidden[...] = h
+        ctx_rows[...] = c_s[...]
+
+
+def mix(x_slots, contexts, weights, gain):
     size, width = x_slots[0].shape
     rows, inner = contexts[0].shape
+    cols = WAYS * inner
     return call(
         mix_kernel,
         (WAYS,),
         [whole(x.shape) for x in x_slots]
         + [whole(c.shape) for c in contexts]
-        + [pl.BlockSpec((width, inner), lambda k: (0, k)), whole(gain.shape)],
-        [((rows, width), bf16), ((size, width), f32), ((size, WAYS * inner), bf16)],
-        [whole((rows, width)), whole((size, width)), pl.BlockSpec((size, inner), lambda k: (0, k))],
-        [pltpu.VMEM((rows, width), f32), pltpu.VMEM((rows, inner), bf16)],
-        flops=2 * rows * width * WAYS * inner,
+        + [whole((width, cols // 2), (0, 3)), whole((width, cols // 2), (0, 4)), whole(gain.shape)],
+        [((rows, width), bf16), ((size, width), f32), ((size, cols), bf16)],
+        [pl.BlockSpec((size, width), lambda i: (i, 0)), whole((size, width)), whole((size, cols))],
+        [pltpu.VMEM((size, width), bf16), pltpu.VMEM((size, cols), bf16)],
+        flops=2 * rows * width * cols,
         size=24 << 20,
-    )(*x_slots, *contexts, w_out_full, gain)
+    )(*x_slots, *contexts, weights, weights, gain)
 
 
 def feed_kernel(n, w_gate, w_up, out):
@@ -373,7 +361,7 @@
 def row_grads(left, right, first, count):
     rows, width = left.shape
     cols = right.shape[2]
-    tile = 256
+    tile = 512
     return call(
         grads_kernel,
         (width // tile,),
@@ -409,18 +397,18 @@
             ref[...] = value
 
 
-def branch(parts, hidden, cotangent, live, gain, w_out_full, inner):
+def branch(parts, hidden, cotangent, live, gain, rest_full, inner):
     size, width = hidden.shape
     return call(
         branch_kernel,
         (WAYS,),
         [whole((size, width))] * 4
-        + [whole(live.shape), whole(gain.shape), pl.BlockSpec((width, inner), lambda k: (0, k))],
+        + [whole(live.shape), whole(gain.shape), pl.BlockSpec((width, inner), lambda k: (0, 6 + k))],
         [((size, width), f32), ((size, width), bf16)] + [((size, inner), bf16)] * WAYS,
         [whole((size, width))] * 2 + [whole((size, inner))] * WAYS,
         flops=2 * size * width * WAYS * inner,
         size=16 << 20,
-    )(*parts, hidden, cotangent, live, gain, w_out_full)
+    )(*parts, hidden, cotangent, live, gain, rest_full)
 
 
 def head_back(d_head, pre_head, gain, c, s):
@@ -521,36 +509,34 @@
     )(*parts, w)
 
 
-def attend_grads_kernel(n, q, k, v, d, c, gains, out):
+def attend_grads_kernel(n, q, k, v, w, out, gain_part):
     n_tile = n[...]
     at = 0
+    total = jnp.zeros(gain_part.shape, f32)
     for ref in (q, k, v):
-        wide = ref.shape[1]
-        out[:, at : at + wide] = tn(n_tile, ref[...]).astype(bf16)
-        at += wide
-    out[:, at : at + c.shape[1]] = tn(d[...], c[...]).astype(bf16)
-    out[:, at + c.shape[1] :] = gains[...]
-
-
-def attend_grads(normed, parts, d_attended, ctx_rows, gains):
+        cols = slice(at, at + ref.shape[1])
+        product = tn(n_tile, ref[...])
+        out[:, cols] = product.astype(bf16)
+        total += jnp.sum(product * w[:, cols].astype(f32), axis=1, keepdims=True)
+        at += ref.shape[1]
+    gain_part[...] = total
+
+
+def attend_grads(normed, parts, w):
     rows, width = normed.shape
-    tile = 256
-    cols = sum(p.shape[1] for p in parts) + ctx_rows.shape[1] + gains.shape[1]
+    tile = 512
+    cols = sum(p.shape[1] for p in parts)
     return call(
         attend_grads_kernel,
         (width // tile,),
         [pl.BlockSpec((rows, tile), lambda j: (0, j))]
         + [whole(p.shape) for p in parts]
-        + [
-            pl.BlockSpec((d_attended.shape[0], tile), lambda j: (0, j)),
-            whole(ctx_rows.shape),
-            pl.BlockSpec((tile, gains.shape[1]), lambda j: (j, 0)),
-        ],
-        [((width, cols), bf16)],
-        [pl.BlockSpec((tile, cols), lambda j: (j, 0))],
-        flops=2 * rows * width * 1536,
-        size=20 << 20,
-    )(normed, *parts, d_attended, ctx_rows, gains)[0]
+        + [pl.BlockSpec((tile, cols), lambda j: (j, 0))],
+        [((width, cols), bf16), ((width, 128), f32)],
+        [pl.BlockSpec((tile, cols), lambda j: (j, 0)), pl.BlockSpec((tile, 128), lambda j: (j, 0))],
+        flops=2 * rows * width * 1024,
+        size=16 << 20,
+    )(normed, *parts, w)
 
 
 def local(
@@ -581,18 +567,19 @@
     ff_width = w_gate.shape[1]
     place_ref = place.reshape(1).astype(jnp.int32)
 
-    x1 = hop(tokens)
-    x2 = hop(x1)
-    x3 = hop(x2)
+    w_out = w_output.T
+    x1, w1 = together(hop(tokens), hop(w_out))
+    offsets = jnp.arange(size, dtype=jnp.int32)
+    position = jnp.concatenate([((place - j) % WAYS) * size + offsets for j in range(WAYS)])
+    cos, sin = rope_tables(position)
     seq_len = sequence_length(lengths, deal_order, lax.axis_index("dp"))
-    offsets = jnp.arange(size, dtype=jnp.int32)
-    own_live = (place * size + offsets < seq_len).astype(f32)[:, None]
-    x3, d_branch, w_out = together(x3, (cotangent.astype(f32) * own_live).astype(bf16), w_output.T)
+    own_live = (position[:size] < seq_len).astype(f32)[:, None]
+    d_branch = (cotangent.astype(f32) * own_live).astype(bf16)
+    x2, w2, cos, sin, d_branch = together(hop(x1), hop(w1), cos, sin, d_branch)
+    w3 = hop(w2)
+    x3, d_branch = together(hop(x2), d_branch)
     x_slots = [tokens, x1, x2, x3]
     d1 = hop(d_branch)
-    w1 = hop(w_out)
-    w2 = hop(w1)
-    w3 = hop(w2)
 
     column = lambda v: jnp.pad(v, (0, shard_rows - v.shape[0]))[:, None]
     attn_part = jnp.concatenate(
@@ -609,16 +596,12 @@
     gain_q = by_shard[:, :, 2].reshape(1, HEAD_SIZE)
     gain_k = by_shard[:, :, 3].reshape(1, HEAD_SIZE)
 
-    gate_up_full = lax.all_gather(
-        jnp.concatenate([w_gate, w_up], axis=1), "dp", axis=0, tiled=True
-    )
-    w_out_full = lax.all_gather(
-        jnp.concatenate([w_out, w1, w2, w3], axis=1), "dp", axis=0, tiled=True
-    )
-    down_full = lax.all_gather(w_down.T, "dp", axis=0, tiled=True)
-
-    position = jnp.concatenate([((place - j) % WAYS) * size + offsets for j in range(WAYS)])
-    cos, sin = rope_tables(position)
+    rest_full = lax.all_gather(
+        jnp.concatenate([w_gate, w_up, w_out, w1, w2, w3], axis=1), "dp", axis=0, tiled=True
+    )
+    w_down_part, x2 = together(w_down.T, x2)
+    x_slots = [tokens, x1, x2, x3]
+    down_full = lax.all_gather(w_down_part, "dp", axis=0, tiled=True)
 
     normed_attn, qkv, pre = project(x_slots, attn_full, norm_attn_all, gain_q, gain_k, cos, sin)
     context, log_total = attend(place_ref, qkv)
@@ -627,63 +610,87 @@
     c2 = hop(c1)
     c3, d1 = together(hop(c2), d1)
     d2 = hop(d1)
-    normed_ffn, hidden, ctx_rows = mix(x_slots, [context, c1, c2, c3], w_out_full, norm_ffn_all)
+    normed_ffn, hidden, ctx_rows = mix(x_slots, [context, c1, c2, c3], rest_full, norm_ffn_all)
 
     normed_ffn, d2 = together(normed_ffn, d2)
     d3 = hop(d2)
-    forward = feed(normed_ffn, gate_up_full, ff_width)
+    forward = feed(normed_ffn, rest_full, ff_width)
     d_branch_all = jnp.concatenate([d_branch, d1, d2, d3], axis=0)
     grads_down = row_grads(d_branch_all, forward, 2, 1)
     forward, grads_down = together(forward, grads_down)
     grads_down = lax.psum_scatter(grads_down, "dp", scatter_dimension=0, tiled=True)
+    y1, y2, y3, y0 = down(forward, down_full, (1, 2, 3, 0), width, size)
+    y1, forward = together(y1, forward)
+    y_sum = hop(y1)
     d_all = feed_back(d_branch_all, down_full, forward)
-    (b1,) = back_feed(d_all, gate_up_full, (1,), width, size)
+    (b1,) = back_feed(d_all, rest_full, (1,), width, size)
+    b1, y_sum = together(b1, y_sum)
     b_sum = hop(b1)
-    b2, b3, b0 = back_feed(d_all, gate_up_full, (2, 3, 0), width, size)
-    b_sum, d_all = together(add(b2, b_sum), d_all)
+    grads_feed = row_grads(normed_ffn, d_all, 0, 2)
+    d_all, grads_feed = together(d_all, grads_feed)
+    b2, b3, b0 = back_feed(d_all, rest_full, (2, 3, 0), width, size)
+    b_sum, grads_feed, grads_down = together(add(b2, b_sum), grads_feed, grads_down)
+    grads_feed = lax.psum_scatter(grads_feed, "dp", scatter_dimension=0, tiled=True)
     b_sum = hop(b_sum)
-    grads_feed = row_grads(normed_ffn, d_all, 0, 2)
-    b_sum, grads_feed, forward = together(add(b3, b_sum), grads_feed, forward)
-    b_sum = hop(b_sum)
-    y1, y2, y3, y0 = down(forward, down_full, (1, 2, 3, 0), width, size)
-    b_sum, y1, y2, y3, y0 = together(b_sum, y1, y2, y3, y0)
-    grads_feed, grads_down = together(grads_feed, grads_down)
-    grads_feed = lax.psum_scatter(grads_feed, "dp", scatter_dimension=0, tiled=True)
+    b_sum, y_sum = together(hop(add(b3, b_sum)), y_sum)
+    y_sum = hop(add(y2, y_sum))
 
     d_hidden, d_attended, p0, p1, p2, p3 = branch(
-        (b0, b_sum), hidden, cotangent, own_live, norm_ffn_all, w_out_full, q_width
-    )
-    s1, s2, s3, y1 = together(shift_by(p3, 1), shift_by(p2, 2), shift_by(p1, -1), y1)
-    y_sum = hop(y1)
+        (b0, b_sum), hidden, cotangent, own_live, norm_ffn_all, rest_full, q_width
+    )
+    p1, p2, p3, y_sum = together(p1, p2, p3, y_sum)
+    grads_out = row_grads(d_attended, ctx_rows[None], 0, 1)
+    s1, s2, s3, grads_out = together(
+        shift_by(p3, 1), shift_by(p2, 2), shift_by(p1, -1), grads_out
+    )
     d_q, d_k, d_v, sum_q, sum_k = attend_back(
         place_ref, qkv, [p0, s1, s2, s3], log_total, pre, cos, sin, gain_q, gain_k
     )
-    d_q, y_sum = together(d_q, y_sum)
+    d_q, grads_out, grads_feed = together(d_q, grads_out, grads_feed)
+    grads_out = lax.psum_scatter(grads_out, "dp", scatter_dimension=0, tiled=True)
     parts = (d_q, d_k, d_v)
     e1, e2, e3, e0 = back_project(parts, attn_full, width, size)
     e_sum, d_q = together(e1, d_q)
     parts = (d_q, d_k, d_v)
     e_sum = hop(e_sum)
+    grads_attn, norm_part = attend_grads(normed_attn, parts, attn_full)
+    own_ffn = jnp.sum(
+        w_gate.astype(f32) * grads_feed[:, :ff_width].astype(f32)
+        + w_up.astype(f32) * grads_feed[:, ff_width:].astype(f32),
+        axis=1,
+    ) / norm_ffn.astype(f32)
+    small = jnp.concatenate(
+        [
+            norm_part[:, 0] / norm_attn_all[0],
+            own_ffn,
+            sum_q[0, :HEAD_SIZE] + sum_q[0, HEAD_SIZE:],
+            sum_k[0, :HEAD_SIZE] + sum_k[0, HEAD_SIZE:],
+        ]
+    )
+    small = small + shift_by(small, 1) + shift_by(small, 2) + shift_by(small, 3)
+    grad_norm_ffn = small[width : width + shard_rows]
     spread = lambda v: jnp.pad(
         v.reshape(data_ways, gain_rows), ((0, 0), (0, shard_rows - gain_rows))
     ).reshape(-1, 1)
-    gains = jnp.concatenate(
+    grads_attn = jnp.concatenate(
         [
-            spread(sum_q[0, :HEAD_SIZE] + sum_q[0, HEAD_SIZE:]),
-            spread(sum_k[0, :HEAD_SIZE] + sum_k[0, HEAD_SIZE:]),
-            jnp.zeros((width, 126), f32),
+            grads_attn,
+            small[:width, None].astype(bf16),
+            spread(small[width + shard_rows : width + shard_rows + HEAD_SIZE]).astype(bf16),
+            spread(small[width + shard_rows + HEAD_SIZE :]).astype(bf16),
+            jnp.zeros((width, 125), bf16),
         ],
         axis=1,
-    ).astype(bf16)
-    grads_attn = attend_grads(normed_attn, parts, d_attended, ctx_rows, gains)
-    grads_attn, grads_feed, e_sum = together(grads_attn, grads_feed, e_sum)
+    )
+    e_sum = hop(add(e2, e_sum))
+    e_sum = hop(add(e3, e_sum))
+    grads_attn, grads_out, e_sum, y_sum = together(
+        grads_attn, grads_out, e_sum, add(y3, y_sum)
+    )
     grads_attn = lax.psum_scatter(grads_attn, "dp", scatter_dimension=0, tiled=True)
-    e_sum = hop(add(e2, e_sum))
-    e_sum, y_sum = together(hop(add(e3, e_sum)), y_sum)
     d_normed_attn = e0.astype(f32) + e_sum.astype(f32)
 
-    y_sum = hop(add(y2, y_sum))
-    y_sum = hop(add(y3, y_sum))
+    y_sum = hop(y_sum)
     ffn_out = y0.astype(f32) + y_sum.astype(f32)
     block_out = ((hidden + ffn_out) * own_live).astype(bf16)
     own_tokens = tokens.astype(f32)
@@ -696,29 +703,16 @@
     grad_query = grad_qkv[:, :q_width]
     grad_key = grad_qkv[:, q_width : q_width + kv_width]
     grad_value = grad_qkv[:, q_width + kv_width :]
-    g0, g1, g2, g3 = [
-        grads_attn[:, qkv_width + k * q_width : qkv_width + (k + 1) * q_width] for k in range(WAYS)
-    ]
+    grad_norm_attn = grads_attn[:, qkv_width].astype(f32)
+    grad_gain_query = grads_attn[:gain_rows, qkv_width + 1].astype(f32)
+    grad_gain_key = grads_attn[:gain_rows, qkv_width + 2].astype(f32)
+    g0, g1, g2, g3 = [grads_out[:, k * q_width : (k + 1) * q_width] for k in range(WAYS)]
     grad_output = (
         g0.astype(f32)
         + shift_by(g1, -1).astype(f32)
         + shift_by(g2, 2).astype(f32)
         + shift_by(g3, 1).astype(f32)
     ).T
-    gain_sums = grads_attn[:gain_rows, qkv_width + WAYS * q_width :].astype(f32)
-    own_attn = jnp.sum(
-        attn_part[:, :qkv_width].astype(f32) * grad_qkv, axis=1
-    ) / norm_attn.astype(f32)
-    own_ffn = jnp.sum(
-        w_gate.astype(f32) * grad_gate + w_up.astype(f32) * grad_up, axis=1
-    ) / norm_ffn.astype(f32)
-    small = jnp.concatenate([own_attn, own_ffn, gain_sums[:, 0], gain_sums[:, 1]])
-    small = small + shift_by(small, 1)
-    small = small + shift_by(small, 2)
-    grad_norm_attn = small[:shard_rows]
-    grad_norm_ffn = small[shard_rows : 2 * shard_rows]
-    grad_gain_query = small[2 * shard_rows : 2 * shard_rows + gain_rows]
-    grad_gain_key = small[2 * shard_rows + gain_rows :]
     return (
         block_out,
         d_tokens.astype(bf16),

time: 638 us -> 604 us (0.947)
  waiting for transfers between devices: 337 us -> 270 us
  local copies, waits for them, and re-layouts: 23.1 us -> 43.3 us
    ppermute x29 -> x30, waiting for transfers between devices: 337 us -> 264 us  [shift_by(): lax.ppermute(value, 'tensor', [(i, (i + step) % WAYS) for i in range(WAYS)])]
    concatenate x1 -> x2, local copies, waits for them, and re-layouts: 0.08 us -> 9.2 us  [the longest x1 8.46 us: local(): jnp.concatenate([grads_attn, small[:width, None].astype(bf16), spread(sma...]
    unnamed x83 -> x82, local copies, waits for them, and re-layouts: 10.8 us -> 19.4 us
    ppermute x29 -> x30, starting transfers between devices: 33.9 us -> 39.1 us  [shift_by(): lax.ppermute(value, 'tensor', [(i, (i + step) % WAYS) for i in range(WAYS)])]
    pallas_call x2 -> x3, Pallas kernels: 31 us -> 36.1 us  [row_grads(): call(grads_kernel, (width // tile,), [pl.BlockSpec((rows, tile), lambda j...]
  transfers between devices with their start and end apart: 36 -> 37, of which waited for: 26 -> 18; matrix products, arithmetic and copies ran while one was open for 7% -> 11% of each run, Pallas kernels for 30% -> 32%
where the time goes in v2:
time: 604 us; the launch traced here: 597 us
  waiting for transfers between devices  270 us (45%)
  Pallas kernels  193 us (32%)
  local copies, waits for them, and re-layouts  43.3 us (7%)
  starting transfers between devices  39.4 us (7%)
  other arithmetic  36.3 us (6%)
  between operations  14.9 us (2%)
    ppermute x30, waiting for transfers between devices, shift_by(): lax.ppermute(value, 'tensor', [(i, (i + step) % WAYS) for i in range(WAYS)])  264 us
    ppermute x30, starting transfers between devices, shift_by(): lax.ppermute(value, 'tensor', [(i, (i + step) % WAYS) for i in range(WAYS)])  39.1 us
    pallas_call x3, Pallas kernels, row_grads(): call(grads_kernel, (width // tile,), [pl.BlockSpec((rows, tile), lambda j...  36.1 us
    pallas_call x2, Pallas kernels, back_feed(): call(functools.partial(back_kernel, slots, size, lone), (width // tile,),...  23.6 us
    pallas_call x1, Pallas kernels, mix(): call(mix_kernel, (WAYS,), [whole(x.shape) for x in x_slots] + [whole(c.sh...  20.2 us
    pallas_call x1, Pallas kernels, feed(): call(feed_kernel, (tiles,), [whole((rows, width)), col(0), col(1)], [((3,...  19.8 us
    unnamed x82, local copies, waits for them, and re-layouts  19.4 us
    pallas_call x1, Pallas kernels, attend_back(): call(attend_back_kernel, (2,), [pl.BlockSpec(memory_space=pltpu.SMEM), co...  18.2 us
  transfers between devices with their start and end apart: 37, of which 18 were waited for; matrix products, arithmetic and copies ran while one was open for 11% of the time, Pallas kernels for 32%

profile of v2, /device:TPU:0, one launch (start us, length us, event | category | flops | bytes accessed | tf_op | source)
XLA Modules:
  0.0 596.7 jit_solution(17743649381489922717)
XLA Ops:
  12.6 3.1 collective-permute-start.1
  22.1 2.7 collective-permute-done.1
  24.9 21.7 %collective-permute-done.below = bf16[256,2048]{1,0:T(8,128)(2,1)} collective-permute-done((bf16[256,2048]{1,0:T(8,128)(2,1)S(1)}, bf16[256,2048]{1,0:T(8,128)(2,1)}, u32[]{:S(2)}, u32[]{:S(2)}) %collective-permute-start) | collective-permute-done | bytes 1048608 | tf_op jit(solution)/shard_map/ppermute | solution.py:61
  51.8 26.7 %collective-permute-done.3 = bf16[256,512]{1,0:T(8,128)(2,1)S(1)} collective-permute-done((bf16[256,512]{1,0:T(8,128)(2,1)S(1)}, bf16[256,512]{1,0:T(8,128)(2,1)S(1)}, u32[]{:S(2)}, u32[]{:S(2)}) %collective-permute-start.3) | collective-permute-done | bytes 262176 | tf_op jit(solution)/shard_map/ppermute | solution.py:61
  80.9 6.1 %collective-permute-done.9 = bf16[256,512]{1,0:T(8,128)(2,1)S(1)} collective-permute-done((bf16[256,512]{1,0:T(8,128)(2,1)S(1)}, bf16[256,512]{1,0:T(8,128)(2,1)S(1)}, u32[]{:S(2)}, u32[]{:S(2)}) %collective-permute-start.9) | collective-permute-done | bytes 262176 | tf_op jit(solution)/shard_map/ppermute | solution.py:61
  87.8 2.3 copy.48
  90.2 24.3 %collective-permute-done.4.above = bf16[256,2048]{1,0:T(8,128)(2,1)S(1)} collective-permute-done((bf16[256,2048]{1,0:T(8,128)(2,1)S(1)}, bf16[256,2048]{1,0:T(8,128)(2,1)S(1)}, u32[]{:S(2)}, u32[]{:S(2)}) %collective-permute-start.4) | collective-permute-done | bytes 1048608 | tf_op jit(solution)/shard_map/ppermute | solution.py:61
  119.5 12.0 %shard_map.246 = (bf16[1024,2048]{1,0:T(8,128)(2,1)}, bf16[1024,1024]{1,0:T(8,128)(2,1)}, f32[1024,768]{1,0:T(8,128)}) custom-call(bf16[256,2048]{1,0:T(8,128)(2,1)} %own.3, bf16[256,2048]{1,0:T(8,128)(2,1)} %collective-permute-done.below, bf16[256,2048]{1,0:T(8,128)(2,1)} %copy-done.16, bf16[256,2048]{1,0:T(8,128)(2,1)} %copy-done.17, ...), custom_call_target="tpu_custom_call" | custom-call | flops 4294967296 | bytes 20971520 | tf_op jit(solution)/shard_map/pallas_call | solution.py:126
  131.4 10.6 %shard_map.247 = (bf16[1024,512]{1,0:T(8,128)(2,1)}, f32[1024,256]{1,0:T(8,128)}) custom-call(s32[1]{0:T(128)} %bitcast.2.place, bf16[1024,1024]{1,0:T(8,128)(2,1)} %get-tuple-element.100.q.k.v, bf16[1024,1024]{1,0:T(8,128)(2,1)} %get-tuple-element.100.q.k.v, bf16[1024,1024]{1,0:T(8,128)(2,1)} %get-tuple-element.100.q.k.v), custom_call_target="tpu_custom_call" | custom-call | flops 1073741824 | bytes 2097152 | tf_op jit(solution)/shard_map/pallas_call | solution.py:184
  142.1 23.2 %collective-permute-done.6.c1 = bf16[1024,512]{1,0:T(8,128)(2,1)S(1)} collective-permute-done((bf16[1024,512]{1,0:T(8,128)(2,1)}, bf16[1024,512]{1,0:T(8,128)(2,1)S(1)}, u32[]{:S(2)}, u32[]{:S(2)}) %collective-permute-start.6) | collective-permute-done | bytes 1048608 | tf_op jit(solution)/shard_map/ppermute | solution.py:61
  166.3 23.3 %collective-permute-done.7.c2 = bf16[1024,512]{1,0:T(8,128)(2,1)S(1)} collective-permute-done((bf16[1024,512]{1,0:T(8,128)(2,1)S(1)}, bf16[1024,512]{1,0:T(8,128)(2,1)S(1)}, u32[]{:S(2)}, u32[]{:S(2)}) %collective-permute-start.7) | collective-permute-done | bytes 1048608 | tf_op jit(solution)/shard_map/ppermute | solution.py:61
  191.0 20.6 %collective-permute-done.8.c3 = bf16[1024,512]{1,0:T(8,128)(2,1)S(1)} collective-permute-done((bf16[1024,512]{1,0:T(8,128)(2,1)S(1)}, bf16[1024,512]{1,0:T(8,128)(2,1)S(1)}, u32[]{:S(2)}, u32[]{:S(2)}) %collective-permute-start.8) | collective-permute-done | bytes 1048608 | tf_op jit(solution)/shard_map/ppermute | solution.py:61
  212.8 2.3 constant_dynamic-update-slice_fusion.8
  215.1 20.2 %shard_map.248 = (bf16[1024,2048]{1,0:T(8,128)(2,1)}, f32[256,2048]{1,0:T(8,128)}, bf16[256,2048]{1,0:T(8,128)(2,1)}) custom-call(bf16[256,2048]{1,0:T(8,128)(2,1)} %own.3, bf16[256,2048]{1,0:T(8,128)(2,1)} %collective-permute-done.below, bf16[256,2048]{1,0:T(8,128)(2,1)} %copy-done.16, bf16[256,2048]{1,0:T(8,128)(2,1)} %copy-done.17, ...), custom_call_target="tpu_custom_call" | custom-call | flops 8589934592 | bytes 25165824 | tf_op jit(solution)/shard_map/pallas_call | solution.py:226
  237.6 19.8 %shard_map.249.a.slopes = bf16[3,1024,1536]{2,1,0:T(8,128)(2,1)} custom-call(bf16[1024,2048]{1,0:T(8,128)(2,1)} %get-tuple-element.110.n, bf16[2048,5120]{1,0:T(8,128)(2,1)} %all-gather.6.cloned.1.call-done.wa.wb.w_gate.w_up.w, bf16[2048,5120]{1,0:T(8,128)(2,1)} %all-gather.6.cloned.1.call-done.wa.wb.w_gate.w_up.w), custom_call_target="tpu_custom_call" | custom-call | flops 12884901888 | bytes 27262976 | tf_op jit(solution)/shard_map/pallas_call | solution.py:258
  258.4 10.7 %shard_map.250 = bf16[2048,1536]{1,0:T(8,128)(2,1)} custom-call(bf16[1024,2048]{1,0:T(8,128)(2,1)} %constant_dynamic-update-slice_fusion.6.n.d, bf16[3,1024,1536]{2,1,0:T(8,128)(2,1)} %shard_map.249.a.slopes), custom_call_target="tpu_custom_call" | custom-call | flops 6442450944 | bytes 13631488 | tf_op jit(solution)/shard_map/pallas_call | solution.py:365
  269.2 10.5 %shard_map.251 = (bf16[256,2048]{1,0:T(8,128)(2,1)}, bf16[256,2048]{1,0:T(8,128)(2,1)}, bf16[256,2048]{1,0:T(8,128)(2,1)}, bf16[256,2048]{1,0:T(8,128)(2,1)}) custom-call(bf16[3,1024,1536]{2,1,0:T(8,128)(2,1)} %shard_map.249.a.slopes, bf16[2048,1536]{1,0:T(8,128)(2,1)} %all-gather.8.cloned.1.call-done.wa.w_down), custom_call_target="tpu_custom_call" | custom-call | flops 6442450944 | bytes 14680064 | tf_op jit(solution)/shard_map/pallas_call | solution.py:343
  279.8 2.8 collective-permute-start.12
  282.6 13.9 %shard_map.252.a.b = bf16[2,1024,1536]{2,1,0:T(8,128)(2,1)} custom-call(bf16[1024,2048]{1,0:T(8,128)(2,1)} %constant_dynamic-update-slice_fusion.6.n.d, bf16[2048,1536]{1,0:T(8,128)(2,1)} %all-gather.8.cloned.1.call-done.wa.w_down, bf16[3,1024,1536]{2,1,0:T(8,128)(2,1)} %shard_map.249.a.slopes), custom_call_target="tpu_custom_call" | custom-call | flops 6442450944 | bytes 23068672 | tf_op jit(solution)/shard_map/pallas_call | solution.py:283
  296.5 8.4 %shard_map.255 = bf16[256,2048]{1,0:T(8,128)(2,1)} custom-call(bf16[2,1024,1536]{2,1,0:T(8,128)(2,1)} %shard_map.252.a.b, bf16[2,1024,1536]{2,1,0:T(8,128)(2,1)} %shard_map.252.a.b, bf16[2048,5120]{1,0:T(8,128)(2,1)} %all-gather.6.cloned.1.call-done.wa.wb.w_gate.w_up.w, bf16[2048,5120]{1,0:T(8,128)(2,1)} %all-gather.6.cloned.1.call-done.wa.wb.w_gate.w_up.w), custom_call_target="tpu_custom_call" | custom-call | flops 3221225472 | bytes 20971520 | tf_op jit(solution)/shard_map/pallas_call | solution.py:317
  306.6 18.7 %shard_map.253 = bf16[2048,3072]{1,0:T(8,128)(2,1)} custom-call(bf16[1024,2048]{1,0:T(8,128)(2,1)} %get-tuple-element.110.n, bf16[2,1024,1536]{2,1,0:T(8,128)(2,1)} %shard_map.252.a.b), custom_call_target="tpu_custom_call" | custom-call | flops 12884901888 | bytes 23068672 | tf_op jit(solution)/shard_map/pallas_call | solution.py:365
  325.3 15.2 %shard_map.254 = (bf16[256,2048]{1,0:T(8,128)(2,1)}, bf16[256,2048]{1,0:T(8,128)(2,1)}, bf16[256,2048]{1,0:T(8,128)(2,1)}) custom-call(bf16[2,1024,1536]{2,1,0:T(8,128)(2,1)} %shard_map.252.a.b, bf16[2,1024,1536]{2,1,0:T(8,128)(2,1)} %shard_map.252.a.b, bf16[2048,5120]{1,0:T(8,128)(2,1)} %all-gather.6.cloned.1.call-done.wa.wb.w_gate.w_up.w, ...), custom_call_target="tpu_custom_call" | custom-call | flops 9663676416 | bytes 20971520 | tf_op jit(solution)/shard_map/pallas_call | solution.py:317
  340.6 2.6 add_convert_fusion.5
  343.3 21.7 %collective-permute-done.14 = bf16[256,2048]{1,0:T(8,128)(2,1)S(1)} collective-permute-done((bf16[256,2048]{1,0:T(8,128)(2,1)}, bf16[256,2048]{1,0:T(8,128)(2,1)S(1)}, u32[]{:S(2)}, u32[]{:S(2)}) %collective-permute-start.14) | collective-permute-done | bytes 1048608 | tf_op jit(solution)/shard_map/ppermute | solution.py:61
  366.6 22.9 %collective-permute-done.15.arrived = bf16[256,2048]{1,0:T(8,128)(2,1)S(1)} collective-permute-done((bf16[256,2048]{1,0:T(8,128)(2,1)S(1)}, bf16[256,2048]{1,0:T(8,128)(2,1)S(1)}, u32[]{:S(2)}, u32[]{:S(2)}) %collective-permute-start.15) | collective-permute-done | bytes 1048608 | tf_op jit(solution)/shard_map/ppermute | solution.py:61
  391.3 10.4 %shard_map.256 = (f32[256,2048]{1,0:T(8,128)}, bf16[256,2048]{1,0:T(8,128)(2,1)}, bf16[256,512]{1,0:T(8,128)(2,1)}, bf16[256,512]{1,0:T(8,128)(2,1)}, bf16[256,5...) custom-call(bf16[256,2048]{1,0:T(8,128)(2,1)} %get-tuple-element.119.own, bf16[256,2048]{1,0:T(8,128)(2,1)} %copy-done.15, ...), custom_call_target="tpu_custom_call" | custom-call | flops 2147483648 | bytes 16777216 | tf_op jit(solution)/shard_map/pallas_call | solution.py:402
  401.7 11.4 %collective-permute-done.16 = bf16[256,2048]{1,0:T(8,128)(2,1)S(1)} collective-permute-done((bf16[256,2048]{1,0:T(8,128)(2,1)S(1)}, bf16[256,2048]{1,0:T(8,128)(2,1)S(1)}, u32[]{:S(2)}, u32[]{:S(2)}) %collective-permute-start.16) | collective-permute-done | bytes 1048608 | tf_op jit(solution)/shard_map/ppermute | solution.py:61
  416.6 3.1 collective-permute-start.19
  419.6 6.6 %shard_map.257 = bf16[2048,2048]{1,0:T(8,128)(2,1)} custom-call(bf16[256,2048]{1,0:T(8,128)(2,1)} %get-tuple-element.138.n, bf16[1,256,2048]{2,1,0:T(8,128)(2,1)} %bitcast.30), custom_call_target="tpu_custom_call" | custom-call | flops 2147483648 | bytes 13631488 | tf_op jit(solution)/shard_map/pallas_call | solution.py:365
  427.9 18.2 %shard_map.258 = (bf16[1024,512]{1,0:T(8,128)(2,1)}, bf16[1024,256]{1,0:T(8,128)(2,1)}, bf16[1024,256]{1,0:T(8,128)(2,1)}, f32[8,256]{1,0:T(8,128)}, f32[8,256]{1,0:T(8,128)}) custom-call(s32[1]{0:T(128)} %bitcast.2.place, bf16[1024,1024]{1,0:T(8,128)(2,1)} %get-tuple-element.100.q.k.v, bf16[1024,1024]{1,0:T(8,128)(2,1)} %get-tuple-element.100.q.k.v, ...), custom_call_target="tpu_custom_call" | custom-call | flops 5368709120 | bytes 12582912 | tf_op jit(solution)/shard_map/pallas_call | solution.py:469
  446.2 7.8 %shard_map.259 = (bf16[256,2048]{1,0:T(8,128)(2,1)}, bf16[256,2048]{1,0:T(8,128)(2,1)}, bf16[256,2048]{1,0:T(8,128)(2,1)}, bf16[256,2048]{1,0:T(8,128)(2,1)}) custom-call(bf16[1024,512]{1,0:T(8,128)(2,1)} %get-tuple-element.152.q, bf16[1024,256]{1,0:T(8,128)(2,1)} %get-tuple-element.149.k, bf16[1024,256]{1,0:T(8,128)(2,1)} %get-tuple-element.150.v, ...), custom_call_target="tpu_custom_call" | custom-call | flops 4294967296 | bytes 10485760 | tf_op jit(solution)/shard_map/pallas_call | solution.py:501
  454.1 3.4 collective-permute-start.23
  458.9 20.9 %collective-permute-done.23 = bf16[256,2048]{1,0:T(8,128)(2,1)S(1)} collective-permute-done((bf16[256,2048]{1,0:T(8,128)(2,1)}, bf16[256,2048]{1,0:T(8,128)(2,1)S(1)}, u32[]{:S(2)}, u32[]{:S(2)}) %collective-permute-start.23) | collective-permute-done | bytes 1048608 | tf_op jit(solution)/shard_map/ppermute | solution.py:61
  479.8 2.6 add_convert_fusion.2
  482.4 9.6 %shard_map.260 = (bf16[2048,1024]{1,0:T(8,128)(2,1)}, f32[2048,128]{1,0:T(8,128)}) custom-call(bf16[1024,2048]{1,0:T(8,128)(2,1)} %get-tuple-element.115.n, bf16[1024,512]{1,0:T(8,128)(2,1)} %get-tuple-element.152.q, bf16[1024,256]{1,0:T(8,128)(2,1)} %get-tuple-element.149.k, bf16[1024,256]{1,0:T(8,128)(2,1)} %get-tuple-element.150.v, ...), custom_call_target="tpu_custom_call" | custom-call | flops 4294967296 | bytes 16777216 | tf_op jit(solution)/shard_map/pallas_call | solution.py:529
  493.6 2.5 fusion.11
  496.1 5.0 collective-permute-start.21
  503.3 5.3 collective-permute-done.24
  508.6 2.6 add_convert_fusion.1
  514.2 8.5 %concatenate.35 = bf16[2048,1152]{1,0:T(8,128)(2,1)} concatenate(bf16[2048,1024]{1,0:T(8,128)(2,1)} %get-tuple-element.153, bf16[2048,1]{1,0:T(8,128)(2,1)S(1)} %convert_element_type.244, bf16[2048,1]{1,0:T(8,128)(2,1)S(1)} %bitcast.29, bf16[2048,1]{1,0:T(8,128)(2,1)S(1)} %bitcast.28, bf16[2048,125]{1,0:T(8,128)(2,1)S(1)} %broadcast_in_dim.39), dimensions={1} | concatenate | bytes 9437184 | tf_op jit(solution)/shard_map/concatenate | solution.py:675
  522.7 6.5 %collective-permute-done.25 = bf16[256,2048]{1,0:T(8,128)(2,1)S(1)} collective-permute-done((bf16[256,2048]{1,0:T(8,128)(2,1)}, bf16[256,2048]{1,0:T(8,128)(2,1)S(1)}, u32[]{:S(2)}, u32[]{:S(2)}) %collective-permute-start.25) | collective-permute-done | bytes 1048608 | tf_op jit(solution)/shard_map/ppermute | solution.py:61
  533.9 4.9 collective-permute-start.27
  539.4 3.8 collective-permute-start.26
  543.2 2.0 fusion
  547.0 7.5 %collective-permute-done.27 = bf16[256,512]{1,0:T(8,128)(2,1)S(1)} collective-permute-done((bf16[256,512]{1,0:T(8,128)(2,1)S(1)}, bf16[256,512]{1,0:T(8,128)(2,1)S(1)}, u32[]{:S(2)}, u32[]{:S(2)}) %collective-permute-start.27) | collective-permute-done | bytes 262176 | tf_op jit(solution)/shard_map/ppermute | solution.py:61
  554.5 18.5 %collective-permute-done.28 = bf16[256,512]{1,0:T(8,128)(2,1)S(1)} collective-permute-done((bf16[256,512]{1,0:T(8,128)(2,1)S(1)}, bf16[256,512]{1,0:T(8,128)(2,1)S(1)}, u32[]{:S(2)}, u32[]{:S(2)}) %collective-permute-start.28) | collective-permute-done | bytes 262176 | tf_op jit(solution)/shard_map/ppermute | solution.py:61
  575.1 3.0 multiply_convert_fusion
  578.1 5.8 reduce-scatter.11.cloned.1.call-done
  (192 shorter events, 65.6 us)
Async XLA Ops:
  7.2 12.0 %copy-start.8 = (bf16[256,1536]{1,0:T(8,128)(2,1)S(1)}, bf16[256,1536]{1,0:T(8,128)(2,1)}, u32[]{:S(2)}) copy-start(bf16[256,1536]{1,0:T(8,128)(2,1)} %param.24) | copy-start | bytes 2359300
  7.2 108.2 %all-gather.4.cloned.1.call-start = ((), (), s32[]{:S(2)}) async-start(), calls=%async_computation.4 | async-start | bytes 5308416 | tf_op jit(solution)/shard_map/all_gather | solution.py:591
  12.4 202.7 %all-gather.6.cloned.1.call-start = ((), (), s32[]{:S(2)}) async-start(), calls=%async_computation.5 | async-start | bytes 23592960 | tf_op jit(solution)/shard_map/all_gather | solution.py:599
  12.6 12.2 %collective-permute-start.1 = (bf16[256,512]{1,0:T(8,128)(2,1)S(1)}, bf16[256,512]{1,0:T(8,128)(2,1)S(1)}, u32[]{:S(2)}, u32[]{:S(2)}) collective-permute-start(bf16[256,512]{1,0:T(8,128)(2,1)S(1)} %bitcast.31), channel_id=1, source_target_pairs={{0,1},{1,2},{2,3},{3,0},{4,5},{5,6},{6,7},{7,4},{8,9},{9,10},{10,1... | collective-permute-start | bytes 786440 | tf_op jit(solution)/shard_map/ppermute | solution.py:61
  15.7 30.9 %collective-permute-start = (bf16[256,2048]{1,0:T(8,128)(2,1)S(1)}, bf16[256,2048]{1,0:T(8,128)(2,1)}, u32[]{:S(2)}, u32[]{:S(2)}) collective-permute-start(bf16[256,2048]{1,0:T(8,128)(2,1)S(1)} %copy-done.1), channel_id=1, source_target_pairs={{0,1},{1,2},{2,3},{3,0},{4,5},{5,6},{6,7},{7,4},{8,9},{9,10},{10,1... | collective-permute-start | bytes 3145736 | tf_op jit(solution)/shard_map/ppermute | solution.py:61
  19.2 29.0 %copy-start.4 = (bf16[256,2048]{1,0:T(8,128)(2,1)S(1)}, bf16[256,2048]{1,0:T(8,128)(2,1)}, u32[]{:S(2)}) copy-start(bf16[256,2048]{1,0:T(8,128)(2,1)} %cotangent.1) | copy-start | bytes 3145732
  46.6 32.0 %collective-permute-start.2 = (bf16[256,2048]{1,0:T(8,128)(2,1)}, bf16[256,2048]{1,0:T(8,128)(2,1)S(1)}, u32[]{:S(2)}, u32[]{:S(2)}) collective-permute-start(bf16[256,2048]{1,0:T(8,128)(2,1)} %collective-permute-done.below), channel_id=1, source_target_pairs={{0,1},{1,2},{2,3},{3,0},{4,5},{5,6},{6,7},{7,4},{8,9},{9,10},{10,1... | collective-permute-start | bytes 3145736 | tf_op jit(solution)/shard_map/ppermute | solution.py:61
  48.5 30.1 %collective-permute-start.3 = (bf16[256,512]{1,0:T(8,128)(2,1)S(1)}, bf16[256,512]{1,0:T(8,128)(2,1)S(1)}, u32[]{:S(2)}, u32[]{:S(2)}) collective-permute-start(bf16[256,512]{1,0:T(8,128)(2,1)S(1)} %collective-permute-done.1), channel_id=1, source_target_pairs={{0,1},{1,2},{2,3},{3,0},{4,5},{5,6},{6,7},{7,4},{8,9},{9,10},{10,1... | collective-permute-start | bytes 786440 | tf_op jit(solution)/shard_map/ppermute | solution.py:61
  78.6 11.6 %copy-start.16 = (bf16[256,2048]{1,0:T(8,128)(2,1)}, bf16[256,2048]{1,0:T(8,128)(2,1)S(1)}, u32[]{:S(2)}) copy-start(bf16[256,2048]{1,0:T(8,128)(2,1)S(1)} %collective-permute-done.2.far) | copy-start | bytes 3145732
  78.6 8.4 %collective-permute-start.9 = (bf16[256,512]{1,0:T(8,128)(2,1)S(1)}, bf16[256,512]{1,0:T(8,128)(2,1)S(1)}, u32[]{:S(2)}, u32[]{:S(2)}) collective-permute-start(bf16[256,512]{1,0:T(8,128)(2,1)S(1)} %collective-permute-done.3), channel_id=1, source_target_pairs={{0,1},{1,2},{2,3},{3,0},{4,5},{5,6},{6,7},{7,4},{8,9},{9,10},{10,1... | collective-permute-start | bytes 786440 | tf_op jit(solution)/shard_map/ppermute | solution.py:61
  87.7 181.5 %all-gather.8.cloned.1.call-start = ((), (), s32[]{:S(2)}) async-start(), calls=%async_computation.6 | async-start | bytes 7077888 | tf_op jit(solution)/shard_map/all_gather | solution.py:604
  90.1 253.1 %reduce-scatter.5.cloned.1.call-start = ((), (), s32[]{:S(2)}) async-start(), calls=%async_computation.7 | async-start | bytes 7077888 | tf_op jit(solution)/shard_map/reduce_scatter | solution.py:621
  90.1 24.4 %collective-permute-start.4 = (bf16[256,2048]{1,0:T(8,128)(2,1)S(1)}, bf16[256,2048]{1,0:T(8,128)(2,1)S(1)}, u32[]{:S(2)}, u32[]{:S(2)}) collective-permute-start(bf16[256,2048]{1,0:T(8,128)(2,1)S(1)} %collective-permute-done.2.far), channel_id=1, source_target_pairs={{0,1},{1,2},{2,3},{3,0},{4,5},{5,6},{6,7},{7,4},{8,9},{9,10},{10,1... | collective-permute-start | bytes 3145736 | tf_op jit(solution)/shard_map/ppermute | solution.py:61
  115.5 26.6 %collective-permute-start.5 = (bf16[256,2048]{1,0:T(8,128)(2,1)S(1)}, bf16[256,2048]{1,0:T(8,128)(2,1)}, u32[]{:S(2)}, u32[]{:S(2)}) collective-permute-start(bf16[256,2048]{1,0:T(8,128)(2,1)S(1)} %multiply_convert_fusion.1), channel_id=1, source_target_pairs={{0,1},{1,2},{2,3},{3,0},{4,5},{5,6},{6,7},{7,4},{8,9},{9,10},{10,1... | collective-permute-start | bytes 3145736 | tf_op jit(solution)/shard_map/ppermute | solution.py:61
  142.0 23.3 %collective-permute-start.6 = (bf16[1024,512]{1,0:T(8,128)(2,1)}, bf16[1024,512]{1,0:T(8,128)(2,1)S(1)}, u32[]{:S(2)}, u32[]{:S(2)}) collective-permute-start(bf16[1024,512]{1,0:T(8,128)(2,1)} %get-tuple-element.103.c0), channel_id=1, source_target_pairs={{0,1},{1,2},{2,3},{3,0},{4,5},{5,6},{6,7},{7,4},{8,9},{9,10},{10,1... | collective-permute-start | bytes 3145736 | tf_op jit(solution)/shard_map/ppermute | solution.py:61
  166.3 23.3 %collective-permute-start.7 = (bf16[1024,512]{1,0:T(8,128)(2,1)S(1)}, bf16[1024,512]{1,0:T(8,128)(2,1)S(1)}, u32[]{:S(2)}, u32[]{:S(2)}) collective-permute-start(bf16[1024,512]{1,0:T(8,128)(2,1)S(1)} %collective-permute-done.6.c1), channel_id=1, source_target_pairs={{0,1},{1,2},{2,3},{3,0},{4,5},{5,6},{6,7},{7,4},{8,9},{9,10},{10,1... | collective-permute-start | bytes 3145736 | tf_op jit(solution)/shard_map/ppermute | solution.py:61
  189.6 22.0 %collective-permute-start.8 = (bf16[1024,512]{1,0:T(8,128)(2,1)S(1)}, bf16[1024,512]{1,0:T(8,128)(2,1)S(1)}, u32[]{:S(2)}, u32[]{:S(2)}) collective-permute-start(bf16[1024,512]{1,0:T(8,128)(2,1)S(1)} %collective-permute-done.7.c2), channel_id=1, source_target_pairs={{0,1},{1,2},{2,3},{3,0},{4,5},{5,6},{6,7},{7,4},{8,9},{9,10},{10,1... | collective-permute-start | bytes 3145736 | tf_op jit(solution)/shard_map/ppermute | solution.py:61
  212.6 22.7 %collective-permute-start.10 = (bf16[256,2048]{1,0:T(8,128)(2,1)}, bf16[256,2048]{1,0:T(8,128)(2,1)S(1)}, u32[]{:S(2)}, u32[]{:S(2)}) collective-permute-start(bf16[256,2048]{1,0:T(8,128)(2,1)} %collective-permute-done.5), channel_id=1, source_target_pairs={{0,1},{1,2},{2,3},{3,0},{4,5},{5,6},{6,7},{7,4},{8,9},{9,10},{10,1... | collective-permute-start | bytes 3145736 | tf_op jit(solution)/shard_map/ppermute | solution.py:61
  235.3 22.1 %collective-permute-start.11 = (bf16[256,2048]{1,0:T(8,128)(2,1)S(1)}, bf16[256,2048]{1,0:T(8,128)(2,1)S(1)}, u32[]{:S(2)}, u32[]{:S(2)}) collective-permute-start(bf16[256,2048]{1,0:T(8,128)(2,1)S(1)} %collective-permute-done.10), channel_id=1, source_target_pairs={{0,1},{1,2},{2,3},{3,0},{4,5},{5,6},{6,7},{7,4},{8,9},{9,10},{10,1... | collective-permute-start | bytes 3145736 | tf_op jit(solution)/shard_map/ppermute | solution.py:61
  269.2 177.0 %reduce-scatter.7.cloned.1.call-start = ((), (), s32[]{:S(2)}) async-start(), calls=%async_computation.8 | async-start | bytes 14155776 | tf_op jit(solution)/shard_map/reduce_scatter | solution.py:633
  279.8 25.1 %collective-permute-start.12 = (bf16[256,2048]{1,0:T(8,128)(2,1)}, bf16[256,2048]{1,0:T(8,128)(2,1)S(1)}, u32[]{:S(2)}, u32[]{:S(2)}) collective-permute-start(bf16[256,2048]{1,0:T(8,128)(2,1)} %get-tuple-element.122), channel_id=1, source_target_pairs={{0,1},{1,2},{2,3},{3,0},{4,5},{5,6},{6,7},{7,4},{8,9},{9,10},{10,1... | collective-permute-start | bytes 3145736 | tf_op jit(solution)/shard_map/ppermute | solution.py:61
  304.9 35.7 %collective-permute-start.13 = (bf16[256,2048]{1,0:T(8,128)(2,1)}, bf16[256,2048]{1,0:T(8,128)(2,1)S(1)}, u32[]{:S(2)}, u32[]{:S(2)}) collective-permute-start(bf16[256,2048]{1,0:T(8,128)(2,1)} %shard_map.255), channel_id=1, source_target_pairs={{0,1},{1,2},{2,3},{3,0},{4,5},{5,6},{6,7},{7,4},{8,9},{9,10},{10,1... | collective-permute-start | bytes 3145736 | tf_op jit(solution)/shard_map/ppermute | solution.py:61
  343.2 46.3 %copy-start.13 = (bf16[256,2048]{1,0:T(8,128)(2,1)S(1)}, bf16[256,2048]{1,0:T(8,128)(2,1)}, u32[]{:S(2)}) copy-start(bf16[256,2048]{1,0:T(8,128)(2,1)} %get-tuple-element.133) | copy-start | bytes 3145732
  343.2 186.0 %reduce-scatter.9.cloned.1.call-start = ((), (), s32[]{:S(2)}) async-start(), calls=%async_computation.9 | async-start | bytes 9437184 | tf_op jit(solution)/shard_map/reduce_scatter | solution.py:650
  343.2 21.7 %collective-permute-start.14 = (bf16[256,2048]{1,0:T(8,128)(2,1)}, bf16[256,2048]{1,0:T(8,128)(2,1)S(1)}, u32[]{:S(2)}, u32[]{:S(2)}) collective-permute-start(bf16[256,2048]{1,0:T(8,128)(2,1)} %add_convert_fusion.5), channel_id=1, source_target_pairs={{0,1},{1,2},{2,3},{3,0},{4,5},{5,6},{6,7},{7,4},{8,9},{9,10},{10,1... | collective-permute-start | bytes 3145736 | tf_op jit(solution)/shard_map/ppermute | solution.py:61
  366.6 22.9 %collective-permute-start.15 = (bf16[256,2048]{1,0:T(8,128)(2,1)S(1)}, bf16[256,2048]{1,0:T(8,128)(2,1)S(1)}, u32[]{:S(2)}, u32[]{:S(2)}) collective-permute-start(bf16[256,2048]{1,0:T(8,128)(2,1)S(1)} %add_convert_fusion.4), channel_id=1, source_target_pairs={{0,1},{1,2},{2,3},{3,0},{4,5},{5,6},{6,7},{7,4},{8,9},{9,10},{10,1... | collective-permute-start | bytes 3145736 | tf_op jit(solution)/shard_map/ppermute | solution.py:61
  389.9 23.3 %collective-permute-start.16 = (bf16[256,2048]{1,0:T(8,128)(2,1)S(1)}, bf16[256,2048]{1,0:T(8,128)(2,1)S(1)}, u32[]{:S(2)}, u32[]{:S(2)}) collective-permute-start(bf16[256,2048]{1,0:T(8,128)(2,1)S(1)} %add_convert_fusion.3), channel_id=1, source_target_pairs={{0,1},{1,2},{2,3},{3,0},{4,5},{5,6},{6,7},{7,4},{8,9},{9,10},{10,1... | collective-permute-start | bytes 3145736 | tf_op jit(solution)/shard_map/ppermute | solution.py:61
  413.2 13.1 %collective-permute-start.17 = (bf16[256,512]{1,0:T(8,128)(2,1)}, bf16[256,512]{1,0:T(8,128)(2,1)S(1)}, u32[]{:S(2)}, u32[]{:S(2)}) collective-permute-start(bf16[256,512]{1,0:T(8,128)(2,1)} %get-tuple-element.135), channel_id=1, source_target_pairs={{0,1},{1,2},{2,3},{3,0},{4,5},{5,6},{6,7},{7,4},{8,9},{9,10},{10,1... | collective-permute-start | bytes 786440 | tf_op jit(solution)/shard_map/ppermute | solution.py:61
  414.7 12.5 %collective-permute-start.18 = (bf16[256,512]{1,0:T(8,128)(2,1)}, bf16[256,512]{1,0:T(8,128)(2,1)S(1)}, u32[]{:S(2)}, u32[]{:S(2)}) collective-permute-start(bf16[256,512]{1,0:T(8,128)(2,1)} %get-tuple-element.136), channel_id=1, source_target_pairs={{0,2},{1,3},{2,0},{3,1},{4,6},{5,7},{6,4},{7,5},{8,10},{9,11},{10,... | collective-permute-start | bytes 786440 | tf_op jit(solution)/shard_map/ppermute | solution.py:61
  416.6 10.6 %collective-permute-start.19 = (bf16[256,512]{1,0:T(8,128)(2,1)}, bf16[256,512]{1,0:T(8,128)(2,1)S(1)}, u32[]{:S(2)}, u32[]{:S(2)}) collective-permute-start(bf16[256,512]{1,0:T(8,128)(2,1)} %get-tuple-element.137), channel_id=1, source_target_pairs={{0,3},{1,0},{2,1},{3,2},{4,7},{5,4},{6,5},{7,6},{8,11},{9,8},{10,9... | collective-permute-start | bytes 786440 | tf_op jit(solution)/shard_map/ppermute | solution.py:61
  446.2 137.7 %reduce-scatter.11.cloned.1.call-start = ((), (), s32[]{:S(2)}) async-start(), calls=%async_computation.10 | async-start | bytes 5308416 | tf_op jit(solution)/shard_map/reduce_scatter | solution.py:690
  454.1 25.7 %collective-permute-start.23 = (bf16[256,2048]{1,0:T(8,128)(2,1)}, bf16[256,2048]{1,0:T(8,128)(2,1)S(1)}, u32[]{:S(2)}, u32[]{:S(2)}) collective-permute-start(bf16[256,2048]{1,0:T(8,128)(2,1)} %get-tuple-element.161), channel_id=1, source_target_pairs={{0,1},{1,2},{2,3},{3,0},{4,5},{5,6},{6,7},{7,4},{8,9},{9,10},{10,1... | collective-permute-start | bytes 3145736 | tf_op jit(solution)/shard_map/ppermute | solution.py:61
  482.3 26.3 %collective-permute-start.24 = (bf16[256,2048]{1,0:T(8,128)(2,1)}, bf16[256,2048]{1,0:T(8,128)(2,1)}, u32[]{:S(2)}, u32[]{:S(2)}) collective-permute-start(bf16[256,2048]{1,0:T(8,128)(2,1)} %add_convert_fusion.2), channel_id=1, source_target_pairs={{0,1},{1,2},{2,3},{3,0},{4,5},{5,6},{6,7},{7,4},{8,9},{9,10},{10,1... | collective-permute-start | bytes 3145736 | tf_op jit(solution)/shard_map/ppermute | solution.py:61
  493.6 15.0 %copy-start.14 = (bf16[256,2048]{1,0:T(8,128)(2,1)S(1)}, bf16[256,2048]{1,0:T(8,128)(2,1)}, u32[]{:S(2)}) copy-start(bf16[256,2048]{1,0:T(8,128)(2,1)} %get-tuple-element.159) | copy-start | bytes 3145732
  496.1 15.4 %copy-start.12 = (bf16[256,2048]{1,0:T(8,128)(2,1)S(1)}, bf16[256,2048]{1,0:T(8,128)(2,1)}, u32[]{:S(2)}) copy-start(bf16[256,2048]{1,0:T(8,128)(2,1)} %get-tuple-element.162) | copy-start | bytes 3145732
  496.1 16.8 %collective-permute-start.21 = (f32[2560]{0:T(1024)S(1)}, f32[2560]{0:T(1024)S(1)}, u32[]{:S(2)}, u32[]{:S(2)}) collective-permute-start(f32[2560]{0:T(1024)S(1)} %pad_maximum_fusion.2), channel_id=1, source_target_pairs={{0,2},{1,3},{2,0},{3,1},{4,6},{5,7},{6,4},{7,5},{8,10},{9,11},{10,... | collective-permute-start | bytes 30728 | tf_op jit(solution)/shard_map/ppermute | solution.py:61
  501.1 11.8 %collective-permute-start.22 = (f32[2560]{0:T(1024)S(1)}, f32[2560]{0:T(1024)S(1)}, u32[]{:S(2)}, u32[]{:S(2)}) collective-permute-start(f32[2560]{0:T(1024)S(1)} %pad_maximum_fusion.2), channel_id=1, source_target_pairs={{0,3},{1,0},{2,1},{3,2},{4,7},{5,4},{6,5},{7,6},{8,11},{9,8},{10,9... | collective-permute-start | bytes 30728 | tf_op jit(solution)/shard_map/ppermute | solution.py:61
  501.9 11.0 %collective-permute-start.20 = (f32[2560]{0:T(1024)S(1)}, f32[2560]{0:T(1024)S(1)}, u32[]{:S(2)}, u32[]{:S(2)}) collective-permute-start(f32[2560]{0:T(1024)S(1)} %pad_maximum_fusion.2), channel_id=1, source_target_pairs={{0,1},{1,2},{2,3},{3,0},{4,5},{5,6},{6,7},{7,4},{8,9},{9,10},{10,1... | collective-permute-start | bytes 30728 | tf_op jit(solution)/shard_map/ppermute | solution.py:61
  511.2 18.0 %collective-permute-start.25 = (bf16[256,2048]{1,0:T(8,128)(2,1)}, bf16[256,2048]{1,0:T(8,128)(2,1)S(1)}, u32[]{:S(2)}, u32[]{:S(2)}) collective-permute-start(bf16[256,2048]{1,0:T(8,128)(2,1)} %add_convert_fusion.1), channel_id=1, source_target_pairs={{0,1},{1,2},{2,3},{3,0},{4,5},{5,6},{6,7},{7,4},{8,9},{9,10},{10,1... | collective-permute-start | bytes 3145736 | tf_op jit(solution)/shard_map/ppermute | solution.py:61
  530.4 12.8 %copy-start.2 = (bf16[256,2048]{1,0:T(8,128)(2,1)S(1)}, bf16[256,2048]{1,0:T(8,128)(2,1)}, u32[]{:S(2)}) copy-start(bf16[256,2048]{1,0:T(8,128)(2,1)} %own.3) | copy-start | bytes 3145732
  532.5 12.6 %copy-start.7 = (bf16[256,2048]{1,0:T(8,128)(2,1)S(1)}, bf16[256,2048]{1,0:T(8,128)(2,1)}, u32[]{:S(2)}) copy-start(bf16[256,2048]{1,0:T(8,128)(2,1)} %copy-done.6) | copy-start | bytes 3145732
  532.6 12.6 %copy-start.11 = (f32[256,2048]{1,0:T(8,128)S(1)}, f32[256,2048]{1,0:T(8,128)}, u32[]{:S(2)}) copy-start(f32[256,2048]{1,0:T(8,128)} %get-tuple-element.165) | copy-start | bytes 6291460
  533.9 20.6 %collective-permute-start.27 = (bf16[256,512]{1,0:T(8,128)(2,1)S(1)}, bf16[256,512]{1,0:T(8,128)(2,1)S(1)}, u32[]{:S(2)}, u32[]{:S(2)}) collective-permute-start(bf16[256,512]{1,0:T(8,128)(2,1)S(1)} %get-tuple-element.223), channel_id=1, source_target_pairs={{0,3},{1,0},{2,1},{3,2},{4,7},{5,4},{6,5},{7,6},{8,11},{9,8},{10,9... | collective-permute-start | bytes 786440 | tf_op jit(solution)/shard_map/ppermute | solution.py:61
  538.8 15.7 %collective-permute-start.29 = (bf16[256,512]{1,0:T(8,128)(2,1)S(1)}, bf16[256,512]{1,0:T(8,128)(2,1)S(1)}, u32[]{:S(2)}, u32[]{:S(2)}) collective-permute-start(bf16[256,512]{1,0:T(8,128)(2,1)S(1)} %get-tuple-element.224), channel_id=1, source_target_pairs={{0,1},{1,2},{2,3},{3,0},{4,5},{5,6},{6,7},{7,4},{8,9},{9,10},{10,1... | collective-permute-start | bytes 786440 | tf_op jit(solution)/shard_map/ppermute | solution.py:61
  538.8 34.2 %collective-permute-start.28 = (bf16[256,512]{1,0:T(8,128)(2,1)S(1)}, bf16[256,512]{1,0:T(8,128)(2,1)S(1)}, u32[]{:S(2)}, u32[]{:S(2)}) collective-permute-start(bf16[256,512]{1,0:T(8,128)(2,1)S(1)} %get-tuple-element.225), channel_id=1, source_target_pairs={{0,2},{1,3},{2,0},{3,1},{4,6},{5,7},{6,4},{7,5},{8,10},{9,11},{10,... | collective-permute-start | bytes 786440 | tf_op jit(solution)/shard_map/ppermute | solution.py:61
  539.4 35.7 %collective-permute-start.26 = (bf16[256,2048]{1,0:T(8,128)(2,1)}, bf16[256,2048]{1,0:T(8,128)(2,1)}, u32[]{:S(2)}, u32[]{:S(2)}) collective-permute-start(bf16[256,2048]{1,0:T(8,128)(2,1)} %add_convert_fusion), channel_id=1, source_target_pairs={{0,1},{1,2},{2,3},{3,0},{4,5},{5,6},{6,7},{7,4},{8,9},{9,10},{10,1... | collective-permute-start | bytes 3145736 | tf_op jit(solution)/shard_map/ppermute | solution.py:61
  547.0 28.1 %copy-start.3 = (f32[256,2048]{1,0:T(8,128)S(1)}, f32[256,2048]{1,0:T(8,128)}, u32[]{:S(2)}) copy-start(f32[256,2048]{1,0:T(8,128)} %get-tuple-element.107.hidden) | copy-start | bytes 6291460
  547.0 28.1 %copy-start.25 = (f32[256]{0:T(256)S(1)}, f32[256]{0:T(256)}, u32[]{:S(2)}) copy-start(f32[256]{0:T(256)} %copy-done.24) | copy-start | bytes 3076
  (21 other events, 105.1 us)
Sparse Core Ops, SparseCore 0:
  12.5 41.6 all-gather.3
  87.8 105.3 all-gather.5
  195.1 45.5 all-gather.7
  269.3 60.7 reduce-scatter.4
  343.3 90.7 reduce-scatter.6
  446.3 72.3 reduce-scatter.8
  529.4 54.4 reduce-scatter.10

commit v3 on v2

--- a/solution.py
+++ b/solution.py
@@ -488,23 +488,29 @@
     )(place, qkv, qkv, qkv, *d_slots, lse, pre, pre, cos, sin, gain_q, gain_k)
 
 
-def back_project_kernel(size, q, k, v, w, *outs):
-    for slot, out in zip((1, 2, 3, 0), outs):
-        rows = slice(slot * size, (slot + 1) * size)
-        total = nt(q[rows], w[:, :512]) + nt(k[rows], w[:, 512:768]) + nt(v[rows], w[:, 768:])
+def back_project_kernel(lone, slots, size, q, k, v, w, *outs):
+    for slot, out in zip(slots, outs):
+        rows = slice(0, size) if lone else slice(slot * size, (slot + 1) * size)
+        total, at = 0.0, 0
+        for ref in (q, k, v):
+            total += nt(ref[rows], w[:, at : at + ref.shape[1]])
+            at += ref.shape[1]
         out[...] = total.astype(bf16)
 
 
-def back_project(parts, w, width, size):
+def back_project(parts, w, slots, width, size):
     tile = 512
-    outs, out_specs = slot_shapes((1, 2, 3, 0), size, width, tile)
-    return call(
-        functools.partial(back_project_kernel, size),
+    lone = len(slots) == 1
+    rows = size if lone else WAYS * size
+    outs, out_specs = slot_shapes(slots, size, width, tile)
+    return call(
+        functools.partial(back_project_kernel, lone, slots, size),
         (width // tile,),
-        [whole(p.shape) for p in parts] + [pl.BlockSpec((tile, 1024), lambda n: (n, 0))],
+        [whole((rows, p.shape[1]), (slots[0] if lone else 0, 0)) for p in parts]
+        + [pl.BlockSpec((tile, 1024), lambda n: (n, 0))],
         outs,
         out_specs,
-        flops=2 * WAYS * size * width * 1024,
+        flops=2 * len(slots) * size * width * 1024,
         size=10 << 20,
     )(*parts, w)
 
@@ -519,6 +525,7 @@
         out[:, cols] = product.astype(bf16)
         total += jnp.sum(product * w[:, cols].astype(f32), axis=1, keepdims=True)
         at += ref.shape[1]
+    out[:, at:] = jnp.zeros((out.shape[0], out.shape[1] - at), bf16)
     gain_part[...] = total
 
 
@@ -532,8 +539,8 @@
         [pl.BlockSpec((rows, tile), lambda j: (0, j))]
         + [whole(p.shape) for p in parts]
         + [pl.BlockSpec((tile, cols), lambda j: (j, 0))],
-        [((width, cols), bf16), ((width, 128), f32)],
-        [pl.BlockSpec((tile, cols), lambda j: (j, 0)), pl.BlockSpec((tile, 128), lambda j: (j, 0))],
+        [((width, cols + 128), bf16), ((width, 128), f32)],
+        [pl.BlockSpec((tile, cols + 128), lambda j: (j, 0)), pl.BlockSpec((tile, 128), lambda j: (j, 0))],
         flops=2 * rows * width * 1024,
         size=16 << 20,
     )(normed, *parts, w)
@@ -568,7 +575,7 @@
     place_ref = place.reshape(1).astype(jnp.int32)
 
     w_out = w_output.T
-    x1, w1 = together(hop(tokens), hop(w_out))
+    x1, w1, w3 = together(hop(tokens), hop(w_out), shift_by(w_out, -1))
     offsets = jnp.arange(size, dtype=jnp.int32)
     position = jnp.concatenate([((place - j) % WAYS) * size + offsets for j in range(WAYS)])
     cos, sin = rope_tables(position)
@@ -576,7 +583,6 @@
     own_live = (position[:size] < seq_len).astype(f32)[:, None]
     d_branch = (cotangent.astype(f32) * own_live).astype(bf16)
     x2, w2, cos, sin, d_branch = together(hop(x1), hop(w1), cos, sin, d_branch)
-    w3 = hop(w2)
     x3, d_branch = together(hop(x2), d_branch)
     x_slots = [tokens, x1, x2, x3]
     d1 = hop(d_branch)
@@ -626,12 +632,13 @@
     (b1,) = back_feed(d_all, rest_full, (1,), width, size)
     b1, y_sum = together(b1, y_sum)
     b_sum = hop(b1)
+    b2, b3, b0 = back_feed(d_all, rest_full, (2, 3, 0), width, size)
+    b_sum, d_all = together(add(b2, b_sum), d_all)
+    b_sum = hop(b_sum)
     grads_feed = row_grads(normed_ffn, d_all, 0, 2)
-    d_all, grads_feed = together(d_all, grads_feed)
-    b2, b3, b0 = back_feed(d_all, rest_full, (2, 3, 0), width, size)
-    b_sum, grads_feed, grads_down = together(add(b2, b_sum), grads_feed, grads_down)
+    b_sum, grads_feed = together(b_sum, grads_feed)
+    grads_feed, grads_down = together(grads_feed, grads_down)
     grads_feed = lax.psum_scatter(grads_feed, "dp", scatter_dimension=0, tiled=True)
-    b_sum = hop(b_sum)
     b_sum, y_sum = together(hop(add(b3, b_sum)), y_sum)
     y_sum = hop(add(y2, y_sum))
 
@@ -646,14 +653,18 @@
     d_q, d_k, d_v, sum_q, sum_k = attend_back(
         place_ref, qkv, [p0, s1, s2, s3], log_total, pre, cos, sin, gain_q, gain_k
     )
-    d_q, grads_out, grads_feed = together(d_q, grads_out, grads_feed)
+    (e1,) = back_project((d_q, d_k, d_v), attn_full, (1,), width, size)
+    e1, d_q, grads_out, grads_feed = together(e1, d_q, grads_out, grads_feed)
     grads_out = lax.psum_scatter(grads_out, "dp", scatter_dimension=0, tiled=True)
+    e_sum = hop(e1)
+    y_sum = hop(add(y3, y_sum))
     parts = (d_q, d_k, d_v)
-    e1, e2, e3, e0 = back_project(parts, attn_full, width, size)
-    e_sum, d_q = together(e1, d_q)
-    parts = (d_q, d_k, d_v)
+    e2, e3, e0 = back_project(parts, attn_full, (2, 3, 0), width, size)
+    grads_attn, norm_part = attend_grads(normed_attn, parts, attn_full)
+    e_sum, grads_attn, norm_part, y_sum = together(
+        add(e2, e_sum), grads_attn, norm_part, y_sum
+    )
     e_sum = hop(e_sum)
-    grads_attn, norm_part = attend_grads(normed_attn, parts, attn_full)
     own_ffn = jnp.sum(
         w_gate.astype(f32) * grads_feed[:, :ff_width].astype(f32)
         + w_up.astype(f32) * grads_feed[:, ff_width:].astype(f32),
@@ -669,28 +680,27 @@
     )
     small = small + shift_by(small, 1) + shift_by(small, 2) + shift_by(small, 3)
     grad_norm_ffn = small[width : width + shard_rows]
-    spread = lambda v: jnp.pad(
-        v.reshape(data_ways, gain_rows), ((0, 0), (0, shard_rows - gain_rows))
-    ).reshape(-1, 1)
-    grads_attn = jnp.concatenate(
-        [
-            grads_attn,
-            small[:width, None].astype(bf16),
-            spread(small[width + shard_rows : width + shard_rows + HEAD_SIZE]).astype(bf16),
-            spread(small[width + shard_rows + HEAD_SIZE :]).astype(bf16),
-            jnp.zeros((width, 125), bf16),
+    gain_row = jnp.concatenate(
+        [
+            small[width + shard_rows :].reshape(2, data_ways, 1, gain_rows)[0],
+            small[width + shard_rows :].reshape(2, data_ways, 1, gain_rows)[1],
+            jnp.zeros((data_ways, 1, 127 - 2 * gain_rows), f32),
         ],
-        axis=1,
-    )
-    e_sum = hop(add(e2, e_sum))
-    e_sum = hop(add(e3, e_sum))
-    grads_attn, grads_out, e_sum, y_sum = together(
-        grads_attn, grads_out, e_sum, add(y3, y_sum)
-    )
+        axis=2,
+    )
+    gain_columns = jnp.concatenate(
+        [
+            small[:width].reshape(data_ways, shard_rows, 1),
+            jnp.pad(gain_row, ((0, 0), (0, shard_rows - 1), (0, 0))),
+        ],
+        axis=2,
+    ).reshape(width, 128).astype(bf16)
+    grads_attn = lax.dynamic_update_slice(grads_attn, gain_columns, (0, qkv_width))
+    grads_attn, grads_out, e_sum = together(grads_attn, grads_out, add(e3, e_sum))
+    e_sum = hop(e_sum)
     grads_attn = lax.psum_scatter(grads_attn, "dp", scatter_dimension=0, tiled=True)
     d_normed_attn = e0.astype(f32) + e_sum.astype(f32)
 
-    y_sum = hop(y_sum)
     ffn_out = y0.astype(f32) + y_sum.astype(f32)
     block_out = ((hidden + ffn_out) * own_live).astype(bf16)
     own_tokens = tokens.astype(f32)
@@ -704,9 +714,11 @@
     grad_key = grad_qkv[:, q_width : q_width + kv_width]
     grad_value = grad_qkv[:, q_width + kv_width :]
     grad_norm_attn = grads_attn[:, qkv_width].astype(f32)
-    grad_gain_query = grads_attn[:gain_rows, qkv_width + 1].astype(f32)
-    grad_gain_key = grads_attn[:gain_rows, qkv_width + 2].astype(f32)
+    gain_at = qkv_width + 1
+    grad_gain_query = grads_attn[0, gain_at : gain_at + gain_rows].astype(f32)
+    grad_gain_key = grads_attn[0, gain_at + gain_rows : gain_at + 2 * gain_rows].astype(f32)
     g0, g1, g2, g3 = [grads_out[:, k * q_width : (k + 1) * q_width] for k in range(WAYS)]
+    g0, d_tokens = together(g0, d_tokens.astype(bf16))
     grad_output = (
         g0.astype(f32)
         + shift_by(g1, -1).astype(f32)
@@ -715,7 +727,7 @@
     ).T
     return (
         block_out,
-        d_tokens.astype(bf16),
+        d_tokens,
         grad_norm_attn,
         grad_query,
         grad_key,

time: 604 us -> 593 us (0.982)
  local copies, waits for them, and re-layouts: 43.3 us -> 34 us
  waiting for transfers between devices: 270 us -> 262 us
    ppermute x30, waiting for transfers between devices: 264 us -> 255 us  [shift_by(): lax.ppermute(value, 'tensor', [(i, (i + step) % WAYS) for i in range(WAYS)])]
    concatenate x1, local copies, waits for them, and re-layouts: 8.46 us -> 0.08 us  [local(): jnp.concatenate([small[width + shard_rows:].reshape(2, data_ways, 1, gain...]
    pallas_call x1 -> x2, Pallas kernels: 7.85 us -> 13 us  [back_project(): call(functools.partial(back_project_kernel, lone, slots, size), (width //...]
    unnamed x82 -> x84, local copies, waits for them, and re-layouts: 19.4 us -> 19.4 us
  transfers between devices with their start and end apart: 37 -> 37, of which waited for: 18 -> 20; matrix products, arithmetic and copies ran while one was open for 11% -> 9% of each run, Pallas kernels for 32% -> 34%
where the time goes in v3:
time: 593 us; the launch traced here: 582 us
  waiting for transfers between devices  262 us (44%)
  Pallas kernels  198 us (33%)
  starting transfers between devices  40.3 us (7%)
  local copies, waits for them, and re-layouts  34 us (6%)
  other arithmetic  32.6 us (5%)
  between operations  15 us (3%)
    ppermute x30, waiting for transfers between devices, shift_by(): lax.ppermute(value, 'tensor', [(i, (i + step) % WAYS) for i in range(WAYS)])  255 us
    ppermute x30, starting transfers between devices, shift_by(): lax.ppermute(value, 'tensor', [(i, (i + step) % WAYS) for i in range(WAYS)])  40 us
    pallas_call x3, Pallas kernels, row_grads(): call(grads_kernel, (width // tile,), [pl.BlockSpec((rows, tile), lambda j...  36.1 us
    pallas_call x2, Pallas kernels, back_feed(): call(functools.partial(back_kernel, slots, size, lone), (width // tile,),...  24.3 us
    pallas_call x1, Pallas kernels, feed(): call(feed_kernel, (tiles,), [whole((rows, width)), col(0), col(1)], [((3,...  19.7 us
    unnamed x84, local copies, waits for them, and re-layouts  19.4 us
    pallas_call x1, Pallas kernels, mix(): call(mix_kernel, (WAYS,), [whole(x.shape) for x in x_slots] + [whole(c.sh...  19.1 us
    pallas_call x1, Pallas kernels, attend_back(): call(attend_back_kernel, (2,), [pl.BlockSpec(memory_space=pltpu.SMEM), co...  18 us
  transfers between devices with their start and end apart: 37, of which 20 were waited for; matrix products, arithmetic and copies ran while one was open for 9% of the time, Pallas kernels for 34%

profile of v3, /device:TPU:0, one launch (start us, length us, event | category | flops | bytes accessed | tf_op | source)
XLA Modules:
  0.0 582.3 jit_solution(16074144228772476349)
XLA Ops:
  10.5 2.0 concatenate.36
  12.7 5.1 collective-permute-start.2
  22.5 1.9 fusion.8
  24.5 6.6 %collective-permute-done.1 = bf16[256,512]{1,0:T(8,128)(2,1)} collective-permute-done((bf16[256,512]{1,0:T(8,128)(2,1)S(1)}, bf16[256,512]{1,0:T(8,128)(2,1)}, u32[]{:S(2)}, u32[]{:S(2)}) %collective-permute-start.1) | collective-permute-done | bytes 262176 | tf_op jit(solution)/shard_map/ppermute | solution.py:61
  31.1 21.3 %collective-permute-done.below = bf16[256,2048]{1,0:T(8,128)(2,1)} collective-permute-done((bf16[256,2048]{1,0:T(8,128)(2,1)S(1)}, bf16[256,2048]{1,0:T(8,128)(2,1)}, u32[]{:S(2)}, u32[]{:S(2)}) %collective-permute-start) | collective-permute-done | bytes 1048608 | tf_op jit(solution)/shard_map/ppermute | solution.py:61
  58.9 25.2 %collective-permute-done.4 = bf16[256,512]{1,0:T(8,128)(2,1)S(1)} collective-permute-done((bf16[256,512]{1,0:T(8,128)(2,1)}, bf16[256,512]{1,0:T(8,128)(2,1)S(1)}, u32[]{:S(2)}, u32[]{:S(2)}) %collective-permute-start.4) | collective-permute-done | bytes 262176 | tf_op jit(solution)/shard_map/ppermute | solution.py:61
  87.0 25.0 %collective-permute-done.5.above = bf16[256,2048]{1,0:T(8,128)(2,1)} collective-permute-done((bf16[256,2048]{1,0:T(8,128)(2,1)S(1)}, bf16[256,2048]{1,0:T(8,128)(2,1)}, u32[]{:S(2)}, u32[]{:S(2)}) %collective-permute-start.5) | collective-permute-done | bytes 1048608 | tf_op jit(solution)/shard_map/ppermute | solution.py:61
  116.0 11.9 %shard_map.246 = (bf16[1024,2048]{1,0:T(8,128)(2,1)}, bf16[1024,1024]{1,0:T(8,128)(2,1)}, f32[1024,768]{1,0:T(8,128)}) custom-call(bf16[256,2048]{1,0:T(8,128)(2,1)} %own.3, bf16[256,2048]{1,0:T(8,128)(2,1)} %collective-permute-done.below, bf16[256,2048]{1,0:T(8,128)(2,1)} %copy-done.20, bf16[256,2048]{1,0:T(8,128)(2,1)} %collective-permute-done.5.above, ...), custom_call_target="tpu_custom_call" | custom-call | flops 4294967296 | bytes 20971520 | tf_op jit(solution)/shard_map/pallas_call | solution.py:126
  128.0 10.3 %shard_map.247 = (bf16[1024,512]{1,0:T(8,128)(2,1)}, f32[1024,256]{1,0:T(8,128)}) custom-call(s32[1]{0:T(128)} %bitcast.2.place, bf16[1024,1024]{1,0:T(8,128)(2,1)} %get-tuple-element.105.q.k.v, bf16[1024,1024]{1,0:T(8,128)(2,1)} %get-tuple-element.105.q.k.v, bf16[1024,1024]{1,0:T(8,128)(2,1)} %get-tuple-element.105.q.k.v), custom_call_target="tpu_custom_call" | custom-call | flops 1073741824 | bytes 2097152 | tf_op jit(solution)/shard_map/pallas_call | solution.py:184
  138.3 24.2 %collective-permute-done.7.c1 = bf16[1024,512]{1,0:T(8,128)(2,1)S(1)} collective-permute-done((bf16[1024,512]{1,0:T(8,128)(2,1)}, bf16[1024,512]{1,0:T(8,128)(2,1)S(1)}, u32[]{:S(2)}, u32[]{:S(2)}) %collective-permute-start.7) | collective-permute-done | bytes 1048608 | tf_op jit(solution)/shard_map/ppermute | solution.py:61
  163.4 23.3 %collective-permute-done.8.c2 = bf16[1024,512]{1,0:T(8,128)(2,1)S(1)} collective-permute-done((bf16[1024,512]{1,0:T(8,128)(2,1)S(1)}, bf16[1024,512]{1,0:T(8,128)(2,1)S(1)}, u32[]{:S(2)}, u32[]{:S(2)}) %collective-permute-start.8) | collective-permute-done | bytes 1048608 | tf_op jit(solution)/shard_map/ppermute | solution.py:61
  188.1 20.9 %collective-permute-done.9.c3 = bf16[1024,512]{1,0:T(8,128)(2,1)S(1)} collective-permute-done((bf16[1024,512]{1,0:T(8,128)(2,1)S(1)}, bf16[1024,512]{1,0:T(8,128)(2,1)S(1)}, u32[]{:S(2)}, u32[]{:S(2)}) %collective-permute-start.9) | collective-permute-done | bytes 1048608 | tf_op jit(solution)/shard_map/ppermute | solution.py:61
  211.3 19.1 %shard_map.248 = (bf16[1024,2048]{1,0:T(8,128)(2,1)}, f32[256,2048]{1,0:T(8,128)}, bf16[256,2048]{1,0:T(8,128)(2,1)}) custom-call(bf16[256,2048]{1,0:T(8,128)(2,1)} %own.3, bf16[256,2048]{1,0:T(8,128)(2,1)} %collective-permute-done.below, bf16[256,2048]{1,0:T(8,128)(2,1)} %copy-done.20, bf16[256,2048]{1,0:T(8,128)(2,1)} %collective-permute-done.5.above, ...), custom_call_target="tpu_custom_call" | custom-call | flops 8589934592 | bytes 25165824 | tf_op jit(solution)/shard_map/pallas_call | solution.py:226
  230.4 3.1 collective-permute-done.10
  234.6 19.7 %shard_map.249.a.slopes = bf16[3,1024,1536]{2,1,0:T(8,128)(2,1)} custom-call(bf16[1024,2048]{1,0:T(8,128)(2,1)} %get-tuple-element.116.n, bf16[2048,5120]{1,0:T(8,128)(2,1)} %all-gather.6.cloned.1.call-done.wa.wb.w_gate.w_up.w, bf16[2048,5120]{1,0:T(8,128)(2,1)} %all-gather.6.cloned.1.call-done.wa.wb.w_gate.w_up.w), custom_call_target="tpu_custom_call" | custom-call | flops 12884901888 | bytes 27262976 | tf_op jit(solution)/shard_map/pallas_call | solution.py:258
  255.4 10.7 %shard_map.250 = bf16[2048,1536]{1,0:T(8,128)(2,1)} custom-call(bf16[1024,2048]{1,0:T(8,128)(2,1)} %constant_dynamic-update-slice_fusion.6.n.d, bf16[3,1024,1536]{2,1,0:T(8,128)(2,1)} %shard_map.249.a.slopes), custom_call_target="tpu_custom_call" | custom-call | flops 6442450944 | bytes 13631488 | tf_op jit(solution)/shard_map/pallas_call | solution.py:365
  266.2 10.6 %shard_map.251 = (bf16[256,2048]{1,0:T(8,128)(2,1)}, bf16[256,2048]{1,0:T(8,128)(2,1)}, bf16[256,2048]{1,0:T(8,128)(2,1)}, bf16[256,2048]{1,0:T(8,128)(2,1)}) custom-call(bf16[3,1024,1536]{2,1,0:T(8,128)(2,1)} %shard_map.249.a.slopes, bf16[2048,1536]{1,0:T(8,128)(2,1)} %all-gather.8.cloned.1.call-done.wa.w_down), custom_call_target="tpu_custom_call" | custom-call | flops 6442450944 | bytes 14680064 | tf_op jit(solution)/shard_map/pallas_call | solution.py:343
  276.9 14.3 %shard_map.252.a.b = bf16[2,1024,1536]{2,1,0:T(8,128)(2,1)} custom-call(bf16[1024,2048]{1,0:T(8,128)(2,1)} %constant_dynamic-update-slice_fusion.6.n.d, bf16[2048,1536]{1,0:T(8,128)(2,1)} %all-gather.8.cloned.1.call-done.wa.w_down, bf16[3,1024,1536]{2,1,0:T(8,128)(2,1)} %shard_map.249.a.slopes), custom_call_target="tpu_custom_call" | custom-call | flops 6442450944 | bytes 23068672 | tf_op jit(solution)/shard_map/pallas_call | solution.py:283
  291.2 9.1 %shard_map.254 = bf16[256,2048]{1,0:T(8,128)(2,1)} custom-call(bf16[2,1024,1536]{2,1,0:T(8,128)(2,1)} %shard_map.252.a.b, bf16[2,1024,1536]{2,1,0:T(8,128)(2,1)} %shard_map.252.a.b, bf16[2048,5120]{1,0:T(8,128)(2,1)} %all-gather.6.cloned.1.call-done.wa.wb.w_gate.w_up.w, bf16[2048,5120]{1,0:T(8,128)(2,1)} %all-gather.6.cloned.1.call-done.wa.wb.w_gate.w_up.w), custom_call_target="tpu_custom_call" | custom-call | flops 3221225472 | bytes 20971520 | tf_op jit(solution)/shard_map/pallas_call | solution.py:317
  300.2 1.9 collective-permute-start.13
  302.1 15.2 %shard_map.253 = (bf16[256,2048]{1,0:T(8,128)(2,1)}, bf16[256,2048]{1,0:T(8,128)(2,1)}, bf16[256,2048]{1,0:T(8,128)(2,1)}) custom-call(bf16[2,1024,1536]{2,1,0:T(8,128)(2,1)} %shard_map.252.a.b, bf16[2,1024,1536]{2,1,0:T(8,128)(2,1)} %shard_map.252.a.b, bf16[2048,5120]{1,0:T(8,128)(2,1)} %all-gather.6.cloned.1.call-done.wa.wb.w_gate.w_up.w, ...), custom_call_target="tpu_custom_call" | custom-call | flops 9663676416 | bytes 20971520 | tf_op jit(solution)/shard_map/pallas_call | solution.py:317
  317.3 4.2 collective-permute-done.13
  323.2 2.4 collective-permute-start.14
  325.5 18.7 %shard_map.255 = bf16[2048,3072]{1,0:T(8,128)(2,1)} custom-call(bf16[1024,2048]{1,0:T(8,128)(2,1)} %get-tuple-element.116.n, bf16[2,1024,1536]{2,1,0:T(8,128)(2,1)} %shard_map.252.a.b), custom_call_target="tpu_custom_call" | custom-call | flops 12884901888 | bytes 23068672 | tf_op jit(solution)/shard_map/pallas_call | solution.py:365
  348.9 21.1 %collective-permute-done.15.arrived = bf16[256,2048]{1,0:T(8,128)(2,1)S(1)} collective-permute-done((bf16[256,2048]{1,0:T(8,128)(2,1)S(1)}, bf16[256,2048]{1,0:T(8,128)(2,1)S(1)}, u32[]{:S(2)}, u32[]{:S(2)}) %collective-permute-start.15) | collective-permute-done | bytes 1048608 | tf_op jit(solution)/shard_map/ppermute | solution.py:61
  370.3 1.9 collective-permute-start.16
  373.5 10.7 %shard_map.256 = (f32[256,2048]{1,0:T(8,128)}, bf16[256,2048]{1,0:T(8,128)(2,1)}, bf16[256,512]{1,0:T(8,128)(2,1)}, bf16[256,512]{1,0:T(8,128)(2,1)}, bf16[256,5...) custom-call(bf16[256,2048]{1,0:T(8,128)(2,1)} %get-tuple-element.123.own, bf16[256,2048]{1,0:T(8,128)(2,1)} %copy-done.16, ...), custom_call_target="tpu_custom_call" | custom-call | flops 2147483648 | bytes 16777216 | tf_op jit(solution)/shard_map/pallas_call | solution.py:402
  384.2 10.4 %collective-permute-done.16 = bf16[256,2048]{1,0:T(8,128)(2,1)S(1)} collective-permute-done((bf16[256,2048]{1,0:T(8,128)(2,1)S(1)}, bf16[256,2048]{1,0:T(8,128)(2,1)S(1)}, u32[]{:S(2)}, u32[]{:S(2)}) %collective-permute-start.16) | collective-permute-done | bytes 1048608 | tf_op jit(solution)/shard_map/ppermute | solution.py:61
  394.6 1.9 collective-permute-start.17
  396.5 1.9 collective-permute-start.18
  398.5 11.4 %collective-permute-start.19 = (bf16[256,512]{1,0:T(8,128)(2,1)}, bf16[256,512]{1,0:T(8,128)(2,1)S(1)}, u32[]{:S(2)}, u32[]{:S(2)}) collective-permute-start(bf16[256,512]{1,0:T(8,128)(2,1)} %get-tuple-element.141), channel_id=1, source_target_pairs={{0,3},{1,0},{2,1},{3,2},{4,7},{5,4},{6,5},{7,6},{8,11},{9,8},{10,9... | collective-permute-start | bytes 786440 | tf_op jit(solution)/shard_map/ppermute | solution.py:61
  409.8 6.7 %shard_map.257 = bf16[2048,2048]{1,0:T(8,128)(2,1)} custom-call(bf16[256,2048]{1,0:T(8,128)(2,1)} %get-tuple-element.142.n, bf16[1,256,2048]{2,1,0:T(8,128)(2,1)} %bitcast.30), custom_call_target="tpu_custom_call" | custom-call | flops 2147483648 | bytes 13631488 | tf_op jit(solution)/shard_map/pallas_call | solution.py:365
  417.4 18.0 %shard_map.258 = (bf16[1024,512]{1,0:T(8,128)(2,1)}, bf16[1024,256]{1,0:T(8,128)(2,1)}, bf16[1024,256]{1,0:T(8,128)(2,1)}, f32[8,256]{1,0:T(8,128)}, f32[8,256]{1,0:T(8,128)}) custom-call(s32[1]{0:T(128)} %bitcast.2.place, bf16[1024,1024]{1,0:T(8,128)(2,1)} %get-tuple-element.105.q.k.v, bf16[1024,1024]{1,0:T(8,128)(2,1)} %get-tuple-element.105.q.k.v, ...), custom_call_target="tpu_custom_call" | custom-call | flops 5368709120 | bytes 12582912 | tf_op jit(solution)/shard_map/pallas_call | solution.py:469
  435.4 5.0 shard_map.259
  444.6 8.0 %shard_map.260 = (bf16[256,2048]{1,0:T(8,128)(2,1)}, bf16[256,2048]{1,0:T(8,128)(2,1)}, bf16[256,2048]{1,0:T(8,128)(2,1)}) custom-call(bf16[1024,512]{1,0:T(8,128)(2,1)} %get-tuple-element.156.q, bf16[1024,256]{1,0:T(8,128)(2,1)} %get-tuple-element.150.k, bf16[1024,256]{1,0:T(8,128)(2,1)} %get-tuple-element.151.v, ...), custom_call_target="tpu_custom_call" | custom-call | flops 3221225472 | bytes 10485760 | tf_op jit(solution)/shard_map/pallas_call | solution.py:506
  452.6 2.5 fusion.15
  455.1 10.1 %shard_map.261 = (bf16[2048,1152]{1,0:T(8,128)(2,1)}, f32[2048,128]{1,0:T(8,128)}) custom-call(bf16[1024,2048]{1,0:T(8,128)(2,1)} %get-tuple-element.159.n, bf16[1024,512]{1,0:T(8,128)(2,1)} %get-tuple-element.156.q, bf16[1024,256]{1,0:T(8,128)(2,1)} %get-tuple-element.150.k, bf16[1024,256]{1,0:T(8,128)(2,1)} %get-tuple-element.151.v, ...), custom_call_target="tpu_custom_call" | custom-call | flops 4294967296 | bytes 16777216 | tf_op jit(solution)/shard_map/pallas_call | solution.py:536
  465.2 22.9 %collective-permute-done.20 = bf16[256,2048]{1,0:T(8,128)(2,1)S(1)} collective-permute-done((bf16[256,2048]{1,0:T(8,128)(2,1)S(1)}, bf16[256,2048]{1,0:T(8,128)(2,1)S(1)}, u32[]{:S(2)}, u32[]{:S(2)}) %collective-permute-start.20) | collective-permute-done | bytes 1048608 | tf_op jit(solution)/shard_map/ppermute | solution.py:61
  489.2 2.1 collective-permute-start.23
  493.6 17.9 %collective-permute-done.23 = f32[2560]{0:T(1024)S(1)} collective-permute-done((f32[2560]{0:T(1024)S(1)}, f32[2560]{0:T(1024)S(1)}, u32[]{:S(2)}, u32[]{:S(2)}) %collective-permute-start.23) | collective-permute-done | bytes 10272 | tf_op jit(solution)/shard_map/ppermute | solution.py:61
  513.9 2.6 add_convert_fusion
  519.0 3.2 copy.62
  522.2 3.4 multiply_convert_fusion
  526.2 2.6 collective-permute-start.27
  530.3 14.5 %collective-permute-done.26 = bf16[256,2048]{1,0:T(8,128)(2,1)S(1)} collective-permute-done((bf16[256,2048]{1,0:T(8,128)(2,1)}, bf16[256,2048]{1,0:T(8,128)(2,1)S(1)}, u32[]{:S(2)}, u32[]{:S(2)}) %collective-permute-start.26) | collective-permute-done | bytes 1048608 | tf_op jit(solution)/shard_map/ppermute | solution.py:61
  547.6 5.7 collective-permute-done.29
  553.3 8.4 %collective-permute-done.28 = bf16[256,512]{1,0:T(8,128)(2,1)S(1)} collective-permute-done((bf16[256,512]{1,0:T(8,128)(2,1)S(1)}, bf16[256,512]{1,0:T(8,128)(2,1)S(1)}, u32[]{:S(2)}, u32[]{:S(2)}) %collective-permute-start.28) | collective-permute-done | bytes 262176 | tf_op jit(solution)/shard_map/ppermute | solution.py:61
  562.8 6.8 %reduce-scatter.11.cloned.1.call-done = bf16[256,1152]{1,0:T(8,128)(2,1)} async-done(((bf16[2048,1152]{1,0:T(8,128)(2,1)}), bf16[256,1152]{1,0:T(8,128)(2,1)}) %reduce-scatter.11.cloned.1.call-update) | async-done | bytes 589840 | tf_op jit(solution)/shard_map/reduce_scatter | solution.py:701
  (198 shorter events, 61.3 us)
Async XLA Ops:
  7.2 13.3 %copy-start.6 = (bf16[256,1536]{1,0:T(8,128)(2,1)S(1)}, bf16[256,1536]{1,0:T(8,128)(2,1)}, u32[]{:S(2)}) copy-start(bf16[256,1536]{1,0:T(8,128)(2,1)} %param.24) | copy-start | bytes 2359300
  7.2 104.8 %all-gather.4.cloned.1.call-start = ((), (), s32[]{:S(2)}) async-start(), calls=%async_computation.4 | async-start | bytes 5308416 | tf_op jit(solution)/shard_map/all_gather | solution.py:597
  12.5 198.8 %all-gather.6.cloned.1.call-start = ((), (), s32[]{:S(2)}) async-start(), calls=%async_computation.5 | async-start | bytes 23592960 | tf_op jit(solution)/shard_map/all_gather | solution.py:605
  12.7 11.8 %collective-permute-start.2 = (bf16[256,512]{1,0:T(8,128)(2,1)S(1)}, bf16[256,512]{1,0:T(8,128)(2,1)S(1)}, u32[]{:S(2)}, u32[]{:S(2)}) collective-permute-start(bf16[256,512]{1,0:T(8,128)(2,1)S(1)} %bitcast.31), channel_id=1, source_target_pairs={{0,3},{1,0},{2,1},{3,2},{4,7},{5,4},{6,5},{7,6},{8,11},{9,8},{10,9... | collective-permute-start | bytes 786440 | tf_op jit(solution)/shard_map/ppermute | solution.py:61
  17.8 13.3 %collective-permute-start.1 = (bf16[256,512]{1,0:T(8,128)(2,1)S(1)}, bf16[256,512]{1,0:T(8,128)(2,1)}, u32[]{:S(2)}, u32[]{:S(2)}) collective-permute-start(bf16[256,512]{1,0:T(8,128)(2,1)S(1)} %bitcast.32), channel_id=1, source_target_pairs={{0,1},{1,2},{2,3},{3,0},{4,5},{5,6},{6,7},{7,4},{8,9},{9,10},{10,1... | collective-permute-start | bytes 786440 | tf_op jit(solution)/shard_map/ppermute | solution.py:61
  17.8 34.7 %collective-permute-start = (bf16[256,2048]{1,0:T(8,128)(2,1)S(1)}, bf16[256,2048]{1,0:T(8,128)(2,1)}, u32[]{:S(2)}, u32[]{:S(2)}) collective-permute-start(bf16[256,2048]{1,0:T(8,128)(2,1)S(1)} %copy-done.1), channel_id=1, source_target_pairs={{0,1},{1,2},{2,3},{3,0},{4,5},{5,6},{6,7},{7,4},{8,9},{9,10},{10,1... | collective-permute-start | bytes 3145736 | tf_op jit(solution)/shard_map/ppermute | solution.py:61
  20.4 34.4 %copy-start.28 = (f32[256]{0:T(256)}, f32[256]{0:T(256)S(1)}, u32[]{:S(2)}) copy-start(f32[256]{0:T(256)S(1)} %compare_convert_fusion) | copy-start | bytes 3076
  21.5 33.3 %copy-start.4 = (bf16[256,2048]{1,0:T(8,128)(2,1)S(1)}, bf16[256,2048]{1,0:T(8,128)(2,1)}, u32[]{:S(2)}) copy-start(bf16[256,2048]{1,0:T(8,128)(2,1)} %cotangent.1) | copy-start | bytes 3145732
  52.5 31.7 %collective-permute-start.3 = (bf16[256,2048]{1,0:T(8,128)(2,1)}, bf16[256,2048]{1,0:T(8,128)(2,1)S(1)}, u32[]{:S(2)}, u32[]{:S(2)}) collective-permute-start(bf16[256,2048]{1,0:T(8,128)(2,1)} %collective-permute-done.below), channel_id=1, source_target_pairs={{0,1},{1,2},{2,3},{3,0},{4,5},{5,6},{6,7},{7,4},{8,9},{9,10},{10,1... | collective-permute-start | bytes 3145736 | tf_op jit(solution)/shard_map/ppermute | solution.py:61
  55.1 29.1 %collective-permute-start.4 = (bf16[256,512]{1,0:T(8,128)(2,1)}, bf16[256,512]{1,0:T(8,128)(2,1)S(1)}, u32[]{:S(2)}, u32[]{:S(2)}) collective-permute-start(bf16[256,512]{1,0:T(8,128)(2,1)} %collective-permute-done.1), channel_id=1, source_target_pairs={{0,1},{1,2},{2,3},{3,0},{4,5},{5,6},{6,7},{7,4},{8,9},{9,10},{10,1... | collective-permute-start | bytes 786440 | tf_op jit(solution)/shard_map/ppermute | solution.py:61
  57.1 28.6 %copy-start.24 = (bf16[1536,256]{1,0:T(8,128)(2,1)S(1)}, bf16[1536,256]{1,0:T(8,128)(2,1)}, u32[]{:S(2)}) copy-start(bf16[1536,256]{1,0:T(8,128)(2,1)} %param.26) | copy-start | bytes 2359300
  85.7 180.6 %all-gather.8.cloned.1.call-start = ((), (), s32[]{:S(2)}) async-start(), calls=%async_computation.6 | async-start | bytes 7077888 | tf_op jit(solution)/shard_map/all_gather | solution.py:610
  86.9 257.5 %reduce-scatter.5.cloned.1.call-start = ((), (), s32[]{:S(2)}) async-start(), calls=%async_computation.7 | async-start | bytes 7077888 | tf_op jit(solution)/shard_map/reduce_scatter | solution.py:627
  87.0 25.1 %collective-permute-start.5 = (bf16[256,2048]{1,0:T(8,128)(2,1)S(1)}, bf16[256,2048]{1,0:T(8,128)(2,1)}, u32[]{:S(2)}, u32[]{:S(2)}) collective-permute-start(bf16[256,2048]{1,0:T(8,128)(2,1)S(1)} %collective-permute-done.3.far), channel_id=1, source_target_pairs={{0,1},{1,2},{2,3},{3,0},{4,5},{5,6},{6,7},{7,4},{8,9},{9,10},{10,1... | collective-permute-start | bytes 3145736 | tf_op jit(solution)/shard_map/ppermute | solution.py:61
  112.0 26.2 %collective-permute-start.6 = (bf16[256,2048]{1,0:T(8,128)(2,1)S(1)}, bf16[256,2048]{1,0:T(8,128)(2,1)S(1)}, u32[]{:S(2)}, u32[]{:S(2)}) collective-permute-start(bf16[256,2048]{1,0:T(8,128)(2,1)S(1)} %multiply_convert_fusion.1), channel_id=1, source_target_pairs={{0,1},{1,2},{2,3},{3,0},{4,5},{5,6},{6,7},{7,4},{8,9},{9,10},{10,1... | collective-permute-start | bytes 3145736 | tf_op jit(solution)/shard_map/ppermute | solution.py:61
  138.2 24.2 %collective-permute-start.7 = (bf16[1024,512]{1,0:T(8,128)(2,1)}, bf16[1024,512]{1,0:T(8,128)(2,1)S(1)}, u32[]{:S(2)}, u32[]{:S(2)}) collective-permute-start(bf16[1024,512]{1,0:T(8,128)(2,1)} %get-tuple-element.108.c0), channel_id=1, source_target_pairs={{0,1},{1,2},{2,3},{3,0},{4,5},{5,6},{6,7},{7,4},{8,9},{9,10},{10,1... | collective-permute-start | bytes 3145736 | tf_op jit(solution)/shard_map/ppermute | solution.py:61
  163.4 23.3 %collective-permute-start.8 = (bf16[1024,512]{1,0:T(8,128)(2,1)S(1)}, bf16[1024,512]{1,0:T(8,128)(2,1)S(1)}, u32[]{:S(2)}, u32[]{:S(2)}) collective-permute-start(bf16[1024,512]{1,0:T(8,128)(2,1)S(1)} %collective-permute-done.7.c1), channel_id=1, source_target_pairs={{0,1},{1,2},{2,3},{3,0},{4,5},{5,6},{6,7},{7,4},{8,9},{9,10},{10,1... | collective-permute-start | bytes 3145736 | tf_op jit(solution)/shard_map/ppermute | solution.py:61
  186.8 22.2 %collective-permute-start.9 = (bf16[1024,512]{1,0:T(8,128)(2,1)S(1)}, bf16[1024,512]{1,0:T(8,128)(2,1)S(1)}, u32[]{:S(2)}, u32[]{:S(2)}) collective-permute-start(bf16[1024,512]{1,0:T(8,128)(2,1)S(1)} %collective-permute-done.8.c2), channel_id=1, source_target_pairs={{0,1},{1,2},{2,3},{3,0},{4,5},{5,6},{6,7},{7,4},{8,9},{9,10},{10,1... | collective-permute-start | bytes 3145736 | tf_op jit(solution)/shard_map/ppermute | solution.py:61
  210.0 23.6 %collective-permute-start.10 = (bf16[256,2048]{1,0:T(8,128)(2,1)S(1)}, bf16[256,2048]{1,0:T(8,128)(2,1)S(1)}, u32[]{:S(2)}, u32[]{:S(2)}) collective-permute-start(bf16[256,2048]{1,0:T(8,128)(2,1)S(1)} %collective-permute-done.6), channel_id=1, source_target_pairs={{0,1},{1,2},{2,3},{3,0},{4,5},{5,6},{6,7},{7,4},{8,9},{9,10},{10,1... | collective-permute-start | bytes 3145736 | tf_op jit(solution)/shard_map/ppermute | solution.py:61
  233.5 20.8 %collective-permute-start.11 = (bf16[256,2048]{1,0:T(8,128)(2,1)S(1)}, bf16[256,2048]{1,0:T(8,128)(2,1)S(1)}, u32[]{:S(2)}, u32[]{:S(2)}) collective-permute-start(bf16[256,2048]{1,0:T(8,128)(2,1)S(1)} %collective-permute-done.10), channel_id=1, source_target_pairs={{0,1},{1,2},{2,3},{3,0},{4,5},{5,6},{6,7},{7,4},{8,9},{9,10},{10,1... | collective-permute-start | bytes 3145736 | tf_op jit(solution)/shard_map/ppermute | solution.py:61
  266.2 174.3 %reduce-scatter.7.cloned.1.call-start = ((), (), s32[]{:S(2)}) async-start(), calls=%async_computation.8 | async-start | bytes 14155776 | tf_op jit(solution)/shard_map/reduce_scatter | solution.py:641
  276.9 23.4 %collective-permute-start.12 = (bf16[256,2048]{1,0:T(8,128)(2,1)}, bf16[256,2048]{1,0:T(8,128)(2,1)S(1)}, u32[]{:S(2)}, u32[]{:S(2)}) collective-permute-start(bf16[256,2048]{1,0:T(8,128)(2,1)} %get-tuple-element.126), channel_id=1, source_target_pairs={{0,1},{1,2},{2,3},{3,0},{4,5},{5,6},{6,7},{7,4},{8,9},{9,10},{10,1... | collective-permute-start | bytes 3145736 | tf_op jit(solution)/shard_map/ppermute | solution.py:61
  300.2 21.3 %collective-permute-start.13 = (bf16[256,2048]{1,0:T(8,128)(2,1)}, bf16[256,2048]{1,0:T(8,128)(2,1)S(1)}, u32[]{:S(2)}, u32[]{:S(2)}) collective-permute-start(bf16[256,2048]{1,0:T(8,128)(2,1)} %shard_map.254), channel_id=1, source_target_pairs={{0,1},{1,2},{2,3},{3,0},{4,5},{5,6},{6,7},{7,4},{8,9},{9,10},{10,1... | collective-permute-start | bytes 3145736 | tf_op jit(solution)/shard_map/ppermute | solution.py:61
  323.2 21.3 %collective-permute-start.14 = (bf16[256,2048]{1,0:T(8,128)(2,1)S(1)}, bf16[256,2048]{1,0:T(8,128)(2,1)}, u32[]{:S(2)}, u32[]{:S(2)}) collective-permute-start(bf16[256,2048]{1,0:T(8,128)(2,1)S(1)} %add_convert_fusion.5), channel_id=1, source_target_pairs={{0,1},{1,2},{2,3},{3,0},{4,5},{5,6},{6,7},{7,4},{8,9},{9,10},{10,1... | collective-permute-start | bytes 3145736 | tf_op jit(solution)/shard_map/ppermute | solution.py:61
  344.5 25.5 %copy-start.13 = (bf16[256,2048]{1,0:T(8,128)(2,1)S(1)}, bf16[256,2048]{1,0:T(8,128)(2,1)}, u32[]{:S(2)}) copy-start(bf16[256,2048]{1,0:T(8,128)(2,1)} %get-tuple-element.137) | copy-start | bytes 3145732
  344.5 172.0 %reduce-scatter.9.cloned.1.call-start = ((), (), s32[]{:S(2)}) async-start(), calls=%async_computation.9 | async-start | bytes 9437184 | tf_op jit(solution)/shard_map/reduce_scatter | solution.py:658
  347.1 22.9 %collective-permute-start.15 = (bf16[256,2048]{1,0:T(8,128)(2,1)S(1)}, bf16[256,2048]{1,0:T(8,128)(2,1)S(1)}, u32[]{:S(2)}, u32[]{:S(2)}) collective-permute-start(bf16[256,2048]{1,0:T(8,128)(2,1)S(1)} %add_convert_fusion.4), channel_id=1, source_target_pairs={{0,1},{1,2},{2,3},{3,0},{4,5},{5,6},{6,7},{7,4},{8,9},{9,10},{10,1... | collective-permute-start | bytes 3145736 | tf_op jit(solution)/shard_map/ppermute | solution.py:61
  370.3 24.3 %collective-permute-start.16 = (bf16[256,2048]{1,0:T(8,128)(2,1)S(1)}, bf16[256,2048]{1,0:T(8,128)(2,1)S(1)}, u32[]{:S(2)}, u32[]{:S(2)}) collective-permute-start(bf16[256,2048]{1,0:T(8,128)(2,1)S(1)} %add_convert_fusion.3), channel_id=1, source_target_pairs={{0,1},{1,2},{2,3},{3,0},{4,5},{5,6},{6,7},{7,4},{8,9},{9,10},{10,1... | collective-permute-start | bytes 3145736 | tf_op jit(solution)/shard_map/ppermute | solution.py:61
  394.6 21.9 %collective-permute-start.17 = (bf16[256,512]{1,0:T(8,128)(2,1)}, bf16[256,512]{1,0:T(8,128)(2,1)S(1)}, u32[]{:S(2)}, u32[]{:S(2)}) collective-permute-start(bf16[256,512]{1,0:T(8,128)(2,1)} %get-tuple-element.139), channel_id=1, source_target_pairs={{0,1},{1,2},{2,3},{3,0},{4,5},{5,6},{6,7},{7,4},{8,9},{9,10},{10,1... | collective-permute-start | bytes 786440 | tf_op jit(solution)/shard_map/ppermute | solution.py:61
  396.5 20.0 %collective-permute-start.18 = (bf16[256,512]{1,0:T(8,128)(2,1)}, bf16[256,512]{1,0:T(8,128)(2,1)S(1)}, u32[]{:S(2)}, u32[]{:S(2)}) collective-permute-start(bf16[256,512]{1,0:T(8,128)(2,1)} %get-tuple-element.140), channel_id=1, source_target_pairs={{0,2},{1,3},{2,0},{3,1},{4,6},{5,7},{6,4},{7,5},{8,10},{9,11},{10,... | collective-permute-start | bytes 786440 | tf_op jit(solution)/shard_map/ppermute | solution.py:61
  398.5 18.1 %collective-permute-start.19 = (bf16[256,512]{1,0:T(8,128)(2,1)}, bf16[256,512]{1,0:T(8,128)(2,1)S(1)}, u32[]{:S(2)}, u32[]{:S(2)}) collective-permute-start(bf16[256,512]{1,0:T(8,128)(2,1)} %get-tuple-element.141), channel_id=1, source_target_pairs={{0,3},{1,0},{2,1},{3,2},{4,7},{5,4},{6,5},{7,6},{8,11},{9,8},{10,9... | collective-permute-start | bytes 786440 | tf_op jit(solution)/shard_map/ppermute | solution.py:61
  440.5 129.2 %reduce-scatter.11.cloned.1.call-start = ((), (), s32[]{:S(2)}) async-start(), calls=%async_computation.10 | async-start | bytes 5308416 | tf_op jit(solution)/shard_map/reduce_scatter | solution.py:701
  443.0 45.5 %collective-permute-start.21 = (bf16[256,2048]{1,0:T(8,128)(2,1)}, bf16[256,2048]{1,0:T(8,128)(2,1)}, u32[]{:S(2)}, u32[]{:S(2)}) collective-permute-start(bf16[256,2048]{1,0:T(8,128)(2,1)} %add_convert_fusion.1), channel_id=1, source_target_pairs={{0,1},{1,2},{2,3},{3,0},{4,5},{5,6},{6,7},{7,4},{8,9},{9,10},{10,1... | collective-permute-start | bytes 3145736 | tf_op jit(solution)/shard_map/ppermute | solution.py:61
  444.5 43.5 %collective-permute-start.20 = (bf16[256,2048]{1,0:T(8,128)(2,1)S(1)}, bf16[256,2048]{1,0:T(8,128)(2,1)S(1)}, u32[]{:S(2)}, u32[]{:S(2)}) collective-permute-start(bf16[256,2048]{1,0:T(8,128)(2,1)S(1)} %copy-done.14), channel_id=1, source_target_pairs={{0,1},{1,2},{2,3},{3,0},{4,5},{5,6},{6,7},{7,4},{8,9},{9,10},{10,1... | collective-permute-start | bytes 3145736 | tf_op jit(solution)/shard_map/ppermute | solution.py:61
  455.1 33.0 %copy-start.17 = (bf16[256,2048]{1,0:T(8,128)(2,1)S(1)}, bf16[256,2048]{1,0:T(8,128)(2,1)}, u32[]{:S(2)}) copy-start(bf16[256,2048]{1,0:T(8,128)(2,1)} %get-tuple-element.157) | copy-start | bytes 3145732
  465.2 23.3 %copy-start.19 = (f32[2048,128]{1,0:T(8,128)S(1)}, f32[2048,128]{1,0:T(8,128)}, u32[]{:S(2)}) copy-start(f32[2048,128]{1,0:T(8,128)} %get-tuple-element.166) | copy-start | bytes 3145732
  488.5 25.4 %copy-start.12 = (bf16[256,2048]{1,0:T(8,128)(2,1)S(1)}, bf16[256,2048]{1,0:T(8,128)(2,1)}, u32[]{:S(2)}) copy-start(bf16[256,2048]{1,0:T(8,128)(2,1)} %get-tuple-element.171) | copy-start | bytes 3145732
  488.9 25.0 %collective-permute-start.25 = (bf16[256,2048]{1,0:T(8,128)(2,1)S(1)}, bf16[256,2048]{1,0:T(8,128)(2,1)}, u32[]{:S(2)}, u32[]{:S(2)}) collective-permute-start(bf16[256,2048]{1,0:T(8,128)(2,1)S(1)} %add_convert_fusion.2), channel_id=1, source_target_pairs={{0,1},{1,2},{2,3},{3,0},{4,5},{5,6},{6,7},{7,4},{8,9},{9,10},{10,1... | collective-permute-start | bytes 3145736 | tf_op jit(solution)/shard_map/ppermute | solution.py:61
  489.2 22.4 %collective-permute-start.23 = (f32[2560]{0:T(1024)S(1)}, f32[2560]{0:T(1024)S(1)}, u32[]{:S(2)}, u32[]{:S(2)}) collective-permute-start(f32[2560]{0:T(1024)S(1)} %pad_maximum_fusion.2), channel_id=1, source_target_pairs={{0,2},{1,3},{2,0},{3,1},{4,6},{5,7},{6,4},{7,5},{8,10},{9,11},{10,... | collective-permute-start | bytes 30728 | tf_op jit(solution)/shard_map/ppermute | solution.py:61
  491.2 20.3 %collective-permute-start.24 = (f32[2560]{0:T(1024)S(1)}, f32[2560]{0:T(1024)S(1)}, u32[]{:S(2)}, u32[]{:S(2)}) collective-permute-start(f32[2560]{0:T(1024)S(1)} %pad_maximum_fusion.2), channel_id=1, source_target_pairs={{0,3},{1,0},{2,1},{3,2},{4,7},{5,4},{6,5},{7,6},{8,11},{9,8},{10,9... | collective-permute-start | bytes 30728 | tf_op jit(solution)/shard_map/ppermute | solution.py:61
  493.0 18.5 %collective-permute-start.22 = (f32[2560]{0:T(1024)S(1)}, f32[2560]{0:T(1024)S(1)}, u32[]{:S(2)}, u32[]{:S(2)}) collective-permute-start(f32[2560]{0:T(1024)S(1)} %pad_maximum_fusion.2), channel_id=1, source_target_pairs={{0,1},{1,2},{2,3},{3,0},{4,5},{5,6},{6,7},{7,4},{8,9},{9,10},{10,1... | collective-permute-start | bytes 30728 | tf_op jit(solution)/shard_map/ppermute | solution.py:61
  516.5 28.3 %collective-permute-start.26 = (bf16[256,2048]{1,0:T(8,128)(2,1)}, bf16[256,2048]{1,0:T(8,128)(2,1)S(1)}, u32[]{:S(2)}, u32[]{:S(2)}) collective-permute-start(bf16[256,2048]{1,0:T(8,128)(2,1)} %add_convert_fusion), channel_id=1, source_target_pairs={{0,1},{1,2},{2,3},{3,0},{4,5},{5,6},{6,7},{7,4},{8,9},{9,10},{10,1... | collective-permute-start | bytes 3145736 | tf_op jit(solution)/shard_map/ppermute | solution.py:61
  525.5 19.3 %copy-start.2 = (bf16[256,2048]{1,0:T(8,128)(2,1)S(1)}, bf16[256,2048]{1,0:T(8,128)(2,1)}, u32[]{:S(2)}) copy-start(bf16[256,2048]{1,0:T(8,128)(2,1)} %own.3) | copy-start | bytes 3145732
  525.5 19.3 %copy-start.5 = (bf16[256,2048]{1,0:T(8,128)(2,1)S(1)}, bf16[256,2048]{1,0:T(8,128)(2,1)}, u32[]{:S(2)}) copy-start(bf16[256,2048]{1,0:T(8,128)(2,1)} %get-tuple-element.175) | copy-start | bytes 3145732
  526.2 19.4 %copy-start.10 = (f32[256,2048]{1,0:T(8,128)S(1)}, f32[256,2048]{1,0:T(8,128)}, u32[]{:S(2)}) copy-start(f32[256,2048]{1,0:T(8,128)} %get-tuple-element.174) | copy-start | bytes 6291460
  526.2 21.4 %collective-permute-start.27 = (bf16[256,512]{1,0:T(8,128)(2,1)S(1)}, bf16[256,512]{1,0:T(8,128)(2,1)S(1)}, u32[]{:S(2)}, u32[]{:S(2)}) collective-permute-start(bf16[256,512]{1,0:T(8,128)(2,1)S(1)} %get-tuple-element.231), channel_id=1, source_target_pairs={{0,3},{1,0},{2,1},{3,2},{4,7},{5,4},{6,5},{7,6},{8,11},{9,8},{10,9... | collective-permute-start | bytes 786440 | tf_op jit(solution)/shard_map/ppermute | solution.py:61
  528.8 24.5 %collective-permute-start.29 = (bf16[256,512]{1,0:T(8,128)(2,1)S(1)}, bf16[256,512]{1,0:T(8,128)(2,1)S(1)}, u32[]{:S(2)}, u32[]{:S(2)}) collective-permute-start(bf16[256,512]{1,0:T(8,128)(2,1)S(1)} %get-tuple-element.232), channel_id=1, source_target_pairs={{0,1},{1,2},{2,3},{3,0},{4,5},{5,6},{6,7},{7,4},{8,9},{9,10},{10,1... | collective-permute-start | bytes 786440 | tf_op jit(solution)/shard_map/ppermute | solution.py:61
  528.8 32.9 %collective-permute-start.28 = (bf16[256,512]{1,0:T(8,128)(2,1)S(1)}, bf16[256,512]{1,0:T(8,128)(2,1)S(1)}, u32[]{:S(2)}, u32[]{:S(2)}) collective-permute-start(bf16[256,512]{1,0:T(8,128)(2,1)S(1)} %get-tuple-element.233), channel_id=1, source_target_pairs={{0,2},{1,3},{2,0},{3,1},{4,6},{5,7},{6,4},{7,5},{8,10},{9,11},{10,... | collective-permute-start | bytes 786440 | tf_op jit(solution)/shard_map/ppermute | solution.py:61
  (25 other events, 106.3 us)
Sparse Core Ops, SparseCore 0:
  12.6 41.6 all-gather.3
  85.8 105.8 all-gather.5
  193.6 45.5 all-gather.7
  266.3 63.2 reduce-scatter.4
  344.6 92.5 reduce-scatter.6
  440.9 71.2 reduce-scatter.8
  516.6 52.9 reduce-scatter.10

commit v4 on v3

--- a/solution.py
+++ b/solution.py
@@ -201,37 +201,59 @@
     )(place, qkv, qkv, qkv)
 
 
-def mix_kernel(own, below, far, above, c0, c1, c2, c3, wa, wb, gain, normed, hidden, ctx_rows, x_s, c_s):
-    i = pl.program_id(0)
-    size = own.shape[0]
+def mix_kernel(own, below, far, above, c0, c1, c2, c3, wa, wb, gain, normed, hidden, ctx_rows, acc, c_s):
+    n = pl.program_id(0)
+    size, tile = own.shape
     inner = c0.shape[1]
-    pick_slot(i, (own, below, far, above), x_s)
-    for k, ref in enumerate((c0, c1, c2, c3)):
-        start = pl.multiple_of(lax.rem(i + WAYS - k, WAYS) * size, size)
-        c_s[:, k * inner : (k + 1) * inner] = ref[pl.ds(start, size), :]
     wide = wa.shape[1]
-    h = x_s[...].astype(f32) + nt(c_s[:, :wide], wa[...]) + nt(c_s[:, wide:], wb[...])
-    normed[...] = (h * rms_scale(h) * gain[...]).astype(bf16)
-
-    @pl.when(i == 0)
+    tiles = acc.shape[0]
+
+    @pl.when(n == 0)
     def _():
-        hidden[...] = h
-        ctx_rows[...] = c_s[...]
+        for k, ref in enumerate((c0, c1, c2, c3)):
+            for i in range(WAYS):
+                source = (i - k) % WAYS
+                c_s[i * size : (i + 1) * size, k * inner : (k + 1) * inner] = ref[
+                    source * size : (source + 1) * size
+                ]
+        ctx_rows[...] = c_s[:size]
+
+    for i, x in enumerate((own, below, far, above)):
+        rows = slice(i * size, (i + 1) * size)
+        acc[n, rows] = (
+            x[...].astype(f32) + nt(c_s[rows, :wide], wa[...]) + nt(c_s[rows, wide:], wb[...])
+        )
+
+    @pl.when(n == tiles - 1)
+    def _():
+        for i in range(WAYS):
+            rows = slice(i * size, (i + 1) * size)
+            squares = sum(
+                jnp.sum(acc[m, rows] * acc[m, rows], axis=-1, keepdims=True) for m in range(tiles)
+            )
+            scale = lax.rsqrt(squares / (tiles * tile) + norm_eps)
+            for m in range(tiles):
+                cols = slice(m * tile, (m + 1) * tile)
+                normed[rows, cols] = (acc[m, rows] * scale * gain[:, cols]).astype(bf16)
+                if i == 0:
+                    hidden[:, cols] = acc[m, rows]
 
 
 def mix(x_slots, contexts, weights, gain):
     size, width = x_slots[0].shape
     rows, inner = contexts[0].shape
     cols = WAYS * inner
+    tile = 512
     return call(
         mix_kernel,
-        (WAYS,),
-        [whole(x.shape) for x in x_slots]
+        (width // tile,),
+        [pl.BlockSpec((size, tile), lambda n: (0, n)) for _ in x_slots]
         + [whole(c.shape) for c in contexts]
-        + [whole((width, cols // 2), (0, 3)), whole((width, cols // 2), (0, 4)), whole(gain.shape)],
+        + [pl.BlockSpec((tile, cols // 2), lambda n: (n, 3))]
+        + [pl.BlockSpec((tile, cols // 2), lambda n: (n, 4)), whole(gain.shape)],
         [((rows, width), bf16), ((size, width), f32), ((size, cols), bf16)],
-        [pl.BlockSpec((size, width), lambda i: (i, 0)), whole((size, width)), whole((size, cols))],
-        [pltpu.VMEM((size, width), bf16), pltpu.VMEM((size, cols), bf16)],
+        [whole((rows, width)), whole((size, width)), whole((size, cols))],
+        [pltpu.VMEM((width // tile, rows, tile), f32), pltpu.VMEM((rows, cols), bf16)],
         flops=2 * rows * width * cols,
         size=24 << 20,
     )(*x_slots, *contexts, weights, weights, gain)
@@ -279,7 +301,7 @@
 def feed_back(d_branch, w_down, forward):
     rows, width = d_branch.shape
     ff_width = forward.shape[2]
-    tile = 256
+    tile = 512
     return call(
         feed_back_kernel,
         (ff_width // tile,),
@@ -645,10 +667,9 @@
     d_hidden, d_attended, p0, p1, p2, p3 = branch(
         (b0, b_sum), hidden, cotangent, own_live, norm_ffn_all, rest_full, q_width
     )
-    p1, p2, p3, y_sum = together(p1, p2, p3, y_sum)
     grads_out = row_grads(d_attended, ctx_rows[None], 0, 1)
-    s1, s2, s3, grads_out = together(
-        shift_by(p3, 1), shift_by(p2, 2), shift_by(p1, -1), grads_out
+    s1, s2, s3, grads_out, y_sum = together(
+        shift_by(p3, 1), shift_by(p2, 2), shift_by(p1, -1), grads_out, y_sum
     )
     d_q, d_k, d_v, sum_q, sum_k = attend_back(
         place_ref, qkv, [p0, s1, s2, s3], log_total, pre, cos, sin, gain_q, gain_k

time: 593 us -> 595 us (level)
  waiting for transfers between devices: 262 us -> 280 us
  starting transfers between devices: 40.3 us -> 28.3 us
    ppermute x30, waiting for transfers between devices: 255 us -> 270 us  [shift_by(): lax.ppermute(value, 'tensor', [(i, (i + step) % WAYS) for i in range(WAYS)])]
    ppermute x30, starting transfers between devices: 40 us -> 28 us  [shift_by(): lax.ppermute(value, 'tensor', [(i, (i + step) % WAYS) for i in range(WAYS)])]
    reduce_scatter x1, waiting for transfers between devices: 0.01 us -> 7.91 us  [local(): lax.psum_scatter(grads_feed, 'dp', scatter_dimension=0, tiled=True)]
  transfers between devices with their start and end apart: 37 -> 37, of which waited for: 20 -> 23; matrix products, arithmetic and copies ran while one was open for 9% -> 9% of each run, Pallas kernels for 34% -> 34%
where the time goes in v4:
time: 595 us; the launch traced here: 586 us
  waiting for transfers between devices  280 us (47%)
  Pallas kernels  197 us (33%)
  other arithmetic  32.7 us (5%)
  local copies, waits for them, and re-layouts  32 us (5%)
  starting transfers between devices  28.3 us (5%)
  between operations  15 us (3%)
    ppermute x30, waiting for transfers between devices, shift_by(): lax.ppermute(value, 'tensor', [(i, (i + step) % WAYS) for i in range(WAYS)])  270 us
    pallas_call x3, Pallas kernels, row_grads(): call(grads_kernel, (width // tile,), [pl.BlockSpec((rows, tile), lambda j...  36 us
    ppermute x30, starting transfers between devices, shift_by(): lax.ppermute(value, 'tensor', [(i, (i + step) % WAYS) for i in range(WAYS)])  28 us
    pallas_call x2, Pallas kernels, back_feed(): call(functools.partial(back_kernel, slots, size, lone), (width // tile,),...  24.5 us
    pallas_call x1, Pallas kernels, feed(): call(feed_kernel, (tiles,), [whole((rows, width)), col(0), col(1)], [((3,...  19.7 us
    pallas_call x1, Pallas kernels, attend_back(): call(attend_back_kernel, (2,), [pl.BlockSpec(memory_space=pltpu.SMEM), co...  18.1 us
    pallas_call x1, Pallas kernels, mix(): call(mix_kernel, (width // tile,), [pl.BlockSpec((size, tile), lambda n:...  18 us
    unnamed x84, local copies, waits for them, and re-layouts  17.4 us
  transfers between devices with their start and end apart: 37, of which 23 were waited for; matrix products, arithmetic and copies ran while one was open for 9% of the time, Pallas kernels for 34%

profile of v4, /device:TPU:0, one launch (start us, length us, event | category | flops | bytes accessed | tf_op | source)
XLA Modules:
  0.0 585.6 jit_solution(10643548486951032174)
XLA Ops:
  10.5 2.0 concatenate.36
  12.7 5.1 collective-permute-start.2
  22.5 1.9 fusion.8
  24.5 6.6 %collective-permute-done.1 = bf16[256,512]{1,0:T(8,128)(2,1)} collective-permute-done((bf16[256,512]{1,0:T(8,128)(2,1)S(1)}, bf16[256,512]{1,0:T(8,128)(2,1)}, u32[]{:S(2)}, u32[]{:S(2)}) %collective-permute-start.1) | collective-permute-done | bytes 262176 | tf_op jit(solution)/shard_map/ppermute | solution.py:61
  31.1 21.3 %collective-permute-done.below = bf16[256,2048]{1,0:T(8,128)(2,1)} collective-permute-done((bf16[256,2048]{1,0:T(8,128)(2,1)S(1)}, bf16[256,2048]{1,0:T(8,128)(2,1)}, u32[]{:S(2)}, u32[]{:S(2)}) %collective-permute-start) | collective-permute-done | bytes 1048608 | tf_op jit(solution)/shard_map/ppermute | solution.py:61
  58.9 25.2 %collective-permute-done.4 = bf16[256,512]{1,0:T(8,128)(2,1)S(1)} collective-permute-done((bf16[256,512]{1,0:T(8,128)(2,1)}, bf16[256,512]{1,0:T(8,128)(2,1)S(1)}, u32[]{:S(2)}, u32[]{:S(2)}) %collective-permute-start.4) | collective-permute-done | bytes 262176 | tf_op jit(solution)/shard_map/ppermute | solution.py:61
  87.0 25.0 %collective-permute-done.5.above = bf16[256,2048]{1,0:T(8,128)(2,1)} collective-permute-done((bf16[256,2048]{1,0:T(8,128)(2,1)S(1)}, bf16[256,2048]{1,0:T(8,128)(2,1)}, u32[]{:S(2)}, u32[]{:S(2)}) %collective-permute-start.5) | collective-permute-done | bytes 1048608 | tf_op jit(solution)/shard_map/ppermute | solution.py:61
  116.0 11.9 %shard_map.246 = (bf16[1024,2048]{1,0:T(8,128)(2,1)}, bf16[1024,1024]{1,0:T(8,128)(2,1)}, f32[1024,768]{1,0:T(8,128)}) custom-call(bf16[256,2048]{1,0:T(8,128)(2,1)} %own.3, bf16[256,2048]{1,0:T(8,128)(2,1)} %collective-permute-done.below, bf16[256,2048]{1,0:T(8,128)(2,1)} %copy-done.20, bf16[256,2048]{1,0:T(8,128)(2,1)} %collective-permute-done.5.above, ...), custom_call_target="tpu_custom_call" | custom-call | flops 4294967296 | bytes 20971520 | tf_op jit(solution)/shard_map/pallas_call | solution.py:126
  128.0 10.3 %shard_map.247 = (bf16[1024,512]{1,0:T(8,128)(2,1)}, f32[1024,256]{1,0:T(8,128)}) custom-call(s32[1]{0:T(128)} %bitcast.2.place, bf16[1024,1024]{1,0:T(8,128)(2,1)} %get-tuple-element.102.q.k.v, bf16[1024,1024]{1,0:T(8,128)(2,1)} %get-tuple-element.102.q.k.v, bf16[1024,1024]{1,0:T(8,128)(2,1)} %get-tuple-element.102.q.k.v), custom_call_target="tpu_custom_call" | custom-call | flops 1073741824 | bytes 2097152 | tf_op jit(solution)/shard_map/pallas_call | solution.py:184
  138.3 24.2 %collective-permute-done.7.c1 = bf16[1024,512]{1,0:T(8,128)(2,1)S(1)} collective-permute-done((bf16[1024,512]{1,0:T(8,128)(2,1)}, bf16[1024,512]{1,0:T(8,128)(2,1)S(1)}, u32[]{:S(2)}, u32[]{:S(2)}) %collective-permute-start.7) | collective-permute-done | bytes 1048608 | tf_op jit(solution)/shard_map/ppermute | solution.py:61
  163.4 23.3 %collective-permute-done.8.c2 = bf16[1024,512]{1,0:T(8,128)(2,1)S(1)} collective-permute-done((bf16[1024,512]{1,0:T(8,128)(2,1)S(1)}, bf16[1024,512]{1,0:T(8,128)(2,1)S(1)}, u32[]{:S(2)}, u32[]{:S(2)}) %collective-permute-start.8) | collective-permute-done | bytes 1048608 | tf_op jit(solution)/shard_map/ppermute | solution.py:61
  188.1 20.9 %collective-permute-done.9.c3 = bf16[1024,512]{1,0:T(8,128)(2,1)S(1)} collective-permute-done((bf16[1024,512]{1,0:T(8,128)(2,1)S(1)}, bf16[1024,512]{1,0:T(8,128)(2,1)S(1)}, u32[]{:S(2)}, u32[]{:S(2)}) %collective-permute-start.9) | collective-permute-done | bytes 1048608 | tf_op jit(solution)/shard_map/ppermute | solution.py:61
  211.2 18.0 %shard_map.248 = (bf16[1024,2048]{1,0:T(8,128)(2,1)}, f32[256,2048]{1,0:T(8,128)}, bf16[256,2048]{1,0:T(8,128)(2,1)}) custom-call(bf16[256,2048]{1,0:T(8,128)(2,1)} %own.3, bf16[256,2048]{1,0:T(8,128)(2,1)} %collective-permute-done.below, bf16[256,2048]{1,0:T(8,128)(2,1)} %copy-done.20, bf16[256,2048]{1,0:T(8,128)(2,1)} %collective-permute-done.5.above, ...), custom_call_target="tpu_custom_call" | custom-call | flops 8589934592 | bytes 25165824 | tf_op jit(solution)/shard_map/pallas_call | solution.py:247
  229.2 4.3 collective-permute-done.10
  234.5 19.7 %shard_map.249.a.slopes = bf16[3,1024,1536]{2,1,0:T(8,128)(2,1)} custom-call(bf16[1024,2048]{1,0:T(8,128)(2,1)} %get-tuple-element.113.n, bf16[2048,5120]{1,0:T(8,128)(2,1)} %all-gather.6.cloned.1.call-done.wa.wb.w_gate.w_up.w, bf16[2048,5120]{1,0:T(8,128)(2,1)} %all-gather.6.cloned.1.call-done.wa.wb.w_gate.w_up.w), custom_call_target="tpu_custom_call" | custom-call | flops 12884901888 | bytes 27262976 | tf_op jit(solution)/shard_map/pallas_call | solution.py:280
  255.3 10.7 %shard_map.250 = bf16[2048,1536]{1,0:T(8,128)(2,1)} custom-call(bf16[1024,2048]{1,0:T(8,128)(2,1)} %constant_dynamic-update-slice_fusion.6.n.d, bf16[3,1024,1536]{2,1,0:T(8,128)(2,1)} %shard_map.249.a.slopes), custom_call_target="tpu_custom_call" | custom-call | flops 6442450944 | bytes 13631488 | tf_op jit(solution)/shard_map/pallas_call | solution.py:387
  266.2 10.6 %shard_map.251 = (bf16[256,2048]{1,0:T(8,128)(2,1)}, bf16[256,2048]{1,0:T(8,128)(2,1)}, bf16[256,2048]{1,0:T(8,128)(2,1)}, bf16[256,2048]{1,0:T(8,128)(2,1)}) custom-call(bf16[3,1024,1536]{2,1,0:T(8,128)(2,1)} %shard_map.249.a.slopes, bf16[2048,1536]{1,0:T(8,128)(2,1)} %all-gather.8.cloned.1.call-done.wa.w_down), custom_call_target="tpu_custom_call" | custom-call | flops 6442450944 | bytes 14680064 | tf_op jit(solution)/shard_map/pallas_call | solution.py:365
  276.8 14.0 %shard_map.252.a.b = bf16[2,1024,1536]{2,1,0:T(8,128)(2,1)} custom-call(bf16[1024,2048]{1,0:T(8,128)(2,1)} %constant_dynamic-update-slice_fusion.6.n.d, bf16[2048,1536]{1,0:T(8,128)(2,1)} %all-gather.8.cloned.1.call-done.wa.w_down, bf16[3,1024,1536]{2,1,0:T(8,128)(2,1)} %shard_map.249.a.slopes), custom_call_target="tpu_custom_call" | custom-call | flops 6442450944 | bytes 23068672 | tf_op jit(solution)/shard_map/pallas_call | solution.py:305
  290.8 9.3 %shard_map.254 = bf16[256,2048]{1,0:T(8,128)(2,1)} custom-call(bf16[2,1024,1536]{2,1,0:T(8,128)(2,1)} %shard_map.252.a.b, bf16[2,1024,1536]{2,1,0:T(8,128)(2,1)} %shard_map.252.a.b, bf16[2048,5120]{1,0:T(8,128)(2,1)} %all-gather.6.cloned.1.call-done.wa.wb.w_gate.w_up.w, bf16[2048,5120]{1,0:T(8,128)(2,1)} %all-gather.6.cloned.1.call-done.wa.wb.w_gate.w_up.w), custom_call_target="tpu_custom_call" | custom-call | flops 3221225472 | bytes 20971520 | tf_op jit(solution)/shard_map/pallas_call | solution.py:339
  301.7 15.2 %shard_map.253 = (bf16[256,2048]{1,0:T(8,128)(2,1)}, bf16[256,2048]{1,0:T(8,128)(2,1)}, bf16[256,2048]{1,0:T(8,128)(2,1)}) custom-call(bf16[2,1024,1536]{2,1,0:T(8,128)(2,1)} %shard_map.252.a.b, bf16[2,1024,1536]{2,1,0:T(8,128)(2,1)} %shard_map.252.a.b, bf16[2048,5120]{1,0:T(8,128)(2,1)} %all-gather.6.cloned.1.call-done.wa.wb.w_gate.w_up.w, ...), custom_call_target="tpu_custom_call" | custom-call | flops 9663676416 | bytes 20971520 | tf_op jit(solution)/shard_map/pallas_call | solution.py:339
  316.9 5.5 collective-permute-done.13
  325.0 18.7 %shard_map.255 = bf16[2048,3072]{1,0:T(8,128)(2,1)} custom-call(bf16[1024,2048]{1,0:T(8,128)(2,1)} %get-tuple-element.113.n, bf16[2,1024,1536]{2,1,0:T(8,128)(2,1)} %shard_map.252.a.b), custom_call_target="tpu_custom_call" | custom-call | flops 12884901888 | bytes 23068672 | tf_op jit(solution)/shard_map/pallas_call | solution.py:387
  343.6 1.9 collective-permute-done.14
  348.3 22.2 %collective-permute-done.15.arrived = bf16[256,2048]{1,0:T(8,128)(2,1)S(1)} collective-permute-done((bf16[256,2048]{1,0:T(8,128)(2,1)S(1)}, bf16[256,2048]{1,0:T(8,128)(2,1)S(1)}, u32[]{:S(2)}, u32[]{:S(2)}) %collective-permute-start.15) | collective-permute-done | bytes 1048608 | tf_op jit(solution)/shard_map/ppermute | solution.py:61
  372.9 11.4 %shard_map.256 = (f32[256,2048]{1,0:T(8,128)}, bf16[256,2048]{1,0:T(8,128)(2,1)}, bf16[256,512]{1,0:T(8,128)(2,1)}, bf16[256,512]{1,0:T(8,128)(2,1)}, bf16[256,5...) custom-call(bf16[256,2048]{1,0:T(8,128)(2,1)} %get-tuple-element.120.own, bf16[256,2048]{1,0:T(8,128)(2,1)} %copy-done.16, ...), custom_call_target="tpu_custom_call" | custom-call | flops 2147483648 | bytes 16777216 | tf_op jit(solution)/shard_map/pallas_call | solution.py:424
  384.4 1.9 collective-permute-start.16
  386.3 1.8 collective-permute-start.17
  389.1 6.6 %shard_map.257 = bf16[2048,2048]{1,0:T(8,128)(2,1)} custom-call(bf16[256,2048]{1,0:T(8,128)(2,1)} %get-tuple-element.134.n, bf16[1,256,2048]{2,1,0:T(8,128)(2,1)} %bitcast.30), custom_call_target="tpu_custom_call" | custom-call | flops 2147483648 | bytes 13631488 | tf_op jit(solution)/shard_map/pallas_call | solution.py:387
  395.7 2.2 collective-permute-done.16.d1
  397.9 8.3 %collective-permute-done.17.d2 = bf16[256,512]{1,0:T(8,128)(2,1)S(1)} collective-permute-done((bf16[256,512]{1,0:T(8,128)(2,1)}, bf16[256,512]{1,0:T(8,128)(2,1)S(1)}, u32[]{:S(2)}, u32[]{:S(2)}) %collective-permute-start.17) | collective-permute-done | bytes 262176 | tf_op jit(solution)/shard_map/ppermute | solution.py:61
  407.0 18.1 %shard_map.258 = (bf16[1024,512]{1,0:T(8,128)(2,1)}, bf16[1024,256]{1,0:T(8,128)(2,1)}, bf16[1024,256]{1,0:T(8,128)(2,1)}, f32[8,256]{1,0:T(8,128)}, f32[8,256]{1,0:T(8,128)}) custom-call(s32[1]{0:T(128)} %bitcast.2.place, bf16[1024,1024]{1,0:T(8,128)(2,1)} %get-tuple-element.102.q.k.v, bf16[1024,1024]{1,0:T(8,128)(2,1)} %get-tuple-element.102.q.k.v, ...), custom_call_target="tpu_custom_call" | custom-call | flops 5368709120 | bytes 12582912 | tf_op jit(solution)/shard_map/pallas_call | solution.py:491
  425.1 5.0 shard_map.259
  430.1 7.9 %reduce-scatter.7.cloned.1.call-done = bf16[256,3072]{1,0:T(8,128)(2,1)} async-done(((bf16[2048,3072]{1,0:T(8,128)(2,1)}), bf16[256,3072]{1,0:T(8,128)(2,1)}) %reduce-scatter.7.cloned.1.call-update) | async-done | bytes 1572880 | tf_op jit(solution)/shard_map/reduce_scatter | solution.py:663
  443.9 7.2 %shard_map.260 = (bf16[256,2048]{1,0:T(8,128)(2,1)}, bf16[256,2048]{1,0:T(8,128)(2,1)}, bf16[256,2048]{1,0:T(8,128)(2,1)}) custom-call(bf16[1024,512]{1,0:T(8,128)(2,1)} %get-tuple-element.150.q, bf16[1024,256]{1,0:T(8,128)(2,1)} %get-tuple-element.144.k, bf16[1024,256]{1,0:T(8,128)(2,1)} %get-tuple-element.145.v, ...), custom_call_target="tpu_custom_call" | custom-call | flops 3221225472 | bytes 10485760 | tf_op jit(solution)/shard_map/pallas_call | solution.py:528
  451.2 2.6 fusion.15
  453.7 10.5 %shard_map.261 = (bf16[2048,1152]{1,0:T(8,128)(2,1)}, f32[2048,128]{1,0:T(8,128)}) custom-call(bf16[1024,2048]{1,0:T(8,128)(2,1)} %get-tuple-element.153.n, bf16[1024,512]{1,0:T(8,128)(2,1)} %get-tuple-element.150.q, bf16[1024,256]{1,0:T(8,128)(2,1)} %get-tuple-element.144.k, bf16[1024,256]{1,0:T(8,128)(2,1)} %get-tuple-element.145.v, ...), custom_call_target="tpu_custom_call" | custom-call | flops 4294967296 | bytes 16777216 | tf_op jit(solution)/shard_map/pallas_call | solution.py:558
  464.2 24.6 %collective-permute-done.20 = bf16[256,2048]{1,0:T(8,128)(2,1)S(1)} collective-permute-done((bf16[256,2048]{1,0:T(8,128)(2,1)S(1)}, bf16[256,2048]{1,0:T(8,128)(2,1)S(1)}, u32[]{:S(2)}, u32[]{:S(2)}) %collective-permute-start.20) | collective-permute-done | bytes 1048608 | tf_op jit(solution)/shard_map/ppermute | solution.py:61
  489.9 2.1 collective-permute-start.23
  494.4 21.9 %collective-permute-done.23 = f32[2560]{0:T(1024)S(1)} collective-permute-done((f32[2560]{0:T(1024)S(1)}, f32[2560]{0:T(1024)S(1)}, u32[]{:S(2)}, u32[]{:S(2)}) %collective-permute-start.23) | collective-permute-done | bytes 10272 | tf_op jit(solution)/shard_map/ppermute | solution.py:61
  518.9 2.6 add_convert_fusion
  524.0 3.2 copy.62
  527.2 3.3 multiply_convert_fusion
  531.2 3.0 collective-permute-start.27
  534.9 14.9 %collective-permute-done.26 = bf16[256,2048]{1,0:T(8,128)(2,1)S(1)} collective-permute-done((bf16[256,2048]{1,0:T(8,128)(2,1)}, bf16[256,2048]{1,0:T(8,128)(2,1)S(1)}, u32[]{:S(2)}, u32[]{:S(2)}) %collective-permute-start.26) | collective-permute-done | bytes 1048608 | tf_op jit(solution)/shard_map/ppermute | solution.py:61
  552.3 3.0 collective-permute-done.27
  555.2 5.6 collective-permute-done.29
  560.8 8.4 %collective-permute-done.28 = bf16[256,512]{1,0:T(8,128)(2,1)S(1)} collective-permute-done((bf16[256,512]{1,0:T(8,128)(2,1)S(1)}, bf16[256,512]{1,0:T(8,128)(2,1)S(1)}, u32[]{:S(2)}, u32[]{:S(2)}) %collective-permute-start.28) | collective-permute-done | bytes 262176 | tf_op jit(solution)/shard_map/ppermute | solution.py:61
  570.4 2.5 reduce-scatter.11.cloned.1.call-done
  (198 shorter events, 64.0 us)
Async XLA Ops:
  7.2 13.3 %copy-start.6 = (bf16[256,1536]{1,0:T(8,128)(2,1)S(1)}, bf16[256,1536]{1,0:T(8,128)(2,1)}, u32[]{:S(2)}) copy-start(bf16[256,1536]{1,0:T(8,128)(2,1)} %param.24) | copy-start | bytes 2359300
  7.2 104.8 %all-gather.4.cloned.1.call-start = ((), (), s32[]{:S(2)}) async-start(), calls=%async_computation.4 | async-start | bytes 5308416 | tf_op jit(solution)/shard_map/all_gather | solution.py:619
  12.5 198.7 %all-gather.6.cloned.1.call-start = ((), (), s32[]{:S(2)}) async-start(), calls=%async_computation.5 | async-start | bytes 23592960 | tf_op jit(solution)/shard_map/all_gather | solution.py:627
  12.7 11.8 %collective-permute-start.2 = (bf16[256,512]{1,0:T(8,128)(2,1)S(1)}, bf16[256,512]{1,0:T(8,128)(2,1)S(1)}, u32[]{:S(2)}, u32[]{:S(2)}) collective-permute-start(bf16[256,512]{1,0:T(8,128)(2,1)S(1)} %bitcast.31), channel_id=1, source_target_pairs={{0,3},{1,0},{2,1},{3,2},{4,7},{5,4},{6,5},{7,6},{8,11},{9,8},{10,9... | collective-permute-start | bytes 786440 | tf_op jit(solution)/shard_map/ppermute | solution.py:61
  17.8 13.3 %collective-permute-start.1 = (bf16[256,512]{1,0:T(8,128)(2,1)S(1)}, bf16[256,512]{1,0:T(8,128)(2,1)}, u32[]{:S(2)}, u32[]{:S(2)}) collective-permute-start(bf16[256,512]{1,0:T(8,128)(2,1)S(1)} %bitcast.32), channel_id=1, source_target_pairs={{0,1},{1,2},{2,3},{3,0},{4,5},{5,6},{6,7},{7,4},{8,9},{9,10},{10,1... | collective-permute-start | bytes 786440 | tf_op jit(solution)/shard_map/ppermute | solution.py:61
  17.8 34.7 %collective-permute-start = (bf16[256,2048]{1,0:T(8,128)(2,1)S(1)}, bf16[256,2048]{1,0:T(8,128)(2,1)}, u32[]{:S(2)}, u32[]{:S(2)}) collective-permute-start(bf16[256,2048]{1,0:T(8,128)(2,1)S(1)} %copy-done.1), channel_id=1, source_target_pairs={{0,1},{1,2},{2,3},{3,0},{4,5},{5,6},{6,7},{7,4},{8,9},{9,10},{10,1... | collective-permute-start | bytes 3145736 | tf_op jit(solution)/shard_map/ppermute | solution.py:61
  20.4 34.4 %copy-start.28 = (f32[256]{0:T(256)}, f32[256]{0:T(256)S(1)}, u32[]{:S(2)}) copy-start(f32[256]{0:T(256)S(1)} %compare_convert_fusion) | copy-start | bytes 3076
  21.5 33.3 %copy-start.4 = (bf16[256,2048]{1,0:T(8,128)(2,1)S(1)}, bf16[256,2048]{1,0:T(8,128)(2,1)}, u32[]{:S(2)}) copy-start(bf16[256,2048]{1,0:T(8,128)(2,1)} %cotangent.1) | copy-start | bytes 3145732
  52.5 31.7 %collective-permute-start.3 = (bf16[256,2048]{1,0:T(8,128)(2,1)}, bf16[256,2048]{1,0:T(8,128)(2,1)S(1)}, u32[]{:S(2)}, u32[]{:S(2)}) collective-permute-start(bf16[256,2048]{1,0:T(8,128)(2,1)} %collective-permute-done.below), channel_id=1, source_target_pairs={{0,1},{1,2},{2,3},{3,0},{4,5},{5,6},{6,7},{7,4},{8,9},{9,10},{10,1... | collective-permute-start | bytes 3145736 | tf_op jit(solution)/shard_map/ppermute | solution.py:61
  55.1 29.1 %collective-permute-start.4 = (bf16[256,512]{1,0:T(8,128)(2,1)}, bf16[256,512]{1,0:T(8,128)(2,1)S(1)}, u32[]{:S(2)}, u32[]{:S(2)}) collective-permute-start(bf16[256,512]{1,0:T(8,128)(2,1)} %collective-permute-done.1), channel_id=1, source_target_pairs={{0,1},{1,2},{2,3},{3,0},{4,5},{5,6},{6,7},{7,4},{8,9},{9,10},{10,1... | collective-permute-start | bytes 786440 | tf_op jit(solution)/shard_map/ppermute | solution.py:61
  57.1 28.6 %copy-start.24 = (bf16[1536,256]{1,0:T(8,128)(2,1)S(1)}, bf16[1536,256]{1,0:T(8,128)(2,1)}, u32[]{:S(2)}) copy-start(bf16[1536,256]{1,0:T(8,128)(2,1)} %param.26) | copy-start | bytes 2359300
  85.7 180.5 %all-gather.8.cloned.1.call-start = ((), (), s32[]{:S(2)}) async-start(), calls=%async_computation.6 | async-start | bytes 7077888 | tf_op jit(solution)/shard_map/all_gather | solution.py:632
  86.9 258.7 %reduce-scatter.5.cloned.1.call-start = ((), (), s32[]{:S(2)}) async-start(), calls=%async_computation.7 | async-start | bytes 7077888 | tf_op jit(solution)/shard_map/reduce_scatter | solution.py:649
  87.0 25.1 %collective-permute-start.5 = (bf16[256,2048]{1,0:T(8,128)(2,1)S(1)}, bf16[256,2048]{1,0:T(8,128)(2,1)}, u32[]{:S(2)}, u32[]{:S(2)}) collective-permute-start(bf16[256,2048]{1,0:T(8,128)(2,1)S(1)} %collective-permute-done.3.far), channel_id=1, source_target_pairs={{0,1},{1,2},{2,3},{3,0},{4,5},{5,6},{6,7},{7,4},{8,9},{9,10},{10,1... | collective-permute-start | bytes 3145736 | tf_op jit(solution)/shard_map/ppermute | solution.py:61
  112.0 26.2 %collective-permute-start.6 = (bf16[256,2048]{1,0:T(8,128)(2,1)S(1)}, bf16[256,2048]{1,0:T(8,128)(2,1)S(1)}, u32[]{:S(2)}, u32[]{:S(2)}) collective-permute-start(bf16[256,2048]{1,0:T(8,128)(2,1)S(1)} %multiply_convert_fusion.1), channel_id=1, source_target_pairs={{0,1},{1,2},{2,3},{3,0},{4,5},{5,6},{6,7},{7,4},{8,9},{9,10},{10,1... | collective-permute-start | bytes 3145736 | tf_op jit(solution)/shard_map/ppermute | solution.py:61
  138.2 24.2 %collective-permute-start.7 = (bf16[1024,512]{1,0:T(8,128)(2,1)}, bf16[1024,512]{1,0:T(8,128)(2,1)S(1)}, u32[]{:S(2)}, u32[]{:S(2)}) collective-permute-start(bf16[1024,512]{1,0:T(8,128)(2,1)} %get-tuple-element.105.c0), channel_id=1, source_target_pairs={{0,1},{1,2},{2,3},{3,0},{4,5},{5,6},{6,7},{7,4},{8,9},{9,10},{10,1... | collective-permute-start | bytes 3145736 | tf_op jit(solution)/shard_map/ppermute | solution.py:61
  163.4 23.3 %collective-permute-start.8 = (bf16[1024,512]{1,0:T(8,128)(2,1)S(1)}, bf16[1024,512]{1,0:T(8,128)(2,1)S(1)}, u32[]{:S(2)}, u32[]{:S(2)}) collective-permute-start(bf16[1024,512]{1,0:T(8,128)(2,1)S(1)} %collective-permute-done.7.c1), channel_id=1, source_target_pairs={{0,1},{1,2},{2,3},{3,0},{4,5},{5,6},{6,7},{7,4},{8,9},{9,10},{10,1... | collective-permute-start | bytes 3145736 | tf_op jit(solution)/shard_map/ppermute | solution.py:61
  186.8 22.2 %collective-permute-start.9 = (bf16[1024,512]{1,0:T(8,128)(2,1)S(1)}, bf16[1024,512]{1,0:T(8,128)(2,1)S(1)}, u32[]{:S(2)}, u32[]{:S(2)}) collective-permute-start(bf16[1024,512]{1,0:T(8,128)(2,1)S(1)} %collective-permute-done.8.c2), channel_id=1, source_target_pairs={{0,1},{1,2},{2,3},{3,0},{4,5},{5,6},{6,7},{7,4},{8,9},{9,10},{10,1... | collective-permute-start | bytes 3145736 | tf_op jit(solution)/shard_map/ppermute | solution.py:61
  210.0 23.5 %collective-permute-start.10 = (bf16[256,2048]{1,0:T(8,128)(2,1)S(1)}, bf16[256,2048]{1,0:T(8,128)(2,1)S(1)}, u32[]{:S(2)}, u32[]{:S(2)}) collective-permute-start(bf16[256,2048]{1,0:T(8,128)(2,1)S(1)} %collective-permute-done.6), channel_id=1, source_target_pairs={{0,1},{1,2},{2,3},{3,0},{4,5},{5,6},{6,7},{7,4},{8,9},{9,10},{10,1... | collective-permute-start | bytes 3145736 | tf_op jit(solution)/shard_map/ppermute | solution.py:61
  233.5 20.8 %collective-permute-start.11 = (bf16[256,2048]{1,0:T(8,128)(2,1)S(1)}, bf16[256,2048]{1,0:T(8,128)(2,1)S(1)}, u32[]{:S(2)}, u32[]{:S(2)}) collective-permute-start(bf16[256,2048]{1,0:T(8,128)(2,1)S(1)} %collective-permute-done.10), channel_id=1, source_target_pairs={{0,1},{1,2},{2,3},{3,0},{4,5},{5,6},{6,7},{7,4},{8,9},{9,10},{10,1... | collective-permute-start | bytes 3145736 | tf_op jit(solution)/shard_map/ppermute | solution.py:61
  266.1 171.9 %reduce-scatter.7.cloned.1.call-start = ((), (), s32[]{:S(2)}) async-start(), calls=%async_computation.8 | async-start | bytes 14155776 | tf_op jit(solution)/shard_map/reduce_scatter | solution.py:663
  276.8 23.3 %collective-permute-start.12 = (bf16[256,2048]{1,0:T(8,128)(2,1)}, bf16[256,2048]{1,0:T(8,128)(2,1)S(1)}, u32[]{:S(2)}, u32[]{:S(2)}) collective-permute-start(bf16[256,2048]{1,0:T(8,128)(2,1)} %get-tuple-element.123), channel_id=1, source_target_pairs={{0,1},{1,2},{2,3},{3,0},{4,5},{5,6},{6,7},{7,4},{8,9},{9,10},{10,1... | collective-permute-start | bytes 3145736 | tf_op jit(solution)/shard_map/ppermute | solution.py:61
  300.1 22.2 %collective-permute-start.13 = (bf16[256,2048]{1,0:T(8,128)(2,1)}, bf16[256,2048]{1,0:T(8,128)(2,1)S(1)}, u32[]{:S(2)}, u32[]{:S(2)}) collective-permute-start(bf16[256,2048]{1,0:T(8,128)(2,1)} %shard_map.254), channel_id=1, source_target_pairs={{0,1},{1,2},{2,3},{3,0},{4,5},{5,6},{6,7},{7,4},{8,9},{9,10},{10,1... | collective-permute-start | bytes 3145736 | tf_op jit(solution)/shard_map/ppermute | solution.py:61
  324.0 21.5 %collective-permute-start.14 = (bf16[256,2048]{1,0:T(8,128)(2,1)S(1)}, bf16[256,2048]{1,0:T(8,128)(2,1)}, u32[]{:S(2)}, u32[]{:S(2)}) collective-permute-start(bf16[256,2048]{1,0:T(8,128)(2,1)S(1)} %add_convert_fusion.5), channel_id=1, source_target_pairs={{0,1},{1,2},{2,3},{3,0},{4,5},{5,6},{6,7},{7,4},{8,9},{9,10},{10,1... | collective-permute-start | bytes 3145736 | tf_op jit(solution)/shard_map/ppermute | solution.py:61
  345.6 25.0 %copy-start.13 = (bf16[256,2048]{1,0:T(8,128)(2,1)S(1)}, bf16[256,2048]{1,0:T(8,128)(2,1)}, u32[]{:S(2)}) copy-start(bf16[256,2048]{1,0:T(8,128)(2,1)} %get-tuple-element.136) | copy-start | bytes 3145732
  345.6 175.9 %reduce-scatter.9.cloned.1.call-start = ((), (), s32[]{:S(2)}) async-start(), calls=%async_computation.9 | async-start | bytes 9437184 | tf_op jit(solution)/shard_map/reduce_scatter | solution.py:679
  347.3 23.2 %collective-permute-start.15 = (bf16[256,2048]{1,0:T(8,128)(2,1)S(1)}, bf16[256,2048]{1,0:T(8,128)(2,1)S(1)}, u32[]{:S(2)}, u32[]{:S(2)}) collective-permute-start(bf16[256,2048]{1,0:T(8,128)(2,1)S(1)} %add_convert_fusion.4), channel_id=1, source_target_pairs={{0,1},{1,2},{2,3},{3,0},{4,5},{5,6},{6,7},{7,4},{8,9},{9,10},{10,1... | collective-permute-start | bytes 3145736 | tf_op jit(solution)/shard_map/ppermute | solution.py:61
  370.9 35.2 %collective-permute-start.19 = (bf16[256,2048]{1,0:T(8,128)(2,1)S(1)}, bf16[256,2048]{1,0:T(8,128)(2,1)S(1)}, u32[]{:S(2)}, u32[]{:S(2)}) collective-permute-start(bf16[256,2048]{1,0:T(8,128)(2,1)S(1)} %add_convert_fusion.3), channel_id=1, source_target_pairs={{0,1},{1,2},{2,3},{3,0},{4,5},{5,6},{6,7},{7,4},{8,9},{9,10},{10,1... | collective-permute-start | bytes 3145736 | tf_op jit(solution)/shard_map/ppermute | solution.py:61
  384.4 13.5 %collective-permute-start.16 = (bf16[256,512]{1,0:T(8,128)(2,1)}, bf16[256,512]{1,0:T(8,128)(2,1)S(1)}, u32[]{:S(2)}, u32[]{:S(2)}) collective-permute-start(bf16[256,512]{1,0:T(8,128)(2,1)} %get-tuple-element.131), channel_id=1, source_target_pairs={{0,1},{1,2},{2,3},{3,0},{4,5},{5,6},{6,7},{7,4},{8,9},{9,10},{10,1... | collective-permute-start | bytes 786440 | tf_op jit(solution)/shard_map/ppermute | solution.py:61
  386.3 19.9 %collective-permute-start.17 = (bf16[256,512]{1,0:T(8,128)(2,1)}, bf16[256,512]{1,0:T(8,128)(2,1)S(1)}, u32[]{:S(2)}, u32[]{:S(2)}) collective-permute-start(bf16[256,512]{1,0:T(8,128)(2,1)} %get-tuple-element.132), channel_id=1, source_target_pairs={{0,2},{1,3},{2,0},{3,1},{4,6},{5,7},{6,4},{7,5},{8,10},{9,11},{10,... | collective-permute-start | bytes 786440 | tf_op jit(solution)/shard_map/ppermute | solution.py:61
  388.1 18.1 %collective-permute-start.18 = (bf16[256,512]{1,0:T(8,128)(2,1)}, bf16[256,512]{1,0:T(8,128)(2,1)S(1)}, u32[]{:S(2)}, u32[]{:S(2)}) collective-permute-start(bf16[256,512]{1,0:T(8,128)(2,1)} %get-tuple-element.133), channel_id=1, source_target_pairs={{0,3},{1,0},{2,1},{3,2},{4,7},{5,4},{6,5},{7,6},{8,11},{9,8},{10,9... | collective-permute-start | bytes 786440 | tf_op jit(solution)/shard_map/ppermute | solution.py:61
  438.1 134.8 %reduce-scatter.11.cloned.1.call-start = ((), (), s32[]{:S(2)}) async-start(), calls=%async_computation.10 | async-start | bytes 5308416 | tf_op jit(solution)/shard_map/reduce_scatter | solution.py:722
  439.5 49.8 %collective-permute-start.21 = (bf16[256,2048]{1,0:T(8,128)(2,1)}, bf16[256,2048]{1,0:T(8,128)(2,1)}, u32[]{:S(2)}, u32[]{:S(2)}) collective-permute-start(bf16[256,2048]{1,0:T(8,128)(2,1)} %add_convert_fusion.1), channel_id=1, source_target_pairs={{0,1},{1,2},{2,3},{3,0},{4,5},{5,6},{6,7},{7,4},{8,9},{9,10},{10,1... | collective-permute-start | bytes 3145736 | tf_op jit(solution)/shard_map/ppermute | solution.py:61
  442.3 46.5 %collective-permute-start.20 = (bf16[256,2048]{1,0:T(8,128)(2,1)S(1)}, bf16[256,2048]{1,0:T(8,128)(2,1)S(1)}, u32[]{:S(2)}, u32[]{:S(2)}) collective-permute-start(bf16[256,2048]{1,0:T(8,128)(2,1)S(1)} %copy-done.14), channel_id=1, source_target_pairs={{0,1},{1,2},{2,3},{3,0},{4,5},{5,6},{6,7},{7,4},{8,9},{9,10},{10,1... | collective-permute-start | bytes 3145736 | tf_op jit(solution)/shard_map/ppermute | solution.py:61
  453.7 35.1 %copy-start.17 = (bf16[256,2048]{1,0:T(8,128)(2,1)S(1)}, bf16[256,2048]{1,0:T(8,128)(2,1)}, u32[]{:S(2)}) copy-start(bf16[256,2048]{1,0:T(8,128)(2,1)} %get-tuple-element.151) | copy-start | bytes 3145732
  464.2 25.0 %copy-start.19 = (f32[2048,128]{1,0:T(8,128)S(1)}, f32[2048,128]{1,0:T(8,128)}, u32[]{:S(2)}) copy-start(f32[2048,128]{1,0:T(8,128)} %get-tuple-element.160) | copy-start | bytes 3145732
  489.2 29.7 %copy-start.12 = (bf16[256,2048]{1,0:T(8,128)(2,1)S(1)}, bf16[256,2048]{1,0:T(8,128)(2,1)}, u32[]{:S(2)}) copy-start(bf16[256,2048]{1,0:T(8,128)(2,1)} %get-tuple-element.165) | copy-start | bytes 3145732
  489.6 29.3 %collective-permute-start.25 = (bf16[256,2048]{1,0:T(8,128)(2,1)S(1)}, bf16[256,2048]{1,0:T(8,128)(2,1)}, u32[]{:S(2)}, u32[]{:S(2)}) collective-permute-start(bf16[256,2048]{1,0:T(8,128)(2,1)S(1)} %add_convert_fusion.2), channel_id=1, source_target_pairs={{0,1},{1,2},{2,3},{3,0},{4,5},{5,6},{6,7},{7,4},{8,9},{9,10},{10,1... | collective-permute-start | bytes 3145736 | tf_op jit(solution)/shard_map/ppermute | solution.py:61
  489.9 26.4 %collective-permute-start.23 = (f32[2560]{0:T(1024)S(1)}, f32[2560]{0:T(1024)S(1)}, u32[]{:S(2)}, u32[]{:S(2)}) collective-permute-start(f32[2560]{0:T(1024)S(1)} %pad_maximum_fusion.2), channel_id=1, source_target_pairs={{0,2},{1,3},{2,0},{3,1},{4,6},{5,7},{6,4},{7,5},{8,10},{9,11},{10,... | collective-permute-start | bytes 30728 | tf_op jit(solution)/shard_map/ppermute | solution.py:61
  492.0 24.3 %collective-permute-start.24 = (f32[2560]{0:T(1024)S(1)}, f32[2560]{0:T(1024)S(1)}, u32[]{:S(2)}, u32[]{:S(2)}) collective-permute-start(f32[2560]{0:T(1024)S(1)} %pad_maximum_fusion.2), channel_id=1, source_target_pairs={{0,3},{1,0},{2,1},{3,2},{4,7},{5,4},{6,5},{7,6},{8,11},{9,8},{10,9... | collective-permute-start | bytes 30728 | tf_op jit(solution)/shard_map/ppermute | solution.py:61
  493.8 22.8 %collective-permute-start.22 = (f32[2560]{0:T(1024)S(1)}, f32[2560]{0:T(1024)S(1)}, u32[]{:S(2)}, u32[]{:S(2)}) collective-permute-start(f32[2560]{0:T(1024)S(1)} %pad_maximum_fusion.2), channel_id=1, source_target_pairs={{0,1},{1,2},{2,3},{3,0},{4,5},{5,6},{6,7},{7,4},{8,9},{9,10},{10,1... | collective-permute-start | bytes 30728 | tf_op jit(solution)/shard_map/ppermute | solution.py:61
  521.5 28.2 %collective-permute-start.26 = (bf16[256,2048]{1,0:T(8,128)(2,1)}, bf16[256,2048]{1,0:T(8,128)(2,1)S(1)}, u32[]{:S(2)}, u32[]{:S(2)}) collective-permute-start(bf16[256,2048]{1,0:T(8,128)(2,1)} %add_convert_fusion), channel_id=1, source_target_pairs={{0,1},{1,2},{2,3},{3,0},{4,5},{5,6},{6,7},{7,4},{8,9},{9,10},{10,1... | collective-permute-start | bytes 3145736 | tf_op jit(solution)/shard_map/ppermute | solution.py:61
  530.5 19.2 %copy-start.2 = (bf16[256,2048]{1,0:T(8,128)(2,1)S(1)}, bf16[256,2048]{1,0:T(8,128)(2,1)}, u32[]{:S(2)}) copy-start(bf16[256,2048]{1,0:T(8,128)(2,1)} %own.3) | copy-start | bytes 3145732
  530.5 19.2 %copy-start.5 = (bf16[256,2048]{1,0:T(8,128)(2,1)S(1)}, bf16[256,2048]{1,0:T(8,128)(2,1)}, u32[]{:S(2)}) copy-start(bf16[256,2048]{1,0:T(8,128)(2,1)} %get-tuple-element.169) | copy-start | bytes 3145732
  531.2 19.3 %copy-start.10 = (f32[256,2048]{1,0:T(8,128)S(1)}, f32[256,2048]{1,0:T(8,128)}, u32[]{:S(2)}) copy-start(f32[256,2048]{1,0:T(8,128)} %get-tuple-element.168) | copy-start | bytes 6291460
  531.2 24.1 %collective-permute-start.27 = (bf16[256,512]{1,0:T(8,128)(2,1)S(1)}, bf16[256,512]{1,0:T(8,128)(2,1)S(1)}, u32[]{:S(2)}, u32[]{:S(2)}) collective-permute-start(bf16[256,512]{1,0:T(8,128)(2,1)S(1)} %get-tuple-element.225), channel_id=1, source_target_pairs={{0,3},{1,0},{2,1},{3,2},{4,7},{5,4},{6,5},{7,6},{8,11},{9,8},{10,9... | collective-permute-start | bytes 786440 | tf_op jit(solution)/shard_map/ppermute | solution.py:61
  534.2 26.6 %collective-permute-start.29 = (bf16[256,512]{1,0:T(8,128)(2,1)S(1)}, bf16[256,512]{1,0:T(8,128)(2,1)S(1)}, u32[]{:S(2)}, u32[]{:S(2)}) collective-permute-start(bf16[256,512]{1,0:T(8,128)(2,1)S(1)} %get-tuple-element.226), channel_id=1, source_target_pairs={{0,1},{1,2},{2,3},{3,0},{4,5},{5,6},{6,7},{7,4},{8,9},{9,10},{10,1... | collective-permute-start | bytes 786440 | tf_op jit(solution)/shard_map/ppermute | solution.py:61
  534.2 35.0 %collective-permute-start.28 = (bf16[256,512]{1,0:T(8,128)(2,1)S(1)}, bf16[256,512]{1,0:T(8,128)(2,1)S(1)}, u32[]{:S(2)}, u32[]{:S(2)}) collective-permute-start(bf16[256,512]{1,0:T(8,128)(2,1)S(1)} %get-tuple-element.227), channel_id=1, source_target_pairs={{0,2},{1,3},{2,0},{3,1},{4,6},{5,7},{6,4},{7,5},{8,10},{9,11},{10,... | collective-permute-start | bytes 786440 | tf_op jit(solution)/shard_map/ppermute | solution.py:61
  (25 other events, 121.2 us)
Sparse Core Ops, SparseCore 0:
  12.6 41.6 all-gather.3
  85.8 105.8 all-gather.5
  193.6 45.5 all-gather.7
  266.2 63.2 reduce-scatter.4
  345.7 92.2 reduce-scatter.6
  441.7 71.2 reduce-scatter.8
  521.6 51.1 reduce-scatter.10

commit v5 on v3

--- a/solution.py
+++ b/solution.py
@@ -645,10 +645,9 @@
     d_hidden, d_attended, p0, p1, p2, p3 = branch(
         (b0, b_sum), hidden, cotangent, own_live, norm_ffn_all, rest_full, q_width
     )
-    p1, p2, p3, y_sum = together(p1, p2, p3, y_sum)
     grads_out = row_grads(d_attended, ctx_rows[None], 0, 1)
-    s1, s2, s3, grads_out = together(
-        shift_by(p3, 1), shift_by(p2, 2), shift_by(p1, -1), grads_out
+    s1, s2, s3, grads_out, y_sum = together(
+        shift_by(p3, 1), shift_by(p2, 2), shift_by(p1, -1), grads_out, y_sum
     )
     d_q, d_k, d_v, sum_q, sum_k = attend_back(
         place_ref, qkv, [p0, s1, s2, s3], log_total, pre, cos, sin, gain_q, gain_k

time: 593 us -> 594 us (level)
    reduce_scatter x1, waiting for transfers between devices: 0.01 us -> 7.83 us  [local(): lax.psum_scatter(grads_feed, 'dp', scatter_dimension=0, tiled=True)]
  transfers between devices with their start and end apart: 37 -> 37, of which waited for: 20 -> 22; matrix products, arithmetic and copies ran while one was open for 9% -> 9% of each run, Pallas kernels for 34% -> 34%
where the time goes in v5:
time: 594 us; the launch traced here: 585 us
  waiting for transfers between devices  267 us (45%)
  Pallas kernels  198 us (33%)
  starting transfers between devices  39.8 us (7%)
  local copies, waits for them, and re-layouts  32.9 us (6%)
  other arithmetic  32.6 us (5%)
  between operations  15 us (3%)
    ppermute x30, waiting for transfers between devices, shift_by(): lax.ppermute(value, 'tensor', [(i, (i + step) % WAYS) for i in range(WAYS)])  256 us
    ppermute x30, starting transfers between devices, shift_by(): lax.ppermute(value, 'tensor', [(i, (i + step) % WAYS) for i in range(WAYS)])  39.6 us
    pallas_call x3, Pallas kernels, row_grads(): call(grads_kernel, (width // tile,), [pl.BlockSpec((rows, tile), lambda j...  36 us
    pallas_call x2, Pallas kernels, back_feed(): call(functools.partial(back_kernel, slots, size, lone), (width // tile,),...  24.3 us
    pallas_call x1, Pallas kernels, feed(): call(feed_kernel, (tiles,), [whole((rows, width)), col(0), col(1)], [((3,...  19.7 us
    pallas_call x1, Pallas kernels, mix(): call(mix_kernel, (WAYS,), [whole(x.shape) for x in x_slots] + [whole(c.sh...  19.1 us
    unnamed x84, local copies, waits for them, and re-layouts  18.4 us
    pallas_call x1, Pallas kernels, attend_back(): call(attend_back_kernel, (2,), [pl.BlockSpec(memory_space=pltpu.SMEM), co...  18.1 us
  transfers between devices with their start and end apart: 37, of which 22 were waited for; matrix products, arithmetic and copies ran while one was open for 9% of the time, Pallas kernels for 34%

profile of v5, /device:TPU:0, one launch (start us, length us, event | category | flops | bytes accessed | tf_op | source)
XLA Modules:
  0.0 584.8 jit_solution(3967165738847410395)
XLA Ops:
  10.5 2.0 concatenate.36
  12.7 5.1 collective-permute-start.2
  22.5 1.9 fusion.8
  24.5 6.6 %collective-permute-done.1 = bf16[256,512]{1,0:T(8,128)(2,1)} collective-permute-done((bf16[256,512]{1,0:T(8,128)(2,1)S(1)}, bf16[256,512]{1,0:T(8,128)(2,1)}, u32[]{:S(2)}, u32[]{:S(2)}) %collective-permute-start.1) | collective-permute-done | bytes 262176 | tf_op jit(solution)/shard_map/ppermute | solution.py:61
  31.1 21.3 %collective-permute-done.below = bf16[256,2048]{1,0:T(8,128)(2,1)} collective-permute-done((bf16[256,2048]{1,0:T(8,128)(2,1)S(1)}, bf16[256,2048]{1,0:T(8,128)(2,1)}, u32[]{:S(2)}, u32[]{:S(2)}) %collective-permute-start) | collective-permute-done | bytes 1048608 | tf_op jit(solution)/shard_map/ppermute | solution.py:61
  58.9 25.2 %collective-permute-done.4 = bf16[256,512]{1,0:T(8,128)(2,1)S(1)} collective-permute-done((bf16[256,512]{1,0:T(8,128)(2,1)}, bf16[256,512]{1,0:T(8,128)(2,1)S(1)}, u32[]{:S(2)}, u32[]{:S(2)}) %collective-permute-start.4) | collective-permute-done | bytes 262176 | tf_op jit(solution)/shard_map/ppermute | solution.py:61
  87.0 25.0 %collective-permute-done.5.above = bf16[256,2048]{1,0:T(8,128)(2,1)} collective-permute-done((bf16[256,2048]{1,0:T(8,128)(2,1)S(1)}, bf16[256,2048]{1,0:T(8,128)(2,1)}, u32[]{:S(2)}, u32[]{:S(2)}) %collective-permute-start.5) | collective-permute-done | bytes 1048608 | tf_op jit(solution)/shard_map/ppermute | solution.py:61
  116.0 11.9 %shard_map.246 = (bf16[1024,2048]{1,0:T(8,128)(2,1)}, bf16[1024,1024]{1,0:T(8,128)(2,1)}, f32[1024,768]{1,0:T(8,128)}) custom-call(bf16[256,2048]{1,0:T(8,128)(2,1)} %own.3, bf16[256,2048]{1,0:T(8,128)(2,1)} %collective-permute-done.below, bf16[256,2048]{1,0:T(8,128)(2,1)} %copy-done.20, bf16[256,2048]{1,0:T(8,128)(2,1)} %collective-permute-done.5.above, ...), custom_call_target="tpu_custom_call" | custom-call | flops 4294967296 | bytes 20971520 | tf_op jit(solution)/shard_map/pallas_call | solution.py:126
  128.0 10.3 %shard_map.247 = (bf16[1024,512]{1,0:T(8,128)(2,1)}, f32[1024,256]{1,0:T(8,128)}) custom-call(s32[1]{0:T(128)} %bitcast.2.place, bf16[1024,1024]{1,0:T(8,128)(2,1)} %get-tuple-element.102.q.k.v, bf16[1024,1024]{1,0:T(8,128)(2,1)} %get-tuple-element.102.q.k.v, bf16[1024,1024]{1,0:T(8,128)(2,1)} %get-tuple-element.102.q.k.v), custom_call_target="tpu_custom_call" | custom-call | flops 1073741824 | bytes 2097152 | tf_op jit(solution)/shard_map/pallas_call | solution.py:184
  138.3 24.2 %collective-permute-done.7.c1 = bf16[1024,512]{1,0:T(8,128)(2,1)S(1)} collective-permute-done((bf16[1024,512]{1,0:T(8,128)(2,1)}, bf16[1024,512]{1,0:T(8,128)(2,1)S(1)}, u32[]{:S(2)}, u32[]{:S(2)}) %collective-permute-start.7) | collective-permute-done | bytes 1048608 | tf_op jit(solution)/shard_map/ppermute | solution.py:61
  163.4 23.3 %collective-permute-done.8.c2 = bf16[1024,512]{1,0:T(8,128)(2,1)S(1)} collective-permute-done((bf16[1024,512]{1,0:T(8,128)(2,1)S(1)}, bf16[1024,512]{1,0:T(8,128)(2,1)S(1)}, u32[]{:S(2)}, u32[]{:S(2)}) %collective-permute-start.8) | collective-permute-done | bytes 1048608 | tf_op jit(solution)/shard_map/ppermute | solution.py:61
  188.1 20.9 %collective-permute-done.9.c3 = bf16[1024,512]{1,0:T(8,128)(2,1)S(1)} collective-permute-done((bf16[1024,512]{1,0:T(8,128)(2,1)S(1)}, bf16[1024,512]{1,0:T(8,128)(2,1)S(1)}, u32[]{:S(2)}, u32[]{:S(2)}) %collective-permute-start.9) | collective-permute-done | bytes 1048608 | tf_op jit(solution)/shard_map/ppermute | solution.py:61
  211.3 19.1 %shard_map.248 = (bf16[1024,2048]{1,0:T(8,128)(2,1)}, f32[256,2048]{1,0:T(8,128)}, bf16[256,2048]{1,0:T(8,128)(2,1)}) custom-call(bf16[256,2048]{1,0:T(8,128)(2,1)} %own.3, bf16[256,2048]{1,0:T(8,128)(2,1)} %collective-permute-done.below, bf16[256,2048]{1,0:T(8,128)(2,1)} %copy-done.20, bf16[256,2048]{1,0:T(8,128)(2,1)} %collective-permute-done.5.above, ...), custom_call_target="tpu_custom_call" | custom-call | flops 8589934592 | bytes 25165824 | tf_op jit(solution)/shard_map/pallas_call | solution.py:226
  230.4 3.1 collective-permute-done.10
  234.6 19.7 %shard_map.249.a.slopes = bf16[3,1024,1536]{2,1,0:T(8,128)(2,1)} custom-call(bf16[1024,2048]{1,0:T(8,128)(2,1)} %get-tuple-element.113.n, bf16[2048,5120]{1,0:T(8,128)(2,1)} %all-gather.6.cloned.1.call-done.wa.wb.w_gate.w_up.w, bf16[2048,5120]{1,0:T(8,128)(2,1)} %all-gather.6.cloned.1.call-done.wa.wb.w_gate.w_up.w), custom_call_target="tpu_custom_call" | custom-call | flops 12884901888 | bytes 27262976 | tf_op jit(solution)/shard_map/pallas_call | solution.py:258
  255.4 10.7 %shard_map.250 = bf16[2048,1536]{1,0:T(8,128)(2,1)} custom-call(bf16[1024,2048]{1,0:T(8,128)(2,1)} %constant_dynamic-update-slice_fusion.6.n.d, bf16[3,1024,1536]{2,1,0:T(8,128)(2,1)} %shard_map.249.a.slopes), custom_call_target="tpu_custom_call" | custom-call | flops 6442450944 | bytes 13631488 | tf_op jit(solution)/shard_map/pallas_call | solution.py:365
  266.2 10.6 %shard_map.251 = (bf16[256,2048]{1,0:T(8,128)(2,1)}, bf16[256,2048]{1,0:T(8,128)(2,1)}, bf16[256,2048]{1,0:T(8,128)(2,1)}, bf16[256,2048]{1,0:T(8,128)(2,1)}) custom-call(bf16[3,1024,1536]{2,1,0:T(8,128)(2,1)} %shard_map.249.a.slopes, bf16[2048,1536]{1,0:T(8,128)(2,1)} %all-gather.8.cloned.1.call-done.wa.w_down), custom_call_target="tpu_custom_call" | custom-call | flops 6442450944 | bytes 14680064 | tf_op jit(solution)/shard_map/pallas_call | solution.py:343
  276.9 14.3 %shard_map.252.a.b = bf16[2,1024,1536]{2,1,0:T(8,128)(2,1)} custom-call(bf16[1024,2048]{1,0:T(8,128)(2,1)} %constant_dynamic-update-slice_fusion.6.n.d, bf16[2048,1536]{1,0:T(8,128)(2,1)} %all-gather.8.cloned.1.call-done.wa.w_down, bf16[3,1024,1536]{2,1,0:T(8,128)(2,1)} %shard_map.249.a.slopes), custom_call_target="tpu_custom_call" | custom-call | flops 6442450944 | bytes 23068672 | tf_op jit(solution)/shard_map/pallas_call | solution.py:283
  291.2 9.1 %shard_map.254 = bf16[256,2048]{1,0:T(8,128)(2,1)} custom-call(bf16[2,1024,1536]{2,1,0:T(8,128)(2,1)} %shard_map.252.a.b, bf16[2,1024,1536]{2,1,0:T(8,128)(2,1)} %shard_map.252.a.b, bf16[2048,5120]{1,0:T(8,128)(2,1)} %all-gather.6.cloned.1.call-done.wa.wb.w_gate.w_up.w, bf16[2048,5120]{1,0:T(8,128)(2,1)} %all-gather.6.cloned.1.call-done.wa.wb.w_gate.w_up.w), custom_call_target="tpu_custom_call" | custom-call | flops 3221225472 | bytes 20971520 | tf_op jit(solution)/shard_map/pallas_call | solution.py:317
  300.2 1.9 collective-permute-start.13
  302.1 15.2 %shard_map.253 = (bf16[256,2048]{1,0:T(8,128)(2,1)}, bf16[256,2048]{1,0:T(8,128)(2,1)}, bf16[256,2048]{1,0:T(8,128)(2,1)}) custom-call(bf16[2,1024,1536]{2,1,0:T(8,128)(2,1)} %shard_map.252.a.b, bf16[2,1024,1536]{2,1,0:T(8,128)(2,1)} %shard_map.252.a.b, bf16[2048,5120]{1,0:T(8,128)(2,1)} %all-gather.6.cloned.1.call-done.wa.wb.w_gate.w_up.w, ...), custom_call_target="tpu_custom_call" | custom-call | flops 9663676416 | bytes 20971520 | tf_op jit(solution)/shard_map/pallas_call | solution.py:317
  317.3 4.2 collective-permute-done.13
  323.2 2.4 collective-permute-start.14
  325.5 18.7 %shard_map.255 = bf16[2048,3072]{1,0:T(8,128)(2,1)} custom-call(bf16[1024,2048]{1,0:T(8,128)(2,1)} %get-tuple-element.113.n, bf16[2,1024,1536]{2,1,0:T(8,128)(2,1)} %shard_map.252.a.b), custom_call_target="tpu_custom_call" | custom-call | flops 12884901888 | bytes 23068672 | tf_op jit(solution)/shard_map/pallas_call | solution.py:365
  348.9 21.1 %collective-permute-done.15.arrived = bf16[256,2048]{1,0:T(8,128)(2,1)S(1)} collective-permute-done((bf16[256,2048]{1,0:T(8,128)(2,1)S(1)}, bf16[256,2048]{1,0:T(8,128)(2,1)S(1)}, u32[]{:S(2)}, u32[]{:S(2)}) %collective-permute-start.15) | collective-permute-done | bytes 1048608 | tf_op jit(solution)/shard_map/ppermute | solution.py:61
  373.5 10.7 %shard_map.256 = (f32[256,2048]{1,0:T(8,128)}, bf16[256,2048]{1,0:T(8,128)(2,1)}, bf16[256,512]{1,0:T(8,128)(2,1)}, bf16[256,512]{1,0:T(8,128)(2,1)}, bf16[256,5...) custom-call(bf16[256,2048]{1,0:T(8,128)(2,1)} %get-tuple-element.120.own, bf16[256,2048]{1,0:T(8,128)(2,1)} %copy-done.16, ...), custom_call_target="tpu_custom_call" | custom-call | flops 2147483648 | bytes 16777216 | tf_op jit(solution)/shard_map/pallas_call | solution.py:402
  385.4 2.2 collective-permute-start.17
  387.5 9.1 %collective-permute-start.18 = (bf16[256,512]{1,0:T(8,128)(2,1)}, bf16[256,512]{1,0:T(8,128)(2,1)S(1)}, u32[]{:S(2)}, u32[]{:S(2)}) collective-permute-start(bf16[256,512]{1,0:T(8,128)(2,1)} %get-tuple-element.133), channel_id=1, source_target_pairs={{0,3},{1,0},{2,1},{3,2},{4,7},{5,4},{6,5},{7,6},{8,11},{9,8},{10,9... | collective-permute-start | bytes 786440 | tf_op jit(solution)/shard_map/ppermute | solution.py:61
  396.6 6.6 %shard_map.257 = bf16[2048,2048]{1,0:T(8,128)(2,1)} custom-call(bf16[256,2048]{1,0:T(8,128)(2,1)} %get-tuple-element.134.n, bf16[1,256,2048]{2,1,0:T(8,128)(2,1)} %bitcast.30), custom_call_target="tpu_custom_call" | custom-call | flops 2147483648 | bytes 13631488 | tf_op jit(solution)/shard_map/pallas_call | solution.py:365
  403.3 2.2 collective-permute-done.17.d2
  406.2 18.1 %shard_map.258 = (bf16[1024,512]{1,0:T(8,128)(2,1)}, bf16[1024,256]{1,0:T(8,128)(2,1)}, bf16[1024,256]{1,0:T(8,128)(2,1)}, f32[8,256]{1,0:T(8,128)}, f32[8,256]{1,0:T(8,128)}) custom-call(s32[1]{0:T(128)} %bitcast.2.place, bf16[1024,1024]{1,0:T(8,128)(2,1)} %get-tuple-element.102.q.k.v, bf16[1024,1024]{1,0:T(8,128)(2,1)} %get-tuple-element.102.q.k.v, ...), custom_call_target="tpu_custom_call" | custom-call | flops 5368709120 | bytes 12582912 | tf_op jit(solution)/shard_map/pallas_call | solution.py:469
  424.3 5.0 shard_map.259
  429.4 7.8 %reduce-scatter.7.cloned.1.call-done = bf16[256,3072]{1,0:T(8,128)(2,1)} async-done(((bf16[2048,3072]{1,0:T(8,128)(2,1)}), bf16[256,3072]{1,0:T(8,128)(2,1)}) %reduce-scatter.7.cloned.1.call-update) | async-done | bytes 1572880 | tf_op jit(solution)/shard_map/reduce_scatter | solution.py:641
  443.1 7.3 %shard_map.260 = (bf16[256,2048]{1,0:T(8,128)(2,1)}, bf16[256,2048]{1,0:T(8,128)(2,1)}, bf16[256,2048]{1,0:T(8,128)(2,1)}) custom-call(bf16[1024,512]{1,0:T(8,128)(2,1)} %get-tuple-element.150.q, bf16[1024,256]{1,0:T(8,128)(2,1)} %get-tuple-element.144.k, bf16[1024,256]{1,0:T(8,128)(2,1)} %get-tuple-element.145.v, ...), custom_call_target="tpu_custom_call" | custom-call | flops 3221225472 | bytes 10485760 | tf_op jit(solution)/shard_map/pallas_call | solution.py:506
  450.4 2.6 fusion.15
  453.0 10.5 %shard_map.261 = (bf16[2048,1152]{1,0:T(8,128)(2,1)}, f32[2048,128]{1,0:T(8,128)}) custom-call(bf16[1024,2048]{1,0:T(8,128)(2,1)} %get-tuple-element.153.n, bf16[1024,512]{1,0:T(8,128)(2,1)} %get-tuple-element.150.q, bf16[1024,256]{1,0:T(8,128)(2,1)} %get-tuple-element.144.k, bf16[1024,256]{1,0:T(8,128)(2,1)} %get-tuple-element.145.v, ...), custom_call_target="tpu_custom_call" | custom-call | flops 4294967296 | bytes 16777216 | tf_op jit(solution)/shard_map/pallas_call | solution.py:536
  463.5 24.6 %collective-permute-done.20 = bf16[256,2048]{1,0:T(8,128)(2,1)S(1)} collective-permute-done((bf16[256,2048]{1,0:T(8,128)(2,1)S(1)}, bf16[256,2048]{1,0:T(8,128)(2,1)S(1)}, u32[]{:S(2)}, u32[]{:S(2)}) %collective-permute-start.20) | collective-permute-done | bytes 1048608 | tf_op jit(solution)/shard_map/ppermute | solution.py:61
  489.2 2.1 collective-permute-start.23
  493.6 22.0 %collective-permute-done.23 = f32[2560]{0:T(1024)S(1)} collective-permute-done((f32[2560]{0:T(1024)S(1)}, f32[2560]{0:T(1024)S(1)}, u32[]{:S(2)}, u32[]{:S(2)}) %collective-permute-start.23) | collective-permute-done | bytes 10272 | tf_op jit(solution)/shard_map/ppermute | solution.py:61
  518.2 2.6 add_convert_fusion
  523.3 3.2 copy.62
  526.5 3.3 multiply_convert_fusion
  530.4 3.1 collective-permute-start.27
  534.1 14.9 %collective-permute-done.26 = bf16[256,2048]{1,0:T(8,128)(2,1)S(1)} collective-permute-done((bf16[256,2048]{1,0:T(8,128)(2,1)}, bf16[256,2048]{1,0:T(8,128)(2,1)S(1)}, u32[]{:S(2)}, u32[]{:S(2)}) %collective-permute-start.26) | collective-permute-done | bytes 1048608 | tf_op jit(solution)/shard_map/ppermute | solution.py:61
  551.5 3.0 collective-permute-done.27
  554.5 5.6 collective-permute-done.29
  560.1 8.4 %collective-permute-done.28 = bf16[256,512]{1,0:T(8,128)(2,1)S(1)} collective-permute-done((bf16[256,512]{1,0:T(8,128)(2,1)S(1)}, bf16[256,512]{1,0:T(8,128)(2,1)S(1)}, u32[]{:S(2)}, u32[]{:S(2)}) %collective-permute-start.28) | collective-permute-done | bytes 262176 | tf_op jit(solution)/shard_map/ppermute | solution.py:61
  569.6 2.5 reduce-scatter.11.cloned.1.call-done
  (198 shorter events, 64.8 us)
Async XLA Ops:
  7.2 13.3 %copy-start.6 = (bf16[256,1536]{1,0:T(8,128)(2,1)S(1)}, bf16[256,1536]{1,0:T(8,128)(2,1)}, u32[]{:S(2)}) copy-start(bf16[256,1536]{1,0:T(8,128)(2,1)} %param.24) | copy-start | bytes 2359300
  7.2 104.8 %all-gather.4.cloned.1.call-start = ((), (), s32[]{:S(2)}) async-start(), calls=%async_computation.4 | async-start | bytes 5308416 | tf_op jit(solution)/shard_map/all_gather | solution.py:597
  12.5 198.8 %all-gather.6.cloned.1.call-start = ((), (), s32[]{:S(2)}) async-start(), calls=%async_computation.5 | async-start | bytes 23592960 | tf_op jit(solution)/shard_map/all_gather | solution.py:605
  12.7 11.8 %collective-permute-start.2 = (bf16[256,512]{1,0:T(8,128)(2,1)S(1)}, bf16[256,512]{1,0:T(8,128)(2,1)S(1)}, u32[]{:S(2)}, u32[]{:S(2)}) collective-permute-start(bf16[256,512]{1,0:T(8,128)(2,1)S(1)} %bitcast.31), channel_id=1, source_target_pairs={{0,3},{1,0},{2,1},{3,2},{4,7},{5,4},{6,5},{7,6},{8,11},{9,8},{10,9... | collective-permute-start | bytes 786440 | tf_op jit(solution)/shard_map/ppermute | solution.py:61
  17.8 13.3 %collective-permute-start.1 = (bf16[256,512]{1,0:T(8,128)(2,1)S(1)}, bf16[256,512]{1,0:T(8,128)(2,1)}, u32[]{:S(2)}, u32[]{:S(2)}) collective-permute-start(bf16[256,512]{1,0:T(8,128)(2,1)S(1)} %bitcast.32), channel_id=1, source_target_pairs={{0,1},{1,2},{2,3},{3,0},{4,5},{5,6},{6,7},{7,4},{8,9},{9,10},{10,1... | collective-permute-start | bytes 786440 | tf_op jit(solution)/shard_map/ppermute | solution.py:61
  17.8 34.7 %collective-permute-start = (bf16[256,2048]{1,0:T(8,128)(2,1)S(1)}, bf16[256,2048]{1,0:T(8,128)(2,1)}, u32[]{:S(2)}, u32[]{:S(2)}) collective-permute-start(bf16[256,2048]{1,0:T(8,128)(2,1)S(1)} %copy-done.1), channel_id=1, source_target_pairs={{0,1},{1,2},{2,3},{3,0},{4,5},{5,6},{6,7},{7,4},{8,9},{9,10},{10,1... | collective-permute-start | bytes 3145736 | tf_op jit(solution)/shard_map/ppermute | solution.py:61
  20.4 34.4 %copy-start.28 = (f32[256]{0:T(256)}, f32[256]{0:T(256)S(1)}, u32[]{:S(2)}) copy-start(f32[256]{0:T(256)S(1)} %compare_convert_fusion) | copy-start | bytes 3076
  21.5 33.3 %copy-start.4 = (bf16[256,2048]{1,0:T(8,128)(2,1)S(1)}, bf16[256,2048]{1,0:T(8,128)(2,1)}, u32[]{:S(2)}) copy-start(bf16[256,2048]{1,0:T(8,128)(2,1)} %cotangent.1) | copy-start | bytes 3145732
  52.5 31.7 %collective-permute-start.3 = (bf16[256,2048]{1,0:T(8,128)(2,1)}, bf16[256,2048]{1,0:T(8,128)(2,1)S(1)}, u32[]{:S(2)}, u32[]{:S(2)}) collective-permute-start(bf16[256,2048]{1,0:T(8,128)(2,1)} %collective-permute-done.below), channel_id=1, source_target_pairs={{0,1},{1,2},{2,3},{3,0},{4,5},{5,6},{6,7},{7,4},{8,9},{9,10},{10,1... | collective-permute-start | bytes 3145736 | tf_op jit(solution)/shard_map/ppermute | solution.py:61
  55.1 29.1 %collective-permute-start.4 = (bf16[256,512]{1,0:T(8,128)(2,1)}, bf16[256,512]{1,0:T(8,128)(2,1)S(1)}, u32[]{:S(2)}, u32[]{:S(2)}) collective-permute-start(bf16[256,512]{1,0:T(8,128)(2,1)} %collective-permute-done.1), channel_id=1, source_target_pairs={{0,1},{1,2},{2,3},{3,0},{4,5},{5,6},{6,7},{7,4},{8,9},{9,10},{10,1... | collective-permute-start | bytes 786440 | tf_op jit(solution)/shard_map/ppermute | solution.py:61
  57.1 28.6 %copy-start.24 = (bf16[1536,256]{1,0:T(8,128)(2,1)S(1)}, bf16[1536,256]{1,0:T(8,128)(2,1)}, u32[]{:S(2)}) copy-start(bf16[1536,256]{1,0:T(8,128)(2,1)} %param.26) | copy-start | bytes 2359300
  85.7 180.6 %all-gather.8.cloned.1.call-start = ((), (), s32[]{:S(2)}) async-start(), calls=%async_computation.6 | async-start | bytes 7077888 | tf_op jit(solution)/shard_map/all_gather | solution.py:610
  86.9 257.5 %reduce-scatter.5.cloned.1.call-start = ((), (), s32[]{:S(2)}) async-start(), calls=%async_computation.7 | async-start | bytes 7077888 | tf_op jit(solution)/shard_map/reduce_scatter | solution.py:627
  87.0 25.1 %collective-permute-start.5 = (bf16[256,2048]{1,0:T(8,128)(2,1)S(1)}, bf16[256,2048]{1,0:T(8,128)(2,1)}, u32[]{:S(2)}, u32[]{:S(2)}) collective-permute-start(bf16[256,2048]{1,0:T(8,128)(2,1)S(1)} %collective-permute-done.3.far), channel_id=1, source_target_pairs={{0,1},{1,2},{2,3},{3,0},{4,5},{5,6},{6,7},{7,4},{8,9},{9,10},{10,1... | collective-permute-start | bytes 3145736 | tf_op jit(solution)/shard_map/ppermute | solution.py:61
  112.0 26.2 %collective-permute-start.6 = (bf16[256,2048]{1,0:T(8,128)(2,1)S(1)}, bf16[256,2048]{1,0:T(8,128)(2,1)S(1)}, u32[]{:S(2)}, u32[]{:S(2)}) collective-permute-start(bf16[256,2048]{1,0:T(8,128)(2,1)S(1)} %multiply_convert_fusion.1), channel_id=1, source_target_pairs={{0,1},{1,2},{2,3},{3,0},{4,5},{5,6},{6,7},{7,4},{8,9},{9,10},{10,1... | collective-permute-start | bytes 3145736 | tf_op jit(solution)/shard_map/ppermute | solution.py:61
  138.2 24.2 %collective-permute-start.7 = (bf16[1024,512]{1,0:T(8,128)(2,1)}, bf16[1024,512]{1,0:T(8,128)(2,1)S(1)}, u32[]{:S(2)}, u32[]{:S(2)}) collective-permute-start(bf16[1024,512]{1,0:T(8,128)(2,1)} %get-tuple-element.105.c0), channel_id=1, source_target_pairs={{0,1},{1,2},{2,3},{3,0},{4,5},{5,6},{6,7},{7,4},{8,9},{9,10},{10,1... | collective-permute-start | bytes 3145736 | tf_op jit(solution)/shard_map/ppermute | solution.py:61
  163.4 23.3 %collective-permute-start.8 = (bf16[1024,512]{1,0:T(8,128)(2,1)S(1)}, bf16[1024,512]{1,0:T(8,128)(2,1)S(1)}, u32[]{:S(2)}, u32[]{:S(2)}) collective-permute-start(bf16[1024,512]{1,0:T(8,128)(2,1)S(1)} %collective-permute-done.7.c1), channel_id=1, source_target_pairs={{0,1},{1,2},{2,3},{3,0},{4,5},{5,6},{6,7},{7,4},{8,9},{9,10},{10,1... | collective-permute-start | bytes 3145736 | tf_op jit(solution)/shard_map/ppermute | solution.py:61
  186.8 22.2 %collective-permute-start.9 = (bf16[1024,512]{1,0:T(8,128)(2,1)S(1)}, bf16[1024,512]{1,0:T(8,128)(2,1)S(1)}, u32[]{:S(2)}, u32[]{:S(2)}) collective-permute-start(bf16[1024,512]{1,0:T(8,128)(2,1)S(1)} %collective-permute-done.8.c2), channel_id=1, source_target_pairs={{0,1},{1,2},{2,3},{3,0},{4,5},{5,6},{6,7},{7,4},{8,9},{9,10},{10,1... | collective-permute-start | bytes 3145736 | tf_op jit(solution)/shard_map/ppermute | solution.py:61
  210.0 23.6 %collective-permute-start.10 = (bf16[256,2048]{1,0:T(8,128)(2,1)S(1)}, bf16[256,2048]{1,0:T(8,128)(2,1)S(1)}, u32[]{:S(2)}, u32[]{:S(2)}) collective-permute-start(bf16[256,2048]{1,0:T(8,128)(2,1)S(1)} %collective-permute-done.6), channel_id=1, source_target_pairs={{0,1},{1,2},{2,3},{3,0},{4,5},{5,6},{6,7},{7,4},{8,9},{9,10},{10,1... | collective-permute-start | bytes 3145736 | tf_op jit(solution)/shard_map/ppermute | solution.py:61
  233.5 20.8 %collective-permute-start.11 = (bf16[256,2048]{1,0:T(8,128)(2,1)S(1)}, bf16[256,2048]{1,0:T(8,128)(2,1)S(1)}, u32[]{:S(2)}, u32[]{:S(2)}) collective-permute-start(bf16[256,2048]{1,0:T(8,128)(2,1)S(1)} %collective-permute-done.10), channel_id=1, source_target_pairs={{0,1},{1,2},{2,3},{3,0},{4,5},{5,6},{6,7},{7,4},{8,9},{9,10},{10,1... | collective-permute-start | bytes 3145736 | tf_op jit(solution)/shard_map/ppermute | solution.py:61
  266.2 171.1 %reduce-scatter.7.cloned.1.call-start = ((), (), s32[]{:S(2)}) async-start(), calls=%async_computation.8 | async-start | bytes 14155776 | tf_op jit(solution)/shard_map/reduce_scatter | solution.py:641
  276.9 23.4 %collective-permute-start.12 = (bf16[256,2048]{1,0:T(8,128)(2,1)}, bf16[256,2048]{1,0:T(8,128)(2,1)S(1)}, u32[]{:S(2)}, u32[]{:S(2)}) collective-permute-start(bf16[256,2048]{1,0:T(8,128)(2,1)} %get-tuple-element.123), channel_id=1, source_target_pairs={{0,1},{1,2},{2,3},{3,0},{4,5},{5,6},{6,7},{7,4},{8,9},{9,10},{10,1... | collective-permute-start | bytes 3145736 | tf_op jit(solution)/shard_map/ppermute | solution.py:61
  300.2 21.3 %collective-permute-start.13 = (bf16[256,2048]{1,0:T(8,128)(2,1)}, bf16[256,2048]{1,0:T(8,128)(2,1)S(1)}, u32[]{:S(2)}, u32[]{:S(2)}) collective-permute-start(bf16[256,2048]{1,0:T(8,128)(2,1)} %shard_map.254), channel_id=1, source_target_pairs={{0,1},{1,2},{2,3},{3,0},{4,5},{5,6},{6,7},{7,4},{8,9},{9,10},{10,1... | collective-permute-start | bytes 3145736 | tf_op jit(solution)/shard_map/ppermute | solution.py:61
  323.2 21.3 %collective-permute-start.14 = (bf16[256,2048]{1,0:T(8,128)(2,1)S(1)}, bf16[256,2048]{1,0:T(8,128)(2,1)}, u32[]{:S(2)}, u32[]{:S(2)}) collective-permute-start(bf16[256,2048]{1,0:T(8,128)(2,1)S(1)} %add_convert_fusion.5), channel_id=1, source_target_pairs={{0,1},{1,2},{2,3},{3,0},{4,5},{5,6},{6,7},{7,4},{8,9},{9,10},{10,1... | collective-permute-start | bytes 3145736 | tf_op jit(solution)/shard_map/ppermute | solution.py:61
  344.5 25.5 %copy-start.13 = (bf16[256,2048]{1,0:T(8,128)(2,1)S(1)}, bf16[256,2048]{1,0:T(8,128)(2,1)}, u32[]{:S(2)}) copy-start(bf16[256,2048]{1,0:T(8,128)(2,1)} %get-tuple-element.136) | copy-start | bytes 3145732
  344.5 176.3 %reduce-scatter.9.cloned.1.call-start = ((), (), s32[]{:S(2)}) async-start(), calls=%async_computation.9 | async-start | bytes 9437184 | tf_op jit(solution)/shard_map/reduce_scatter | solution.py:657
  347.1 22.9 %collective-permute-start.15 = (bf16[256,2048]{1,0:T(8,128)(2,1)S(1)}, bf16[256,2048]{1,0:T(8,128)(2,1)S(1)}, u32[]{:S(2)}, u32[]{:S(2)}) collective-permute-start(bf16[256,2048]{1,0:T(8,128)(2,1)S(1)} %add_convert_fusion.4), channel_id=1, source_target_pairs={{0,1},{1,2},{2,3},{3,0},{4,5},{5,6},{6,7},{7,4},{8,9},{9,10},{10,1... | collective-permute-start | bytes 3145736 | tf_op jit(solution)/shard_map/ppermute | solution.py:61
  370.3 35.1 %collective-permute-start.19 = (bf16[256,2048]{1,0:T(8,128)(2,1)S(1)}, bf16[256,2048]{1,0:T(8,128)(2,1)S(1)}, u32[]{:S(2)}, u32[]{:S(2)}) collective-permute-start(bf16[256,2048]{1,0:T(8,128)(2,1)S(1)} %add_convert_fusion.3), channel_id=1, source_target_pairs={{0,1},{1,2},{2,3},{3,0},{4,5},{5,6},{6,7},{7,4},{8,9},{9,10},{10,1... | collective-permute-start | bytes 3145736 | tf_op jit(solution)/shard_map/ppermute | solution.py:61
  384.2 19.0 %collective-permute-start.16 = (bf16[256,512]{1,0:T(8,128)(2,1)}, bf16[256,512]{1,0:T(8,128)(2,1)S(1)}, u32[]{:S(2)}, u32[]{:S(2)}) collective-permute-start(bf16[256,512]{1,0:T(8,128)(2,1)} %get-tuple-element.131), channel_id=1, source_target_pairs={{0,1},{1,2},{2,3},{3,0},{4,5},{5,6},{6,7},{7,4},{8,9},{9,10},{10,1... | collective-permute-start | bytes 786440 | tf_op jit(solution)/shard_map/ppermute | solution.py:61
  385.4 20.1 %collective-permute-start.17 = (bf16[256,512]{1,0:T(8,128)(2,1)}, bf16[256,512]{1,0:T(8,128)(2,1)S(1)}, u32[]{:S(2)}, u32[]{:S(2)}) collective-permute-start(bf16[256,512]{1,0:T(8,128)(2,1)} %get-tuple-element.132), channel_id=1, source_target_pairs={{0,2},{1,3},{2,0},{3,1},{4,6},{5,7},{6,4},{7,5},{8,10},{9,11},{10,... | collective-permute-start | bytes 786440 | tf_op jit(solution)/shard_map/ppermute | solution.py:61
  387.5 17.9 %collective-permute-start.18 = (bf16[256,512]{1,0:T(8,128)(2,1)}, bf16[256,512]{1,0:T(8,128)(2,1)S(1)}, u32[]{:S(2)}, u32[]{:S(2)}) collective-permute-start(bf16[256,512]{1,0:T(8,128)(2,1)} %get-tuple-element.133), channel_id=1, source_target_pairs={{0,3},{1,0},{2,1},{3,2},{4,7},{5,4},{6,5},{7,6},{8,11},{9,8},{10,9... | collective-permute-start | bytes 786440 | tf_op jit(solution)/shard_map/ppermute | solution.py:61
  437.3 134.9 %reduce-scatter.11.cloned.1.call-start = ((), (), s32[]{:S(2)}) async-start(), calls=%async_computation.10 | async-start | bytes 5308416 | tf_op jit(solution)/shard_map/reduce_scatter | solution.py:700
  438.7 49.8 %collective-permute-start.21 = (bf16[256,2048]{1,0:T(8,128)(2,1)}, bf16[256,2048]{1,0:T(8,128)(2,1)}, u32[]{:S(2)}, u32[]{:S(2)}) collective-permute-start(bf16[256,2048]{1,0:T(8,128)(2,1)} %add_convert_fusion.1), channel_id=1, source_target_pairs={{0,1},{1,2},{2,3},{3,0},{4,5},{5,6},{6,7},{7,4},{8,9},{9,10},{10,1... | collective-permute-start | bytes 3145736 | tf_op jit(solution)/shard_map/ppermute | solution.py:61
  441.6 46.5 %collective-permute-start.20 = (bf16[256,2048]{1,0:T(8,128)(2,1)S(1)}, bf16[256,2048]{1,0:T(8,128)(2,1)S(1)}, u32[]{:S(2)}, u32[]{:S(2)}) collective-permute-start(bf16[256,2048]{1,0:T(8,128)(2,1)S(1)} %copy-done.14), channel_id=1, source_target_pairs={{0,1},{1,2},{2,3},{3,0},{4,5},{5,6},{6,7},{7,4},{8,9},{9,10},{10,1... | collective-permute-start | bytes 3145736 | tf_op jit(solution)/shard_map/ppermute | solution.py:61
  453.0 35.1 %copy-start.17 = (bf16[256,2048]{1,0:T(8,128)(2,1)S(1)}, bf16[256,2048]{1,0:T(8,128)(2,1)}, u32[]{:S(2)}) copy-start(bf16[256,2048]{1,0:T(8,128)(2,1)} %get-tuple-element.151) | copy-start | bytes 3145732
  463.5 25.0 %copy-start.19 = (f32[2048,128]{1,0:T(8,128)S(1)}, f32[2048,128]{1,0:T(8,128)}, u32[]{:S(2)}) copy-start(f32[2048,128]{1,0:T(8,128)} %get-tuple-element.160) | copy-start | bytes 3145732
  488.5 29.7 %copy-start.12 = (bf16[256,2048]{1,0:T(8,128)(2,1)S(1)}, bf16[256,2048]{1,0:T(8,128)(2,1)}, u32[]{:S(2)}) copy-start(bf16[256,2048]{1,0:T(8,128)(2,1)} %get-tuple-element.165) | copy-start | bytes 3145732
  488.9 29.3 %collective-permute-start.25 = (bf16[256,2048]{1,0:T(8,128)(2,1)S(1)}, bf16[256,2048]{1,0:T(8,128)(2,1)}, u32[]{:S(2)}, u32[]{:S(2)}) collective-permute-start(bf16[256,2048]{1,0:T(8,128)(2,1)S(1)} %add_convert_fusion.2), channel_id=1, source_target_pairs={{0,1},{1,2},{2,3},{3,0},{4,5},{5,6},{6,7},{7,4},{8,9},{9,10},{10,1... | collective-permute-start | bytes 3145736 | tf_op jit(solution)/shard_map/ppermute | solution.py:61
  489.2 26.4 %collective-permute-start.23 = (f32[2560]{0:T(1024)S(1)}, f32[2560]{0:T(1024)S(1)}, u32[]{:S(2)}, u32[]{:S(2)}) collective-permute-start(f32[2560]{0:T(1024)S(1)} %pad_maximum_fusion.2), channel_id=1, source_target_pairs={{0,2},{1,3},{2,0},{3,1},{4,6},{5,7},{6,4},{7,5},{8,10},{9,11},{10,... | collective-permute-start | bytes 30728 | tf_op jit(solution)/shard_map/ppermute | solution.py:61
  491.2 24.4 %collective-permute-start.24 = (f32[2560]{0:T(1024)S(1)}, f32[2560]{0:T(1024)S(1)}, u32[]{:S(2)}, u32[]{:S(2)}) collective-permute-start(f32[2560]{0:T(1024)S(1)} %pad_maximum_fusion.2), channel_id=1, source_target_pairs={{0,3},{1,0},{2,1},{3,2},{4,7},{5,4},{6,5},{7,6},{8,11},{9,8},{10,9... | collective-permute-start | bytes 30728 | tf_op jit(solution)/shard_map/ppermute | solution.py:61
  493.0 22.8 %collective-permute-start.22 = (f32[2560]{0:T(1024)S(1)}, f32[2560]{0:T(1024)S(1)}, u32[]{:S(2)}, u32[]{:S(2)}) collective-permute-start(f32[2560]{0:T(1024)S(1)} %pad_maximum_fusion.2), channel_id=1, source_target_pairs={{0,1},{1,2},{2,3},{3,0},{4,5},{5,6},{6,7},{7,4},{8,9},{9,10},{10,1... | collective-permute-start | bytes 30728 | tf_op jit(solution)/shard_map/ppermute | solution.py:61
  520.8 28.2 %collective-permute-start.26 = (bf16[256,2048]{1,0:T(8,128)(2,1)}, bf16[256,2048]{1,0:T(8,128)(2,1)S(1)}, u32[]{:S(2)}, u32[]{:S(2)}) collective-permute-start(bf16[256,2048]{1,0:T(8,128)(2,1)} %add_convert_fusion), channel_id=1, source_target_pairs={{0,1},{1,2},{2,3},{3,0},{4,5},{5,6},{6,7},{7,4},{8,9},{9,10},{10,1... | collective-permute-start | bytes 3145736 | tf_op jit(solution)/shard_map/ppermute | solution.py:61
  529.8 19.2 %copy-start.2 = (bf16[256,2048]{1,0:T(8,128)(2,1)S(1)}, bf16[256,2048]{1,0:T(8,128)(2,1)}, u32[]{:S(2)}) copy-start(bf16[256,2048]{1,0:T(8,128)(2,1)} %own.3) | copy-start | bytes 3145732
  529.8 19.2 %copy-start.5 = (bf16[256,2048]{1,0:T(8,128)(2,1)S(1)}, bf16[256,2048]{1,0:T(8,128)(2,1)}, u32[]{:S(2)}) copy-start(bf16[256,2048]{1,0:T(8,128)(2,1)} %get-tuple-element.169) | copy-start | bytes 3145732
  530.4 19.3 %copy-start.10 = (f32[256,2048]{1,0:T(8,128)S(1)}, f32[256,2048]{1,0:T(8,128)}, u32[]{:S(2)}) copy-start(f32[256,2048]{1,0:T(8,128)} %get-tuple-element.168) | copy-start | bytes 6291460
  530.4 24.1 %collective-permute-start.27 = (bf16[256,512]{1,0:T(8,128)(2,1)S(1)}, bf16[256,512]{1,0:T(8,128)(2,1)S(1)}, u32[]{:S(2)}, u32[]{:S(2)}) collective-permute-start(bf16[256,512]{1,0:T(8,128)(2,1)S(1)} %get-tuple-element.225), channel_id=1, source_target_pairs={{0,3},{1,0},{2,1},{3,2},{4,7},{5,4},{6,5},{7,6},{8,11},{9,8},{10,9... | collective-permute-start | bytes 786440 | tf_op jit(solution)/shard_map/ppermute | solution.py:61
  533.5 26.6 %collective-permute-start.29 = (bf16[256,512]{1,0:T(8,128)(2,1)S(1)}, bf16[256,512]{1,0:T(8,128)(2,1)S(1)}, u32[]{:S(2)}, u32[]{:S(2)}) collective-permute-start(bf16[256,512]{1,0:T(8,128)(2,1)S(1)} %get-tuple-element.226), channel_id=1, source_target_pairs={{0,1},{1,2},{2,3},{3,0},{4,5},{5,6},{6,7},{7,4},{8,9},{9,10},{10,1... | collective-permute-start | bytes 786440 | tf_op jit(solution)/shard_map/ppermute | solution.py:61
  533.5 35.0 %collective-permute-start.28 = (bf16[256,512]{1,0:T(8,128)(2,1)S(1)}, bf16[256,512]{1,0:T(8,128)(2,1)S(1)}, u32[]{:S(2)}, u32[]{:S(2)}) collective-permute-start(bf16[256,512]{1,0:T(8,128)(2,1)S(1)} %get-tuple-element.227), channel_id=1, source_target_pairs={{0,2},{1,3},{2,0},{3,1},{4,6},{5,7},{6,4},{7,5},{8,10},{9,11},{10,... | collective-permute-start | bytes 786440 | tf_op jit(solution)/shard_map/ppermute | solution.py:61
  (25 other events, 115.5 us)
Sparse Core Ops, SparseCore 0:
  12.6 41.6 all-gather.3
  85.8 105.8 all-gather.5
  193.6 45.5 all-gather.7
  266.3 63.2 reduce-scatter.4
  344.6 92.5 reduce-scatter.6
  440.9 71.2 reduce-scatter.8
  520.9 51.1 reduce-scatter.10
